TPU v7x, 128 devices: a whole 4x4x4 slice. The times are simulated.
128 devices in a mesh: section: 4 (over y_lo, core), dp: 16 (over z, x), mp: 2 (over y_hi).
Axes of the slice: x: 4, y: 4 (y_hi: 2, y_lo: 2; y = y_hi * 2 + y_lo), z: 4, core: 2. Of those that a mesh axis runs over, the one named last changes fastest.
Arguments:
- siglip_features: bfloat16 [8192, 1152], P('dp'), may hold values from -6 to 6
- convnext_features: bfloat16 [8192, 1536], P('dp'), may hold values from -6 to 6
- siglip_projection: bfloat16 [1152, 8192], P(None, ('section', 'mp')), may hold values from -0.125 to 0.125
- convnext_projection: bfloat16 [1536, 8192], P(None, ('section', 'mp')), may hold values from -0.125 to 0.125
- newline_embed: bfloat16 [8192], P(('section', 'mp')), may hold values from -6 to 6
- key_value_weight: bfloat16 [2048, 8192], P(None, ('section', 'mp')), may hold values from -0.0625 to 0.0625
- tile_rank: int32 [256, 1], replicated, may hold values from 0 to 15; in each aligned block of 16 rows (0 to 15, 16 to 31, ...) at most 2 rows name the same one
- row_end: int32 [256], replicated, may hold values 0 or 1
- key_value_grad: bfloat16 [16384, 2048], P('dp'), may hold values from -0.059814453 to 0.059814453
- newline_grad: bfloat16 [512, 2048], P('dp'), may hold values from -1.796875 to 1.796875
Outputs:
- siglip_weight_grad: float32 [1152, 8192], P('dp', ('section', 'mp'))
- convnext_weight_grad: float32 [1536, 8192], P('dp', ('section', 'mp'))
- key_value_weight_grad: float32 [2048, 8192], P('dp', ('section', 'mp'))
Inputs may be any that keep to these rules, and one draw needn't show every extreme that they name: `tile_rank`: each aligned block of 16 tiles (the tiles of one index of dp) sends at most 2 tiles to one rank, and exactly 2 to some rank.
All inputs are finite; a program needn't handle non-finite values.
Results may differ from a plain program's by a relative error of at most 0.007.
Values may be sent and summed in bfloat16 or wider, within the bound.
No kernel may reach another device: no remote copies, remote signals or barrier semaphores. Data moves between devices by JAX's collectives and lax.ppermute only.
A program may use at most 128 MiB of HBM per device.

v0:
```python
import jax
import jax.numpy as jnp
from jax import lax
from jax.sharding import PartitionSpec as P

D = 8192


epsilon = 1e-06


def tile_places(tile_rank, groups):
    dest_rank = tile_rank[:, 0]
    tile_count = dest_rank.shape[0]
    per_device = tile_count // groups
    onehot = (dest_rank[:, None] == jnp.arange(groups, dtype=jnp.int32)[None, :]).astype(jnp.int32)
    blocks = onehot.reshape(groups, per_device, groups)
    before = jnp.cumsum(blocks, axis=1) - blocks
    slot_place = jnp.sum(before * blocks, axis=2).reshape(tile_count)
    source = jnp.arange(tile_count, dtype=jnp.int32) // per_device
    return (dest_rank, source, slot_place)


def row_norms(squares):
    return lax.psum((squares[0], squares[1]), ("section", "mp"))


def row_products(products):
    return lax.psum(products, ("section", "mp"))


def norm_backward(inverse_rms, grad_values, proj_values):
    products = row_products(jnp.sum(grad_values * proj_values, axis=1))[:, None]
    return (inverse_rms * grad_values - inverse_rms**3 * proj_values * products / D).astype(
        jnp.bfloat16
    )


def local(
    siglip_features,
    convnext_features,
    siglip_projection,
    convnext_projection,
    newline_embed,
    key_value_weight,
    tile_rank,
    row_end,
    key_value_grad,
    newline_grad,
):
    groups = lax.axis_size("dp")
    my_rank = lax.axis_index("dp")
    dest_rank, source, slot_place = tile_places(tile_rank, groups)
    per_device = dest_rank.shape[0] // groups
    capacity = 2 * per_device // groups
    row_count = siglip_features.shape[0]
    tile_rows = row_count // per_device
    share = siglip_projection.shape[1]
    mine_dest = lax.dynamic_slice_in_dim(dest_rank, my_rank * per_device, per_device)
    mine_place = lax.dynamic_slice_in_dim(slot_place, my_rank * per_device, per_device)
    rank_ids = jnp.arange(groups, dtype=jnp.int32)[:, None, None]
    place_ids = jnp.arange(capacity, dtype=jnp.int32)[None, :, None]
    select = (
        (mine_dest[None, None, :] == rank_ids) & (mine_place[None, None, :] == place_ids)
    ).astype(jnp.bfloat16)
    projected = (
        jnp.dot(siglip_features, siglip_projection, preferred_element_type=jnp.float32)
        + jnp.dot(convnext_features, convnext_projection, preferred_element_type=jnp.float32)
    ).astype(jnp.bfloat16)
    line_vector = newline_embed.astype(jnp.float32)
    line_square = jnp.sum(line_vector * line_vector)
    outgoing = jnp.einsum(
        "gcj,jtx->gctx",
        select,
        projected.reshape(per_device, tile_rows, share),
        preferred_element_type=jnp.float32,
    ).astype(jnp.bfloat16)
    outgoing = outgoing.reshape(groups, capacity * tile_rows, share)
    received = lax.all_to_all(outgoing, "dp", split_axis=0, concat_axis=0, tiled=True).reshape(
        groups * capacity * tile_rows, share
    )
    recv_values = received.astype(jnp.float32)
    statistic = row_norms((jnp.sum(recv_values * recv_values, axis=1), line_square))
    recv_inverse = lax.rsqrt(statistic[0] / D + epsilon)[:, None]
    line_total_sq = statistic[1]
    normed = (recv_values * recv_inverse).astype(jnp.bfloat16)
    line_normed = (line_vector * lax.rsqrt(line_total_sq / D + epsilon)).astype(jnp.bfloat16)
    slot_global = source * capacity + slot_place
    line_live = (dest_rank == my_rank) & (row_end == 1)
    slot_ids = jnp.arange(groups * capacity, dtype=jnp.int32)[None, :]
    newline_mask = jnp.sum(
        ((slot_global[:, None] == slot_ids) & line_live[:, None]).astype(jnp.int32), axis=0
    )
    line_total = jnp.dot(
        newline_mask.astype(jnp.bfloat16)[None, :], newline_grad, preferred_element_type=jnp.float32
    )[0]
    kv_term = lax.dot_general(
        key_value_grad, normed, (((0,), (0,)), ((), ())), preferred_element_type=jnp.float32
    )
    kv_term = kv_term + line_total[:, None] * line_normed.astype(jnp.float32)[None, :]
    normed_grad = jnp.dot(
        key_value_grad, key_value_weight, preferred_element_type=jnp.float32
    ).astype(jnp.bfloat16)
    returning = norm_backward(recv_inverse, normed_grad.astype(jnp.float32), recv_values)
    returned = lax.all_to_all(
        returning.reshape(groups, capacity * tile_rows, share),
        "dp",
        split_axis=0,
        concat_axis=0,
        tiled=True,
    )
    tile_back = jnp.einsum(
        "gcj,gctx->jtx",
        select,
        returned.reshape(groups, capacity, tile_rows, share),
        preferred_element_type=jnp.float32,
    ).reshape(row_count, share)
    projected_grad = tile_back.astype(jnp.bfloat16)
    contract = (((0,), (0,)), ((), ()))
    siglip_term = lax.dot_general(
        siglip_features, projected_grad, contract, preferred_element_type=jnp.float32
    )
    convnext_term = lax.dot_general(
        convnext_features, projected_grad, contract, preferred_element_type=jnp.float32
    )
    siglip_result, convnext_result, kv_result = (
        lax.psum_scatter(siglip_term, "dp", scatter_dimension=0, tiled=True),
        lax.psum_scatter(convnext_term, "dp", scatter_dimension=0, tiled=True),
        lax.psum_scatter(kv_term, "dp", scatter_dimension=0, tiled=True),
    )
    return (siglip_result, convnext_result, kv_result)


def solution(mesh):
    in_specs = (
        P("dp", None),
        P("dp", None),
        P(None, ("section", "mp")),
        P(None, ("section", "mp")),
        P(("section", "mp")),
        P(None, ("section", "mp")),
        P(),
        P(),
        P("dp", None),
        P("dp", None),
    )
    out_specs = (P("dp", ("section", "mp")), P("dp", ("section", "mp")), P("dp", ("section", "mp")))
    return jax.shard_map(local, mesh=mesh, in_specs=in_specs, out_specs=out_specs, check_vma=False)
```

profile of v0, /device:TPU:0, one launch (start us, length us, event | category | flops | bytes accessed | tf_op | source)
XLA Modules:
  0.0 415.1 jit_solution(3388433435332822408)
XLA Ops:
  7.7 1.6 reduce.6
  11.0 3.7 fusion.30
  14.7 1.8 add_convert_fusion
  16.5 1.0 convolution_convert_fusion.1
  17.4 2.5 copy.55
  19.9 8.1 %all-to-all-start = ((bf16[16,64,1024]{2,1,0:T(8,128)(2,1)}), bf16[16,64,1024]{2,1,0:T(8,128)(2,1)S(1)}, u32[]{:S(2)}, u32[]{:S(2)}) async-start(bf16[16,64,1024]{2,1,0:T(8,128)(2,1)} %copy.55), calls=%async_computation | async-start | bytes 4194304 | tf_op jit(solution)/shard_map/all_to_all | solution.py:79
  28.7 31.0 %all-to-all-done = bf16[16,64,1024]{2,1,0:T(8,128)(2,1)S(1)} async-done(((bf16[16,64,1024]{2,1,0:T(8,128)(2,1)}), bf16[16,64,1024]{2,1,0:T(8,128)(2,1)S(1)}, u32[]{:S(2)}, u32[]{:S(2)}) %all-to-all-start) | async-done | bytes 2097184 | tf_op jit(solution)/shard_map/all_to_all | solution.py:79
  60.2 9.2 %fusion.2 = (f32[1024]{0:T(1024)S(1)}, bf16[1024,1024]{1,0:T(8,128)(2,1)}) fusion(bf16[16,64,1024]{2,1,0:T(8,128)(2,1)S(1)} %all-to-all-done, bf16[1024,2048]{1,0:T(8,128)(2,1)} %param.18, bf16[2048,1024]{1,0:T(8,128)(2,1)} %param.15), kind=kOutput, calls=%fused_computation.7 | convolution fusion | flops 4300209152 | bytes 12587008 | tf_op jit(solution)/shard_map/dot_general | solution.py:101
  69.5 18.3 %all-reduce.1 = (f32[1024]{0:T(1024)S(1)}, f32[1024]{0:T(1024)S(1)}, f32[]{:T(128)}) all-reduce(f32[1024]{0:T(1024)S(1)} %get-tuple-element.25, f32[1024]{0:T(1024)S(1)} %reduce_sum.49, f32[]{:T(128)} %fusion.21), channel_id=1, replica_groups=mesh['section'=4,'dp'=16,'mp'=2] {'section','mp'}, use_global_device_ids=true, to_apply=%region_5.6 | all-reduce | flops 2049 | bytes 16392 | tf_op jit(solution)/shard_map/psum | solution.py:29
  87.9 3.8 fusion.6
  91.6 32.7 %all_to_all.10 = bf16[16,64,1024]{2,1,0:T(8,128)(2,1)S(1)} all-to-all(bf16[16,64,1024]{2,1,0:T(8,128)(2,1)S(1)} %bitcast.61), channel_id=1, replica_groups=mesh['section'=4,'dp'=16,'mp'=2] {'dp'}, dimensions={0} | all-to-all | bytes 4194304 | tf_op jit(solution)/shard_map/all_to_all | solution.py:105
  124.3 2.4 bitcast_convert_fusion
  127.3 3.8 convolution_bitcast_fusion.1
  132.9 9.7 %bitcast_add_fusion = f32[2048,1024]{0,1:T(8,128)} fusion(bf16[1024,1024]{1,0:T(8,128)(2,1)S(1)} %copy-done.2, bf16[1024,2048]{1,0:T(8,128)(2,1)} %param.18, f32[1024]{0:T(1024)S(1)} %fusion.23, f32[2048]{0:T(1024)S(1)} %bitcast.67), kind=kOutput, calls=%fused_computation | convolution fusion | flops 4299161600 | bytes 14692352 | tf_op jit(solution)/shard_map/dot_general | solution.py:97
  142.7 1.3 copy-done.9
  144.0 4.4 %convolution_bitcast_fusion = f32[1536,1024]{0,1:T(8,128)} fusion(bf16[512,1024]{1,0:T(8,128)(2,1)S(1)} %bitcast.65, bf16[512,1536]{1,0:T(8,128)(2,1)S(1)} %copy-done.9), kind=kOutput, calls=%fused_computation.3 | convolution fusion | flops 1610612736 | bytes 8912896 | tf_op jit(solution)/shard_map/dot_general | solution.py:123
  148.4 6.7 %copy.69 = f32[1536,1024]{1,0:T(8,128)} copy(f32[1536,1024]{0,1:T(8,128)} %convolution_bitcast_fusion) | data formatting | bytes 12582912
  155.1 0.8 copy-done.10
  157.2 77.5 %all-reduce.4.cloned.1.call-done = f32[1152,1024]{0,1:T(8,128)} async-done(((f32[1152,1024]{0,1:T(8,128)}), f32[1152,1024]{0,1:T(8,128)}) %all-reduce.4.cloned.1.call-update) | async-done | bytes 4718608
  234.6 2.2 constant_dynamic-slice_fusion
  236.8 1.9 copy.60
  238.8 84.4 %reduce-scatter.6.cloned.1.call-done = f32[128,1024]{0,1:T(8,128)} async-done(((f32[2048,1024]{0,1:T(8,128)}), f32[128,1024]{0,1:T(8,128)}) %reduce-scatter.6.cloned.1.call-update) | async-done | bytes 524304 | tf_op jit(solution)/shard_map/reduce_scatter | solution.py:129
  323.2 2.0 copy.62
  325.2 83.3 %reduce-scatter.8.cloned.1.call-done = f32[96,1024]{1,0:T(8,128)} async-done(((f32[1536,1024]{1,0:T(8,128)}), f32[96,1024]{1,0:T(8,128)}) %reduce-scatter.8.cloned.1.call-update) | async-done | bytes 393232
  (48 shorter events, 5.7 us)
Async XLA Ops:
  7.2 7.5 %copy-start = (bf16[1536,1024]{1,0:T(8,128)(2,1)S(1)}, bf16[1536,1024]{1,0:T(8,128)(2,1)}, u32[]{:S(2)}) copy-start(bf16[1536,1024]{1,0:T(8,128)(2,1)} %param.13) | copy-start | bytes 9437188
  11.0 3.7 copy-start.8
  19.9 8.2 %copy-start.5 = (bf16[1024]{0:T(1024)(128)(2,1)S(1)}, bf16[1024]{0:T(1024)(128)(2,1)}, u32[]{:S(2)}) copy-start(bf16[1024]{0:T(1024)(128)(2,1)} %param.14) | copy-start | bytes 6148
  19.9 39.8 %all-to-all-start = ((bf16[16,64,1024]{2,1,0:T(8,128)(2,1)}), bf16[16,64,1024]{2,1,0:T(8,128)(2,1)S(1)}, u32[]{:S(2)}, u32[]{:S(2)}) async-start(bf16[16,64,1024]{2,1,0:T(8,128)(2,1)} %copy.55), calls=%async_computation | async-start | bytes 4194304 | tf_op jit(solution)/shard_map/all_to_all | solution.py:79
  28.0 206.6 %all-reduce.4.cloned.1.call-start = ((), (), s32[]{:S(2)}) async-start(), calls=%async_computation.6 | async-start | bytes 9437184
  124.3 3.0 copy-start.3
  131.1 0.7 copy-start.6
  131.1 0.7 copy-start.7
  131.1 0.9 copy-start.4
  131.1 1.8 copy-start.2
  131.1 192.0 %reduce-scatter.6.cloned.1.call-start = ((), (), s32[]{:S(2)}) async-start(), calls=%async_computation.4 | async-start | bytes 8912896 | tf_op jit(solution)/shard_map/reduce_scatter | solution.py:129
  142.6 1.4 copy-start.9
  142.6 265.9 %reduce-scatter.8.cloned.1.call-start = ((), (), s32[]{:S(2)}) async-start(), calls=%async_computation.5 | async-start | bytes 6684672
  155.1 253.4 %copy-start.1 = (bf16[1536,1024]{1,0:T(8,128)(2,1)S(1)}, bf16[1536,1024]{1,0:T(8,128)(2,1)}, u32[]{:S(2)}) copy-start(bf16[1536,1024]{1,0:T(8,128)(2,1)} %param.13) | copy-start | bytes 9437188
  155.1 0.8 copy-start.10
Sparse Core Ops, SparseCore 0:
  131.3 103.2 all-reduce.3
  238.4 84.7 reduce-scatter.5
  327.6 80.9 reduce-scatter.7
where the time goes:
time: 416 us; the launch traced here: 415 us
  waiting for transfers between devices  276 us (66%)
  blocking collectives  51.1 us (12%)
  matrix products  36.1 us (9%)
  local copies, waits for them, and re-layouts  21.1 us (5%)
  between operations  15.2 us (4%)
  starting transfers between devices  8.22 us (2%)
  other arithmetic  7.15 us (2%)
    unnamed x5, waiting for transfers between devices  161 us
    reduce_scatter x1, waiting for transfers between devices, local(): lax.psum_scatter(kv_term, 'dp', scatter_dimension=0, tiled=True)  84.4 us
    all_to_all x1, blocking collectives, local(): lax.all_to_all(returning.reshape(groups, capacity * tile_rows, share), 'd...  32.7 us
    all_to_all x1, waiting for transfers between devices, local(): lax.all_to_all(outgoing, 'dp', split_axis=0, concat_axis=0, tiled=True)  31 us
    psum x1, blocking collectives, row_products(): return lax.psum(products, ('section', 'mp'))  18.3 us
    unnamed x28, local copies, waits for them, and re-layouts  16.9 us
    dot_general x1, matrix products, local(): lax.dot_general(key_value_grad, normed, (((0,), (0,)), ((), ())), preferr...  9.68 us
    dot_general x1, matrix products, local(): jnp.dot(key_value_grad, key_value_weight, preferred_element_type=jnp.floa...  9.25 us
  transfers between devices with their start and end apart: 4, of which 4 were waited for; matrix products, arithmetic and copies ran while one was open for 7% of the time, Pallas kernels for 0%

commit v1 on v0

v1 whole, which is shorter than its diff:
```python
import jax
import jax.numpy as jnp
from jax import lax
from jax.experimental import pallas as pl
from jax.experimental.pallas import tpu as pltpu
from jax.sharding import Mesh, PartitionSpec as P

D = 8192
epsilon = 1e-06
N = 4
TT = 32
CAP = 2
BF = jnp.bfloat16
F32 = jnp.float32
DP = ("z", "x")
Y = ("ylo", "yhi")


def shift(value, axis, size, step):
    return lax.ppermute(value, axis, [(i, (i + step) % size) for i in range(size)])


def shift_y(value, step):
    place = lambda y: (y % 2) * 2 + y // 2
    return lax.ppermute(value, Y, [(place(y), place((y + step) % N)) for y in range(N)])


def all_sum(value):
    value = value + shift(value, "core", 2, 1)
    parts = [shift_y(value, step) for step in (1, 2, 3)]
    return value + parts[0] + parts[1] + parts[2]


def slices_out(key_value_grad, member):
    blocks = N * N
    rows = key_value_grad.shape[0] // blocks
    width = key_value_grad.shape[1] // blocks

    def kernel(member_ref, source, out, sems):
        me = member_ref[0]
        copies = []
        for dest in range(blocks):
            for part in range(2):
                place = 2 * me + part
                dx, dz = place // N, place % N
                column = ((dest // N + dz) % N) * N + (dest % N + dx) % N
                copy = pltpu.make_async_copy(
                    source.at[pl.ds(dest * rows, rows), pl.ds(pl.multiple_of(column * width, width), width)],
                    out.at[dest, :, pl.ds(part * width, width)],
                    sems.at[dest * 2 + part],
                )
                copy.start()
                copies.append(copy)
        for copy in copies:
            copy.wait()

    return pl.pallas_call(
        kernel,
        out_shape=jax.ShapeDtypeStruct((blocks, rows, 2 * width), key_value_grad.dtype),
        grid_spec=pltpu.PrefetchScalarGridSpec(
            num_scalar_prefetch=1,
            grid=(1,),
            in_specs=[pl.BlockSpec(memory_space=pl.ANY)],
            out_specs=pl.BlockSpec(memory_space=pl.ANY),
            scratch_shapes=[pltpu.SemaphoreType.DMA((2 * blocks,))],
        ),
        name="slices_out",
    )(member, key_value_grad)


def block_order(source, table):
    count = table.shape[0]

    def kernel(table_ref, source_ref, out, sems):
        copies = []
        for i in range(count):
            copy = pltpu.make_async_copy(source_ref.at[table_ref[i]], out.at[i], sems.at[i])
            copy.start()
            copies.append(copy)
        for copy in copies:
            copy.wait()

    return pl.pallas_call(
        kernel,
        out_shape=jax.ShapeDtypeStruct((count,) + source.shape[1:], source.dtype),
        grid_spec=pltpu.PrefetchScalarGridSpec(
            num_scalar_prefetch=1,
            grid=(1,),
            in_specs=[pl.BlockSpec(memory_space=pl.ANY)],
            out_specs=pl.BlockSpec(memory_space=pl.ANY),
            scratch_shapes=[pltpu.SemaphoreType.DMA((count,))],
        ),
        name="block_order",
    )(table, source)


def pick_tiles(received, dests):
    tiles = dests.shape[0]
    slots, _, width = received.shape

    def kernel(dest_ref, source, out):
        names = [dest_ref[j] for j in range(tiles)]
        for j in range(tiles):
            before = jnp.int32(0)
            for i in range(j):
                before = before + (names[i] == names[j]).astype(jnp.int32)
            out[j] = source[names[j] * CAP + before]

    return pl.pallas_call(
        kernel,
        out_shape=jax.ShapeDtypeStruct((tiles, TT, width), received.dtype),
        grid_spec=pltpu.PrefetchScalarGridSpec(
            num_scalar_prefetch=1,
            grid=(1,),
            in_specs=[pl.BlockSpec((slots, TT, width), lambda i, t: (0, 0, 0))],
            out_specs=pl.BlockSpec((tiles, TT, width), lambda i, t: (0, 0, 0)),
        ),
        name="pick_tiles",
    )(dests, received)


def assemble(pieces, places):
    rows, wide = pieces[0].shape
    width = wide // 2
    count = len(pieces)

    def kernel(place_ref, *refs):
        sources, first, second = refs[:count], refs[count], refs[count + 1]
        for p in range(count):
            for part in range(2):
                place = 2 * place_ref[p] + part
                other = (place % N) * N + place // N
                value = sources[p][:, part * width:(part + 1) * width]
                first[:, pl.ds(pl.multiple_of(place * width, width), width)] = value
                second[:, pl.ds(pl.multiple_of(other * width, width), width)] = value

    shape = jax.ShapeDtypeStruct((rows, wide * count), pieces[0].dtype)
    whole = pl.BlockSpec((rows, wide * count), lambda i, t: (0, 0))
    return pl.pallas_call(
        kernel,
        out_shape=(shape, shape),
        grid_spec=pltpu.PrefetchScalarGridSpec(
            num_scalar_prefetch=1,
            grid=(1,),
            in_specs=[pl.BlockSpec((rows, wide), lambda i, t: (0, 0))] * count,
            out_specs=(whole, whole),
        ),
        compiler_params=pltpu.CompilerParams(vmem_limit_bytes=40 * 1024 * 1024),
        name="assemble",
    )(places, *pieces)


def reduce_scatter(piece, first, second, rows, part):
    big = N * rows
    half = 2 * rows
    down = rows - part
    ahead = shift(piece(big + half, big).astype(BF), first, N, 1)
    behind = shift(piece(2 * big + half, big).astype(BF), first, N, 3)
    ahead2 = shift((piece(big, half) + ahead[half:].astype(F32)).astype(BF), first, N, 1)
    behind2 = shift((piece(3 * big + half, half) + behind[:half].astype(F32)).astype(BF), first, N, 3)

    def low(start, stop):
        return (
            piece(start, stop - start)
            + behind[half + start:half + stop].astype(F32)
            + ahead2[start:stop].astype(F32)
        )

    def high(start, stop):
        return (
            piece(start, stop - start)
            + ahead[start - half:stop - half].astype(F32)
            + behind2[start - half:stop - half].astype(F32)
        )

    send_a = jnp.concatenate(
        [low(rows + part, half).astype(BF), high(half, half + part).astype(BF)], axis=0
    )
    send_b = high(half + part, half + rows + part).astype(BF)
    ahead3 = shift(send_a, second, N, 1)
    behind3 = shift(send_b, second, N, 3)
    ahead4 = shift((low(rows, rows + part) + ahead3[down:].astype(F32)).astype(BF), second, N, 1)
    behind4 = shift(
        (high(half + rows + part, big) + behind3[:down].astype(F32)).astype(BF), second, N, 3
    )
    top = low(0, part) + behind3[down:].astype(F32) + ahead4.astype(F32)
    bottom = low(part, rows) + ahead3[:down].astype(F32) + behind4.astype(F32)
    return jnp.concatenate([top, bottom], axis=0)


def local(
    siglip_features,
    convnext_features,
    siglip_projection,
    convnext_projection,
    newline_embed,
    key_value_weight,
    tile_rank,
    row_end,
    key_value_grad,
    newline_grad,
):
    blocks = N * N
    z, x = lax.axis_index("z"), lax.axis_index("x")
    ylo, core, yhi = lax.axis_index("ylo"), lax.axis_index("core"), lax.axis_index("yhi")
    my_rank = z * N + x
    member = (ylo * 2 + core) * 2 + yhi
    tiles = tile_rank.shape[0]
    per_device = tiles // blocks
    rows = siglip_features.shape[0]
    share = siglip_projection.shape[1]
    half = share // 2
    kv_rows = key_value_weight.shape[0] // blocks
    sig_rows = siglip_features.shape[1] // blocks
    conv_rows = convnext_features.shape[1] // blocks

    dest_rank = tile_rank.reshape(tiles)
    mine = lax.dynamic_slice_in_dim(dest_rank, my_rank * per_device, per_device)
    outgoing = slices_out(key_value_grad, member.reshape(1).astype(jnp.int32))
    received = lax.all_to_all(outgoing, DP, split_axis=0, concat_axis=0, tiled=True)

    projected = (
        jnp.dot(siglip_features, siglip_projection, preferred_element_type=F32)
        + jnp.dot(convnext_features, convnext_projection, preferred_element_type=F32)
    ).astype(BF)
    proj_values = projected.astype(F32)
    line_vector = newline_embed.astype(F32)
    squares = jnp.sum(proj_values * proj_values, axis=1).reshape(rows // 128, 128)
    line_square = jnp.broadcast_to(jnp.sum(line_vector * line_vector), (4, 128))
    statistic = all_sum(jnp.concatenate([squares, line_square], axis=0))
    inverse = lax.rsqrt(statistic[: rows // 128].reshape(rows) / D + epsilon)[:, None]
    line_normed = (line_vector * lax.rsqrt(statistic[rows // 128, 0] / D + epsilon)).astype(BF).astype(F32)
    normed = (proj_values * inverse).astype(BF)

    step = jnp.arange(blocks, dtype=jnp.int32)
    outer, inner = step // N, step % N
    table1 = ((z + inner) % N) * N + (x + outer) % N
    table2 = ((z + outer) % N) * N + (x + inner) % N
    features = jnp.concatenate(
        [
            siglip_features.T.reshape(blocks, sig_rows, rows),
            convnext_features.T.reshape(blocks, conv_rows, rows),
        ],
        axis=1,
    )
    x_rows = sig_rows + conv_rows
    features1 = block_order(features, table1).reshape(blocks * x_rows, rows)
    features2 = block_order(features, table2).reshape(blocks * x_rows, rows)
    weight = block_order(key_value_weight.reshape(blocks, kv_rows, share), table1).reshape(
        blocks * kv_rows, share
    )

    onehot = (dest_rank[:, None] == jnp.arange(blocks, dtype=jnp.int32)[None, :]).astype(jnp.int32)
    grouped = onehot.reshape(blocks, per_device, blocks)
    before = jnp.cumsum(grouped, axis=1) - grouped
    slot_place = jnp.sum(before * grouped, axis=2).reshape(tiles)
    slot = (jnp.arange(tiles, dtype=jnp.int32) // per_device) * CAP + slot_place
    live = (dest_rank == my_rank) & (row_end == 1)
    mask = jnp.sum(
        ((slot[:, None] == jnp.arange(blocks * CAP, dtype=jnp.int32)[None, :]) & live[:, None]).astype(
            jnp.int32
        ),
        axis=0,
    )
    line_total = jnp.dot(mask.astype(BF)[None, :], newline_grad, preferred_element_type=F32)[0]
    line_blocks = line_total.reshape(blocks, kv_rows)
    line1 = line_blocks[table1].reshape(blocks * kv_rows)[:, None]
    line2 = line_blocks[table2].reshape(blocks * kv_rows)[:, None]

    own = pick_tiles(received.reshape(blocks * CAP, TT, received.shape[2]), mine).reshape(
        rows, received.shape[2]
    )
    ring = [own] + [shift_y(own, s) for s in (1, 3, 2)]
    pieces = ring + [shift(piece, "core", 2, 1) for piece in ring]
    places = []
    y = yhi * 2 + ylo
    for side in (0, 1):
        for s in (0, 1, 3, 2):
            other = (y - s) % N
            places.append(((other % 2) * 2 + (core + side) % 2) * 2 + other // 2)
    grads1, grads2 = assemble(pieces, jnp.stack(places).astype(jnp.int32))

    def kv_piece(grads, line, columns):
        right = normed[:, columns]
        across = line_normed[None, columns]

        def piece(start, count):
            return (
                lax.dot_general(
                    grads[:, start:start + count],
                    right,
                    (((0,), (0,)), ((), ())),
                    preferred_element_type=F32,
                )
                + line[start:start + count] * across
            )

        return piece

    left, right = slice(0, half), slice(half, share)
    kv_result = jnp.concatenate(
        [
            reduce_scatter(kv_piece(grads1, line1, left), "x", "z", kv_rows, kv_rows // 2),
            reduce_scatter(kv_piece(grads2, line2, right), "z", "x", kv_rows, kv_rows // 2),
        ],
        axis=1,
    )

    grad_values = jnp.dot(grads1, weight, preferred_element_type=F32).astype(BF).astype(F32)
    products = all_sum(jnp.sum(grad_values * proj_values, axis=1).reshape(rows // 128, 128))
    products = products.reshape(rows)[:, None]
    projected_grad = (
        inverse * grad_values - inverse**3 * proj_values * products / D
    ).astype(BF)

    def x_piece(lhs, columns):
        right = projected_grad[:, columns]

        def piece(start, count):
            return jnp.dot(lhs[start:start + count], right, preferred_element_type=F32)

        return piece

    part = (x_rows // 2 + 7) // 8 * 8
    x_result = jnp.concatenate(
        [
            reduce_scatter(x_piece(features1, left), "x", "z", x_rows, part),
            reduce_scatter(x_piece(features2, right), "z", "x", x_rows, part),
        ],
        axis=1,
    )
    return x_result[:sig_rows], x_result[sig_rows:], kv_result


def solution(mesh):
    fine = Mesh(mesh.devices.reshape(2, 2, N, N, 2), ("ylo", "core", "z", "x", "yhi"))
    wide = ("ylo", "core", "yhi")
    in_specs = (
        P(DP, None),
        P(DP, None),
        P(None, wide),
        P(None, wide),
        P(wide),
        P(None, wide),
        P(),
        P(),
        P(DP, None),
        P(DP, None),
    )
    out_specs = (P(DP, wide), P(DP, wide), P(DP, wide))
    return jax.shard_map(local, mesh=fine, in_specs=in_specs, out_specs=out_specs, check_vma=False)
```

time: 416 us -> 518 us (1.25)
  Pallas kernels: 0 us -> 323 us
  waiting for transfers between devices: 276 us -> 63.2 us
  starting transfers between devices: 8.22 us -> 62.8 us
  blocking collectives: 51.1 us -> 0 us
  between operations: 15.2 us -> 2.27 us
    pallas_call x0 -> x6, Pallas kernels: none -> 323 us  [the longest x3 300 us: block_order(): pl.pallas_call(kernel, out_shape=jax.ShapeDtypeStruct((count,) + source.s...]
    unnamed x5 -> x0, waiting for transfers between devices: 161 us -> none
    reduce_scatter x1 -> x0, waiting for transfers between devices: 84.4 us -> none  [local(): lax.psum_scatter(kv_term, 'dp', scatter_dimension=0, tiled=True)]
    ppermute x0 -> x47, waiting for transfers between devices: none -> 63.2 us  [the longest x38 53.8 us: shift(): lax.ppermute(value, axis, [(i, (i + step) % size) for i in range(size)])]
    ppermute x0 -> x47, starting transfers between devices: none -> 54.7 us  [the longest x38 39.1 us: shift(): lax.ppermute(value, axis, [(i, (i + step) % size) for i in range(size)])]
    all_to_all x1 -> x0, blocking collectives: 32.7 us -> none  [local(): lax.all_to_all(returning.reshape(groups, capacity * tile_rows, share), 'd...]
    all_to_all x1, waiting for transfers between devices: 31 us -> 0.01 us  [local(): lax.all_to_all(outgoing, DP, split_axis=0, concat_axis=0, tiled=True)]
    psum x1 -> x0, blocking collectives: 18.3 us -> none  [row_products(): return lax.psum(products, ('section', 'mp'))]
  transfers between devices with their start and end apart: 4 -> 48, of which waited for: 4 -> 17; matrix products, arithmetic and copies ran while one was open for 7% -> 10% of each run, Pallas kernels for 0% -> 58%
where the time goes in v1:
time: 518 us; the launch traced here: 517 us
  Pallas kernels  323 us (62%)
  waiting for transfers between devices  63.2 us (12%)
  starting transfers between devices  62.8 us (12%)
  matrix products  38.4 us (7%)
  local copies, waits for them, and re-layouts  17.3 us (3%)
  other arithmetic  10 us (2%)
    pallas_call x3, Pallas kernels, block_order(): pl.pallas_call(kernel, out_shape=jax.ShapeDtypeStruct((count,) + source.s...  300 us
    ppermute x38, waiting for transfers between devices, shift(): lax.ppermute(value, axis, [(i, (i + step) % size) for i in range(size)])  53.8 us
    ppermute x38, starting transfers between devices, shift(): lax.ppermute(value, axis, [(i, (i + step) % size) for i in range(size)])  39.1 us
    dot_general x22, matrix products, piece(): return jnp.dot(lhs[start:start + count], right, preferred_element_type=F32)  19.2 us
    pallas_call x1, Pallas kernels, slices_out(): pl.pallas_call(kernel, out_shape=jax.ShapeDtypeStruct((blocks, rows, 2 *...  17.3 us
    ppermute x9, starting transfers between devices, shift_y(): lax.ppermute(value, Y, [(place(y), place((y + step) % N)) for y in range(...  15.6 us
  transfers between devices with their start and end apart: 48, of which 17 were waited for; matrix products, arithmetic and copies ran while one was open for 10% of the time, Pallas kernels for 58%

profile of v1, /device:TPU:0, one launch (start us, length us, event | category | flops | bytes accessed | tf_op | source)
XLA Modules:
  0.0 516.6 jit_solution(11590886098541884151)
XLA Ops:
  0.7 17.3 %slices_out.1 = bf16[16,64,256]{2,1,0:T(8,128)(2,1)} custom-call(s32[1]{0:T(128)} %bitcast.16.member_ref, bf16[1024,2048]{1,0:T(8,128)(2,1)} %source.1), custom_call_target="tpu_custom_call" | custom-call | tf_op jit(solution)/shard_map/slices_out/pallas_call | solution.py:57
  18.0 8.0 %all-to-all-start = ((bf16[16,64,256]{2,1,0:T(8,128)(2,1)}), bf16[16,64,256]{2,1,0:T(8,128)(2,1)}, u32[]{:S(2)}, u32[]{:S(2)}) async-start(bf16[16,64,256]{2,1,0:T(8,128)(2,1)} %slices_out.1), calls=%async_computation | async-start | bytes 1048576 | tf_op jit(solution)/shard_map/all_to_all | solution.py:220
  35.3 3.5 pad_maximum_fusion.source_ref
  38.8 85.3 %block_order.3 = bf16[16,168,512]{2,1,0:T(8,128)(2,1)} custom-call(s32[16]{0:T(128)} %get-tuple-element.42.table_ref, bf16[16,168,512]{2,1,0:T(8,128)(2,1)} %pad_maximum_fusion.source_ref), custom_call_target="tpu_custom_call" | custom-call | tf_op jit(solution)/shard_map/block_order/pallas_call | solution.py:83
  126.6 85.3 %block_order.5 = bf16[16,168,512]{2,1,0:T(8,128)(2,1)} custom-call(s32[16]{0:T(128)} %get-tuple-element.43.table_ref, bf16[16,168,512]{2,1,0:T(8,128)(2,1)} %pad_maximum_fusion.source_ref), custom_call_target="tpu_custom_call" | custom-call | tf_op jit(solution)/shard_map/block_order/pallas_call | solution.py:83
  215.0 4.9 fusion.234
  222.4 3.2 collective-permute-start.6
  233.5 4.1 collective-permute-done.4.refs_1_
  238.2 129.1 %block_order.4 = bf16[16,128,1024]{2,1,0:T(8,128)(2,1)} custom-call(s32[16]{0:T(128)} %get-tuple-element.42.table_ref, bf16[16,128,1024]{2,1,0:T(8,128)(2,1)} %bitcast.140), custom_call_target="tpu_custom_call" | custom-call | tf_op jit(solution)/shard_map/block_order/pallas_call | solution.py:83
  368.6 3.2 assemble.1
  371.8 4.7 convolution_convert_fusion
  420.6 7.7 %collective-permute-done.16 = bf16[672,512]{1,0:T(8,128)(2,1)S(1)} collective-permute-done((bf16[672,512]{1,0:T(8,128)(2,1)S(1)}, bf16[672,512]{1,0:T(8,128)(2,1)S(1)}, u32[]{:S(2)}, u32[]{:S(2)}) %collective-permute-start.16) | collective-permute-done | bytes 688160 | tf_op jit(solution)/shard_map/ppermute | solution.py:20
  445.0 5.8 %collective-permute-done.36 = bf16[128,512]{1,0:T(8,128)(2,1)S(1)} collective-permute-done((bf16[128,512]{1,0:T(8,128)(2,1)S(1)}, bf16[128,512]{1,0:T(8,128)(2,1)S(1)}, u32[]{:S(2)}, u32[]{:S(2)}) %collective-permute-start.36) | collective-permute-done | bytes 131104 | tf_op jit(solution)/shard_map/ppermute | solution.py:20
  451.1 4.7 collective-permute-done.35
  456.7 5.3 %collective-permute-done.44 = bf16[128,512]{1,0:T(8,128)(2,1)S(1)} collective-permute-done((bf16[128,512]{1,0:T(8,128)(2,1)S(1)}, bf16[128,512]{1,0:T(8,128)(2,1)S(1)}, u32[]{:S(2)}, u32[]{:S(2)}) %collective-permute-start.44) | collective-permute-done | bytes 131104 | tf_op jit(solution)/shard_map/ppermute | solution.py:20
  462.2 4.7 collective-permute-done.43
  467.3 5.1 collective-permute-done.37
  472.7 4.0 collective-permute-done.38
  477.0 5.1 collective-permute-done.45
  482.4 4.4 collective-permute-done.46
  491.5 3.3 collective-permute-start.19
  498.3 3.3 collective-permute-start.27
  503.9 3.3 collective-permute-start.22
  509.6 3.3 collective-permute-start.30
  (213 shorter events, 105.8 us)
Async XLA Ops:
  18.0 201.9 %all-to-all-start = ((bf16[16,64,256]{2,1,0:T(8,128)(2,1)}), bf16[16,64,256]{2,1,0:T(8,128)(2,1)}, u32[]{:S(2)}, u32[]{:S(2)}) async-start(bf16[16,64,256]{2,1,0:T(8,128)(2,1)} %slices_out.1), calls=%async_computation | async-start | bytes 1048576 | tf_op jit(solution)/shard_map/all_to_all | solution.py:220
  225.6 12.0 %collective-permute-start.4 = (bf16[512,256]{1,0:T(8,128)(2,1)}, bf16[512,256]{1,0:T(8,128)(2,1)}, u32[]{:S(2)}, u32[]{:S(2)}) collective-permute-start(bf16[512,256]{1,0:T(8,128)(2,1)} %bitcast.120), channel_id=1, source_target_pairs={{0,64},{64,1},{1,65},{65,0},{2,66},{66,3},{3,67},{67,2},{4,68},{68... | collective-permute-start | bytes 786440 | tf_op jit(solution)/shard_map/ppermute | solution.py:25
  226.3 11.7 %collective-permute-start.5 = (bf16[512,256]{1,0:T(8,128)(2,1)}, bf16[512,256]{1,0:T(8,128)(2,1)}, u32[]{:S(2)}, u32[]{:S(2)}) collective-permute-start(bf16[512,256]{1,0:T(8,128)(2,1)} %bitcast.121), channel_id=1, source_target_pairs={{0,65},{64,0},{1,64},{65,1},{2,67},{66,2},{3,66},{67,3},{4,69},{68... | collective-permute-start | bytes 786440 | tf_op jit(solution)/shard_map/ppermute | solution.py:25
  230.9 137.6 %collective-permute-start.7 = (bf16[512,256]{1,0:T(8,128)(2,1)}, bf16[512,256]{1,0:T(8,128)(2,1)}, u32[]{:S(2)}, u32[]{:S(2)}) collective-permute-start(bf16[512,256]{1,0:T(8,128)(2,1)} %bitcast.122), channel_id=1, source_target_pairs={{0,32},{32,0},{1,33},{33,1},{2,34},{34,2},{3,35},{35,3},{4,36},{36... | collective-permute-start | bytes 786440 | tf_op jit(solution)/shard_map/ppermute | solution.py:20
  233.5 135.1 %collective-permute-start.10 = (bf16[512,256]{1,0:T(8,128)(2,1)}, bf16[512,256]{1,0:T(8,128)(2,1)}, u32[]{:S(2)}, u32[]{:S(2)}) collective-permute-start(bf16[512,256]{1,0:T(8,128)(2,1)} %collective-permute-done.6.refs_3_), channel_id=1, source_target_pairs={{0,32},{32,0},{1,33},{33,1},{2,34},{34,2},{3,35},{35,3},{4,36},{36... | collective-permute-start | bytes 786440 | tf_op jit(solution)/shard_map/ppermute | solution.py:20
  237.6 130.9 %collective-permute-start.8 = (bf16[512,256]{1,0:T(8,128)(2,1)}, bf16[512,256]{1,0:T(8,128)(2,1)}, u32[]{:S(2)}, u32[]{:S(2)}) collective-permute-start(bf16[512,256]{1,0:T(8,128)(2,1)} %collective-permute-done.4.refs_1_), channel_id=1, source_target_pairs={{0,32},{32,0},{1,33},{33,1},{2,34},{34,2},{3,35},{35,3},{4,36},{36... | collective-permute-start | bytes 786440 | tf_op jit(solution)/shard_map/ppermute | solution.py:20
  238.0 130.6 %collective-permute-start.9 = (bf16[512,256]{1,0:T(8,128)(2,1)}, bf16[512,256]{1,0:T(8,128)(2,1)}, u32[]{:S(2)}, u32[]{:S(2)}) collective-permute-start(bf16[512,256]{1,0:T(8,128)(2,1)} %collective-permute-done.5.refs_2_), channel_id=1, source_target_pairs={{0,32},{32,0},{1,33},{33,1},{2,34},{34,2},{3,35},{35,3},{4,36},{36... | collective-permute-start | bytes 786440 | tf_op jit(solution)/shard_map/ppermute | solution.py:20
  397.5 16.1 %collective-permute-start.32 = (bf16[512,512]{1,0:T(8,128)(2,1)S(1)}, bf16[512,512]{1,0:T(8,128)(2,1)S(1)}, u32[]{:S(2)}, u32[]{:S(2)}) collective-permute-start(bf16[512,512]{1,0:T(8,128)(2,1)S(1)} %fusion.8), channel_id=1, source_target_pairs={{0,2},{2,4},{4,6},{6,0},{1,3},{3,5},{5,7},{7,1},{8,10},{10,12},{12... | collective-permute-start | bytes 1572872 | tf_op jit(solution)/shard_map/ppermute | solution.py:20
  399.6 15.9 %collective-permute-start.31 = (bf16[512,512]{1,0:T(8,128)(2,1)S(1)}, bf16[512,512]{1,0:T(8,128)(2,1)S(1)}, u32[]{:S(2)}, u32[]{:S(2)}) collective-permute-start(bf16[512,512]{1,0:T(8,128)(2,1)S(1)} %fusion.7), channel_id=1, source_target_pairs={{0,6},{2,0},{4,2},{6,4},{1,7},{3,1},{5,3},{7,5},{8,14},{10,8},{12,... | collective-permute-start | bytes 1572872 | tf_op jit(solution)/shard_map/ppermute | solution.py:20
  401.8 15.6 %collective-permute-start.40 = (bf16[512,512]{1,0:T(8,128)(2,1)S(1)}, bf16[512,512]{1,0:T(8,128)(2,1)S(1)}, u32[]{:S(2)}, u32[]{:S(2)}) collective-permute-start(bf16[512,512]{1,0:T(8,128)(2,1)S(1)} %fusion.10), channel_id=1, source_target_pairs={{0,8},{8,16},{16,24},{24,0},{1,9},{9,17},{17,25},{25,1},{2,10},{10... | collective-permute-start | bytes 1572872 | tf_op jit(solution)/shard_map/ppermute | solution.py:20
  404.0 15.7 %collective-permute-start.39 = (bf16[512,512]{1,0:T(8,128)(2,1)S(1)}, bf16[512,512]{1,0:T(8,128)(2,1)S(1)}, u32[]{:S(2)}, u32[]{:S(2)}) collective-permute-start(bf16[512,512]{1,0:T(8,128)(2,1)S(1)} %fusion.9), channel_id=1, source_target_pairs={{0,24},{8,0},{16,8},{24,16},{1,25},{9,1},{17,9},{25,17},{2,26},{10... | collective-permute-start | bytes 1572872 | tf_op jit(solution)/shard_map/ppermute | solution.py:20
  406.2 22.0 %collective-permute-start.16 = (bf16[672,512]{1,0:T(8,128)(2,1)S(1)}, bf16[672,512]{1,0:T(8,128)(2,1)S(1)}, u32[]{:S(2)}, u32[]{:S(2)}) collective-permute-start(bf16[672,512]{1,0:T(8,128)(2,1)S(1)} %convolution_convert_fusion.3), channel_id=1, source_target_pairs={{0,2},{2,4},{4,6},{6,0},{1,3},{3,5},{5,7},{7,1},{8,10},{10,12},{12... | collective-permute-start | bytes 2064392 | tf_op jit(solution)/shard_map/ppermute | solution.py:20
  413.6 16.5 %collective-permute-start.15 = (bf16[672,512]{1,0:T(8,128)(2,1)S(1)}, bf16[672,512]{1,0:T(8,128)(2,1)S(1)}, u32[]{:S(2)}, u32[]{:S(2)}) collective-permute-start(bf16[672,512]{1,0:T(8,128)(2,1)S(1)} %convolution_convert_fusion.4), channel_id=1, source_target_pairs={{0,6},{2,0},{4,2},{6,4},{1,7},{3,1},{5,3},{7,5},{8,14},{10,8},{12,... | collective-permute-start | bytes 2064392 | tf_op jit(solution)/shard_map/ppermute | solution.py:20
  415.6 16.5 %collective-permute-start.24 = (bf16[672,512]{1,0:T(8,128)(2,1)S(1)}, bf16[672,512]{1,0:T(8,128)(2,1)S(1)}, u32[]{:S(2)}, u32[]{:S(2)}) collective-permute-start(bf16[672,512]{1,0:T(8,128)(2,1)S(1)} %convolution_convert_fusion.1), channel_id=1, source_target_pairs={{0,8},{8,16},{16,24},{24,0},{1,9},{9,17},{17,25},{25,1},{2,10},{10... | collective-permute-start | bytes 2064392 | tf_op jit(solution)/shard_map/ppermute | solution.py:20
  417.5 16.8 %collective-permute-start.23 = (bf16[672,512]{1,0:T(8,128)(2,1)S(1)}, bf16[672,512]{1,0:T(8,128)(2,1)S(1)}, u32[]{:S(2)}, u32[]{:S(2)}) collective-permute-start(bf16[672,512]{1,0:T(8,128)(2,1)S(1)} %convolution_convert_fusion.2), channel_id=1, source_target_pairs={{0,24},{8,0},{16,8},{24,16},{1,25},{9,1},{17,9},{25,17},{2,26},{10... | collective-permute-start | bytes 2064392 | tf_op jit(solution)/shard_map/ppermute | solution.py:20
  419.7 15.5 %collective-permute-start.33 = (bf16[256,512]{1,0:T(8,128)(2,1)S(1)}, bf16[256,512]{1,0:T(8,128)(2,1)S(1)}, u32[]{:S(2)}, u32[]{:S(2)}) collective-permute-start(bf16[256,512]{1,0:T(8,128)(2,1)S(1)} %fusion.15), channel_id=1, source_target_pairs={{0,2},{2,4},{4,6},{6,0},{1,3},{3,5},{5,7},{7,1},{8,10},{10,12},{12... | collective-permute-start | bytes 786440 | tf_op jit(solution)/shard_map/ppermute | solution.py:20
  430.2 14.4 %collective-permute-start.41 = (bf16[256,512]{1,0:T(8,128)(2,1)S(1)}, bf16[256,512]{1,0:T(8,128)(2,1)S(1)}, u32[]{:S(2)}, u32[]{:S(2)}) collective-permute-start(bf16[256,512]{1,0:T(8,128)(2,1)S(1)} %fusion.17), channel_id=1, source_target_pairs={{0,8},{8,16},{16,24},{24,0},{1,9},{9,17},{17,25},{25,1},{2,10},{10... | collective-permute-start | bytes 786440 | tf_op jit(solution)/shard_map/ppermute | solution.py:20
  434.3 53.6 %collective-permute-start.17 = (bf16[336,512]{1,0:T(8,128)(2,1)S(1)}, bf16[336,512]{1,0:T(8,128)(2,1)S(1)}, u32[]{:S(2)}, u32[]{:S(2)}) collective-permute-start(bf16[336,512]{1,0:T(8,128)(2,1)S(1)} %add_convert_fusion.4), channel_id=1, source_target_pairs={{0,2},{2,4},{4,6},{6,0},{1,3},{3,5},{5,7},{7,1},{8,10},{10,12},{12... | collective-permute-start | bytes 1032200 | tf_op jit(solution)/shard_map/ppermute | solution.py:20
  435.2 53.9 %collective-permute-start.18 = (bf16[336,512]{1,0:T(8,128)(2,1)S(1)}, bf16[336,512]{1,0:T(8,128)(2,1)S(1)}, u32[]{:S(2)}, u32[]{:S(2)}) collective-permute-start(bf16[336,512]{1,0:T(8,128)(2,1)S(1)} %add_convert_fusion.3), channel_id=1, source_target_pairs={{0,6},{2,0},{4,2},{6,4},{1,7},{3,1},{5,3},{7,5},{8,14},{10,8},{12,... | collective-permute-start | bytes 1032200 | tf_op jit(solution)/shard_map/ppermute | solution.py:20
  438.6 56.2 %collective-permute-start.25 = (bf16[336,512]{1,0:T(8,128)(2,1)S(1)}, bf16[336,512]{1,0:T(8,128)(2,1)S(1)}, u32[]{:S(2)}, u32[]{:S(2)}) collective-permute-start(bf16[336,512]{1,0:T(8,128)(2,1)S(1)} %add_convert_fusion.2), channel_id=1, source_target_pairs={{0,8},{8,16},{16,24},{24,0},{1,9},{9,17},{17,25},{25,1},{2,10},{10... | collective-permute-start | bytes 1032200 | tf_op jit(solution)/shard_map/ppermute | solution.py:20
  441.2 54.6 %collective-permute-start.26 = (bf16[336,512]{1,0:T(8,128)(2,1)S(1)}, bf16[336,512]{1,0:T(8,128)(2,1)S(1)}, u32[]{:S(2)}, u32[]{:S(2)}) collective-permute-start(bf16[336,512]{1,0:T(8,128)(2,1)S(1)} %add_convert_fusion.1), channel_id=1, source_target_pairs={{0,24},{8,0},{16,8},{24,16},{1,25},{9,1},{17,9},{25,17},{2,26},{10... | collective-permute-start | bytes 1032200 | tf_op jit(solution)/shard_map/ppermute | solution.py:20
  490.2 11.4 %collective-permute-start.20 = (bf16[168,512]{1,0:T(8,128)(2,1)S(1)}, bf16[168,512]{1,0:T(8,128)(2,1)S(1)}, u32[]{:S(2)}, u32[]{:S(2)}) collective-permute-start(bf16[168,512]{1,0:T(8,128)(2,1)S(1)} %pad_maximum_fusion.3), channel_id=1, source_target_pairs={{0,8},{8,16},{16,24},{24,0},{1,9},{9,17},{17,25},{25,1},{2,10},{10... | collective-permute-start | bytes 516104 | tf_op jit(solution)/shard_map/ppermute | solution.py:20
  491.5 11.3 %collective-permute-start.19 = (bf16[168,512]{1,0:T(8,128)(2,1)S(1)}, bf16[168,512]{1,0:T(8,128)(2,1)S(1)}, u32[]{:S(2)}, u32[]{:S(2)}) collective-permute-start(bf16[168,512]{1,0:T(8,128)(2,1)S(1)} %add_convert_fusion.6), channel_id=1, source_target_pairs={{0,24},{8,0},{16,8},{24,16},{1,25},{9,1},{17,9},{25,17},{2,26},{10... | collective-permute-start | bytes 516104 | tf_op jit(solution)/shard_map/ppermute | solution.py:20
  502.7 12.2 %collective-permute-start.21 = (bf16[88,512]{1,0:T(8,128)(2,1)S(1)}, bf16[88,512]{1,0:T(8,128)(2,1)S(1)}, u32[]{:S(2)}, u32[]{:S(2)}) collective-permute-start(bf16[88,512]{1,0:T(8,128)(2,1)S(1)} %add_convert_fusion.9), channel_id=1, source_target_pairs={{0,8},{8,16},{16,24},{24,0},{1,9},{9,17},{17,25},{25,1},{2,10},{10... | collective-permute-start | bytes 270344 | tf_op jit(solution)/shard_map/ppermute | solution.py:20
  (39 other events, 797.9 us)

commit v2 on v1

--- a/solution.py
+++ b/solution.py
@@ -61,11 +61,41 @@
             num_scalar_prefetch=1,
             grid=(1,),
             in_specs=[pl.BlockSpec(memory_space=pl.ANY)],
-            out_specs=pl.BlockSpec(memory_space=pl.ANY),
+            out_specs=pl.BlockSpec(memory_space=pltpu.VMEM),
             scratch_shapes=[pltpu.SemaphoreType.DMA((2 * blocks,))],
         ),
         name="slices_out",
     )(member, key_value_grad)
+
+
+CUTS = ((6, 10), (10, 14), (4, 6), (14, 16), (0, 4))
+
+
+def cut_orders(source, tables):
+    blocks, rows, width = source.shape
+    orders = tables.shape[0] // blocks
+
+    def kernel(table_ref, source_ref, *outs):
+        for order in range(orders):
+            for piece, (start, stop) in enumerate(CUTS):
+                out = outs[order * len(CUTS) + piece]
+                for i in range(start, stop):
+                    out[(i - start) * rows:(i - start + 1) * rows] = source_ref[table_ref[order * blocks + i]]
+
+    shapes = [jax.ShapeDtypeStruct(((stop - start) * rows, width), source.dtype) for start, stop in CUTS] * orders
+    outs = pl.pallas_call(
+        kernel,
+        out_shape=shapes,
+        grid_spec=pltpu.PrefetchScalarGridSpec(
+            num_scalar_prefetch=1,
+            grid=(1,),
+            in_specs=[pl.BlockSpec(source.shape, lambda i, t: (0, 0, 0))],
+            out_specs=[pl.BlockSpec(shape.shape, lambda i, t: (0, 0)) for shape in shapes],
+        ),
+        compiler_params=pltpu.CompilerParams(vmem_limit_bytes=40 * 1024 * 1024),
+        name="cut_orders",
+    )(tables, source)
+    return [outs[order * len(CUTS):(order + 1) * len(CUTS)] for order in range(orders)]
 
 
 def block_order(source, table):
@@ -87,9 +117,10 @@
             num_scalar_prefetch=1,
             grid=(1,),
             in_specs=[pl.BlockSpec(memory_space=pl.ANY)],
-            out_specs=pl.BlockSpec(memory_space=pl.ANY),
+            out_specs=pl.BlockSpec(memory_space=pltpu.VMEM),
             scratch_shapes=[pltpu.SemaphoreType.DMA((count,))],
         ),
+        compiler_params=pltpu.CompilerParams(vmem_limit_bytes=16 * 1024 * 1024),
         name="block_order",
     )(table, source)
 
@@ -125,67 +156,93 @@
     count = len(pieces)
 
     def kernel(place_ref, *refs):
-        sources, first, second = refs[:count], refs[count], refs[count + 1]
+        sources = refs[:count]
+        whole = refs[count]
+        cuts = refs[count + 1:count + 1 + 2 * len(CUTS)]
+        second = refs[-1]
         for p in range(count):
             for part in range(2):
                 place = 2 * place_ref[p] + part
                 other = (place % N) * N + place // N
                 value = sources[p][:, part * width:(part + 1) * width]
-                first[:, pl.ds(pl.multiple_of(place * width, width), width)] = value
+                whole[:, pl.ds(pl.multiple_of(place * width, width), width)] = value
                 second[:, pl.ds(pl.multiple_of(other * width, width), width)] = value
-
-    shape = jax.ShapeDtypeStruct((rows, wide * count), pieces[0].dtype)
-    whole = pl.BlockSpec((rows, wide * count), lambda i, t: (0, 0))
-    return pl.pallas_call(
+        for order, source in enumerate((whole, second)):
+            for piece, (start, stop) in enumerate(CUTS):
+                cuts[order * len(CUTS) + piece][...] = source[:, start * width:stop * width]
+
+    dtype = pieces[0].dtype
+    shapes = [jax.ShapeDtypeStruct((rows, wide * count), dtype)] + [
+        jax.ShapeDtypeStruct((rows, (stop - start) * width), dtype) for start, stop in CUTS
+    ] * 2
+    outs = pl.pallas_call(
         kernel,
-        out_shape=(shape, shape),
+        out_shape=shapes,
         grid_spec=pltpu.PrefetchScalarGridSpec(
             num_scalar_prefetch=1,
             grid=(1,),
             in_specs=[pl.BlockSpec((rows, wide), lambda i, t: (0, 0))] * count,
-            out_specs=(whole, whole),
+            out_specs=[pl.BlockSpec(shape.shape, lambda i, t: (0, 0)) for shape in shapes],
+            scratch_shapes=[pltpu.VMEM((rows, wide * count), dtype)],
         ),
         compiler_params=pltpu.CompilerParams(vmem_limit_bytes=40 * 1024 * 1024),
         name="assemble",
     )(places, *pieces)
-
-
-def reduce_scatter(piece, first, second, rows, part):
-    big = N * rows
-    half = 2 * rows
-    down = rows - part
-    ahead = shift(piece(big + half, big).astype(BF), first, N, 1)
-    behind = shift(piece(2 * big + half, big).astype(BF), first, N, 3)
-    ahead2 = shift((piece(big, half) + ahead[half:].astype(F32)).astype(BF), first, N, 1)
-    behind2 = shift((piece(3 * big + half, half) + behind[:half].astype(F32)).astype(BF), first, N, 3)
-
-    def low(start, stop):
+    return outs[0], outs[1:1 + len(CUTS)], outs[1 + len(CUTS):]
+
+
+class Sums:
+    def __init__(self, pieces, rows, part):
+        self.pieces, self.rows, self.part = pieces, rows, part
+        self.half, self.down = 2 * rows, rows - part
+
+    def first_a(self):
+        return self.pieces[0]().astype(BF), self.pieces[1]().astype(BF)
+
+    def first_b(self, ahead, behind):
+        self.ahead, self.behind = ahead.astype(F32), behind.astype(F32)
         return (
-            piece(start, stop - start)
-            + behind[half + start:half + stop].astype(F32)
-            + ahead2[start:stop].astype(F32)
+            (self.pieces[2]() + self.ahead[self.half:]).astype(BF),
+            (self.pieces[3]() + self.behind[:self.half]).astype(BF),
         )
 
-    def high(start, stop):
+    def second_a(self, ahead, behind):
+        half, rows, part = self.half, self.rows, self.part
+        own = self.pieces[4]()
+        self.low = own[:half] + self.behind[half:] + ahead.astype(F32)
+        self.high = own[half:] + self.ahead[:half] + behind.astype(F32)
         return (
-            piece(start, stop - start)
-            + ahead[start - half:stop - half].astype(F32)
-            + behind2[start - half:stop - half].astype(F32)
+            jnp.concatenate([self.low[rows + part:].astype(BF), self.high[:part].astype(BF)], axis=0),
+            self.high[part:rows + part].astype(BF),
         )
 
-    send_a = jnp.concatenate(
-        [low(rows + part, half).astype(BF), high(half, half + part).astype(BF)], axis=0
-    )
-    send_b = high(half + part, half + rows + part).astype(BF)
-    ahead3 = shift(send_a, second, N, 1)
-    behind3 = shift(send_b, second, N, 3)
-    ahead4 = shift((low(rows, rows + part) + ahead3[down:].astype(F32)).astype(BF), second, N, 1)
-    behind4 = shift(
-        (high(half + rows + part, big) + behind3[:down].astype(F32)).astype(BF), second, N, 3
-    )
-    top = low(0, part) + behind3[down:].astype(F32) + ahead4.astype(F32)
-    bottom = low(part, rows) + ahead3[:down].astype(F32) + behind4.astype(F32)
-    return jnp.concatenate([top, bottom], axis=0)
+    def second_b(self, ahead, behind):
+        rows, part, down = self.rows, self.part, self.down
+        self.ahead2, self.behind2 = ahead.astype(F32), behind.astype(F32)
+        return (
+            (self.low[rows:rows + part] + self.ahead2[down:]).astype(BF),
+            (self.high[rows + part:] + self.behind2[:down]).astype(BF),
+        )
+
+    def result(self, ahead, behind):
+        rows, part, down = self.rows, self.part, self.down
+        return jnp.concatenate(
+            [
+                self.low[:part] + self.behind2[down:] + ahead.astype(F32),
+                self.low[part:rows] + self.ahead2[:down] + behind.astype(F32),
+            ],
+            axis=0,
+        )
+
+
+def both_ways(pair, axis):
+    return shift(pair[0], axis, N, 1), shift(pair[1], axis, N, 3)
+
+
+def packed_both_ways(one, two, axis):
+    size = one[0].shape[0]
+    moved = both_ways([jnp.concatenate([a, b], axis=0) for a, b in zip(one, two)], axis)
+    return [m[:size] for m in moved], [m[size:] for m in moved]
 
 
 def local(
@@ -230,22 +287,11 @@
     statistic = all_sum(jnp.concatenate([squares, line_square], axis=0))
     inverse = lax.rsqrt(statistic[: rows // 128].reshape(rows) / D + epsilon)[:, None]
     line_normed = (line_vector * lax.rsqrt(statistic[rows // 128, 0] / D + epsilon)).astype(BF).astype(F32)
-    normed = (proj_values * inverse).astype(BF)
 
     step = jnp.arange(blocks, dtype=jnp.int32)
     outer, inner = step // N, step % N
     table1 = ((z + inner) % N) * N + (x + outer) % N
     table2 = ((z + outer) % N) * N + (x + inner) % N
-    features = jnp.concatenate(
-        [
-            siglip_features.T.reshape(blocks, sig_rows, rows),
-            convnext_features.T.reshape(blocks, conv_rows, rows),
-        ],
-        axis=1,
-    )
-    x_rows = sig_rows + conv_rows
-    features1 = block_order(features, table1).reshape(blocks * x_rows, rows)
-    features2 = block_order(features, table2).reshape(blocks * x_rows, rows)
     weight = block_order(key_value_weight.reshape(blocks, kv_rows, share), table1).reshape(
         blocks * kv_rows, share
     )
@@ -267,8 +313,14 @@
     line1 = line_blocks[table1].reshape(blocks * kv_rows)[:, None]
     line2 = line_blocks[table2].reshape(blocks * kv_rows)[:, None]
 
+    received, weight, projected = lax.optimization_barrier((received, weight, projected))
+    proj_values = projected.astype(F32)
+    normed = (proj_values * inverse).astype(BF)
     own = pick_tiles(received.reshape(blocks * CAP, TT, received.shape[2]), mine).reshape(
         rows, received.shape[2]
+    )
+    own, siglip_features, convnext_features = lax.optimization_barrier(
+        (own, siglip_features, convnext_features)
     )
     ring = [own] + [shift_y(own, s) for s in (1, 3, 2)]
     pieces = ring + [shift(piece, "core", 2, 1) for piece in ring]
@@ -278,57 +330,75 @@
         for s in (0, 1, 3, 2):
             other = (y - s) % N
             places.append(((other % 2) * 2 + (core + side) % 2) * 2 + other // 2)
-    grads1, grads2 = assemble(pieces, jnp.stack(places).astype(jnp.int32))
-
-    def kv_piece(grads, line, columns):
-        right = normed[:, columns]
-        across = line_normed[None, columns]
-
-        def piece(start, count):
-            return (
-                lax.dot_general(
-                    grads[:, start:start + count],
-                    right,
-                    (((0,), (0,)), ((), ())),
-                    preferred_element_type=F32,
-                )
-                + line[start:start + count] * across
-            )
-
-        return piece
-
-    left, right = slice(0, half), slice(half, share)
-    kv_result = jnp.concatenate(
+    features = jnp.concatenate(
         [
-            reduce_scatter(kv_piece(grads1, line1, left), "x", "z", kv_rows, kv_rows // 2),
-            reduce_scatter(kv_piece(grads2, line2, right), "z", "x", kv_rows, kv_rows // 2),
+            siglip_features.T.reshape(blocks, sig_rows, rows),
+            convnext_features.T.reshape(blocks, conv_rows, rows),
         ],
         axis=1,
     )
-
-    grad_values = jnp.dot(grads1, weight, preferred_element_type=F32).astype(BF).astype(F32)
-    products = all_sum(jnp.sum(grad_values * proj_values, axis=1).reshape(rows // 128, 128))
+    x_rows = sig_rows + conv_rows
+    features1, features2 = cut_orders(features, jnp.concatenate([table1, table2]))
+    grads, grads1, grads2 = assemble(pieces, jnp.stack(places).astype(jnp.int32))
+
+    left, right = slice(0, half), slice(half, share)
+
+    def kv_pieces(cuts, line, columns):
+        def piece(cut, start, stop):
+            lines = line[start * kv_rows:stop * kv_rows]
+            return lambda: (
+                lax.dot_general(
+                    cut, normed[:, columns], (((0,), (0,)), ((), ())), preferred_element_type=F32
+                )
+                + lines * line_normed[None, columns]
+            )
+
+        return [piece(cut, *where) for cut, where in zip(cuts, CUTS)]
+
+    kv0 = Sums(kv_pieces(grads1, line1, left), kv_rows, kv_rows // 2)
+    kv1 = Sums(kv_pieces(grads2, line2, right), kv_rows, kv_rows // 2)
+    out0, out1 = kv0.first_a(), kv1.first_a()
+    out0, out1, grads = lax.optimization_barrier((out0, out1, grads))
+    in0, in1 = both_ways(out0, "x"), both_ways(out1, "z")
+
+    grad_values = jnp.dot(grads, weight, preferred_element_type=F32).astype(BF).astype(F32)
+    products = jnp.sum(grad_values * proj_values, axis=1).reshape(rows // 128, 128)
+    members = 8
+    products = jnp.sum(
+        lax.all_to_all(
+            jnp.broadcast_to(products[None], (members,) + products.shape),
+            ("ylo", "core", "yhi"),
+            split_axis=0,
+            concat_axis=0,
+            tiled=True,
+        ),
+        axis=0,
+    )
     products = products.reshape(rows)[:, None]
     projected_grad = (
         inverse * grad_values - inverse**3 * proj_values * products / D
     ).astype(BF)
-
-    def x_piece(lhs, columns):
-        right = projected_grad[:, columns]
-
-        def piece(start, count):
-            return jnp.dot(lhs[start:start + count], right, preferred_element_type=F32)
-
-        return piece
+    out0, out1 = kv0.first_b(*in0), kv1.first_b(*in1)
+    in0, in1 = both_ways(out0, "x"), both_ways(out1, "z")
+    kv_out0, kv_out1 = kv0.second_a(*in0), kv1.second_a(*in1)
+
+    def x_pieces(cuts, columns):
+        return [
+            lambda cut=cut: jnp.dot(cut, projected_grad[:, columns], preferred_element_type=F32)
+            for cut in cuts
+        ]
 
     part = (x_rows // 2 + 7) // 8 * 8
-    x_result = jnp.concatenate(
-        [
-            reduce_scatter(x_piece(features1, left), "x", "z", x_rows, part),
-            reduce_scatter(x_piece(features2, right), "z", "x", x_rows, part),
-        ],
-        axis=1,
-    )
+    x0 = Sums(x_pieces(features1, left), x_rows, part)
+    x1 = Sums(x_pieces(features2, right), x_rows, part)
+    in0, in1 = both_ways(x0.first_a(), "x"), both_ways(x1.first_a(), "z")
+    in0, kv_in1 = packed_both_ways(x0.first_b(*in0), kv_out1, "x")
+    in1, kv_in0 = packed_both_ways(x1.first_b(*in1), kv_out0, "z")
+    in0, kv_in0 = packed_both_ways(x0.second_a(*in0), kv0.second_b(*kv_in0), "z")
+    in1, kv_in1 = packed_both_ways(x1.second_a(*in1), kv1.second_b(*kv_in1), "x")
+    kv_result = jnp.concatenate([kv0.result(*kv_in0), kv1.result(*kv_in1)], axis=1)
+    in0, in1 = both_ways(x0.second_b(*in0), "z"), both_ways(x1.second_b(*in1), "x")
+    x_result = jnp.concatenate([x0.result(*in0), x1.result(*in1)], axis=1)
     return x_result[:sig_rows], x_result[sig_rows:], kv_result
 
 

time: 518 us -> 161 us (0.31)
  Pallas kernels: 323 us -> 9.65 us
  waiting for transfers between devices: 63.2 us -> 40 us
  matrix products: 38.4 us -> 25.2 us
  starting transfers between devices: 62.8 us -> 51.1 us
  other arithmetic: 10 us -> 15.2 us
    pallas_call x3 -> x1, Pallas kernels: 300 us -> 1.06 us  [block_order(): pl.pallas_call(kernel, out_shape=jax.ShapeDtypeStruct((count,) + source.s...]
    ppermute x38 -> x29, waiting for transfers between devices: 53.8 us -> 33.8 us  [shift(): lax.ppermute(value, axis, [(i, (i + step) % size) for i in range(size)])]
    pallas_call x1, Pallas kernels: 17.3 us -> 2.22 us  [slices_out(): pl.pallas_call(kernel, out_shape=jax.ShapeDtypeStruct((blocks, rows, 2 *...]
    dot_general x45 -> x21, matrix products: 31.2 us -> 18.6 us  [the longest x10 10.7 us: piece(): lax.dot_general(cut, normed[:, columns], (((0,), (0,)), ((), ())), prefer...]
    ppermute x38 -> x29, starting transfers between devices: 39.1 us -> 30.3 us  [shift(): lax.ppermute(value, axis, [(i, (i + step) % size) for i in range(size)])]
    convert_element_type x0 -> x23, other arithmetic: none -> 7.92 us  [the longest x8 5.4 us: first_b(): self.ahead, self.behind = (ahead.astype(F32), behind.astype(F32))]
    slice x5 -> x13, local copies, waits for them, and re-layouts: 8.14 us -> 0.72 us  [the longest x1 0.6 us: piece(): line_normed[None, columns]]
    ppermute x9 -> x6, starting transfers between devices: 15.6 us -> 9.47 us  [shift_y(): lax.ppermute(value, Y, [(place(y), place((y + step) % N)) for y in range(...]
  transfers between devices with their start and end apart: 48 -> 37, of which waited for: 17 -> 20; matrix products, arithmetic and copies ran while one was open for 10% -> 25% of each run, Pallas kernels for 58% -> 1%
where the time goes in v2:
time: 161 us; the launch traced here: 160 us
  starting transfers between devices  51.1 us (32%)
  waiting for transfers between devices  40 us (25%)
  matrix products  25.2 us (16%)
  local copies, waits for them, and re-layouts  16.3 us (10%)
  other arithmetic  15.2 us (9%)
  Pallas kernels  9.65 us (6%)
  between operations  2.65 us (2%)
    ppermute x29, waiting for transfers between devices, shift(): lax.ppermute(value, axis, [(i, (i + step) % size) for i in range(size)])  33.8 us
    ppermute x29, starting transfers between devices, shift(): lax.ppermute(value, axis, [(i, (i + step) % size) for i in range(size)])  30.3 us
    dot_general x10, matrix products, piece(): lax.dot_general(cut, normed[:, columns], (((0,), (0,)), ((), ())), prefer...  10.7 us
    ppermute x6, starting transfers between devices, shift_y(): lax.ppermute(value, Y, [(place(y), place((y + step) % N)) for y in range(...  9.47 us
    all_to_all x1, starting transfers between devices, local(): lax.all_to_all(outgoing, DP, split_axis=0, concat_axis=0, tiled=True)  8.02 us
    ppermute x6, waiting for transfers between devices, shift_y(): lax.ppermute(value, Y, [(place(y), place((y + step) % N)) for y in range(...  6.13 us
    unnamed x99, local copies, waits for them, and re-layouts  6.04 us
    convert_element_type x8, other arithmetic, first_b(): self.ahead, self.behind = (ahead.astype(F32), behind.astype(F32))  5.4 us
  transfers between devices with their start and end apart: 37, of which 20 were waited for; matrix products, arithmetic and copies ran while one was open for 25% of the time, Pallas kernels for 1%

profile of v2, /device:TPU:0, one launch (start us, length us, event | category | flops | bytes accessed | tf_op | source)
XLA Modules:
  0.0 160.1 jit_solution(13822432685779811587)
XLA Ops:
  0.7 2.2 %slices_out.1 = bf16[16,64,256]{2,1,0:T(8,128)(2,1)} custom-call(s32[1]{0:T(128)} %bitcast.1.member_ref, bf16[1024,2048]{1,0:T(8,128)(2,1)} %source.1), custom_call_target="tpu_custom_call" | custom-call | tf_op jit(solution)/shard_map/slices_out/pallas_call | solution.py:57
  2.9 8.0 %all-to-all-start = ((bf16[16,64,256]{2,1,0:T(8,128)(2,1)}), bf16[16,64,256]{2,1,0:T(8,128)(2,1)}, u32[]{:S(2)}, u32[]{:S(2)}) async-start(bf16[16,64,256]{2,1,0:T(8,128)(2,1)} %slices_out.1), calls=%async_computation | async-start | bytes 1048576 | tf_op jit(solution)/shard_map/all_to_all | solution.py:277
  11.5 3.7 %fusion.123 = f32[512,1024]{1,0:T(8,128)S(1)} fusion(bf16[512,1152]{1,0:T(8,128)(2,1)} %param.10, bf16[1152,1024]{1,0:T(8,128)(2,1)} %param.12), kind=kOutput, calls=%fused_computation.253 | convolution fusion | flops 1207959552 | bytes 5636096 | tf_op jit(solution)/shard_map/dot_general | solution.py:280
  15.3 2.8 %multiply_reduce_fusion = (f32[512]{0:T(512)S(1)}, bf16[512,1024]{1,0:T(8,128)(2,1)}) fusion(f32[512,1024]{1,0:T(8,128)S(1)} %fusion.123, bf16[512,1536]{1,0:T(8,128)(2,1)S(1)} %copy-done.26, bf16[1536,1024]{1,0:T(8,128)(2,1)S(1)} %copy-done), kind=kOutput, calls=%fused_computation.13 | convolution fusion | flops 1613233664 | bytes 7866368 | tf_op jit(solution)/shard_map/dot_general | solution.py:281
  27.7 2.9 %collective-permute-start.2 = (f32[8,128]{1,0:T(8,128)S(1)}, f32[8,128]{1,0:T(8,128)S(1)}, u32[]{:S(2)}, u32[]{:S(2)}) collective-permute-start(f32[8,128]{1,0:T(8,128)S(1)} %pad_add_fusion), channel_id=1, source_target_pairs={{0,1},{64,65},{1,0},{65,64},{2,3},{66,67},{3,2},{67,66},{4,5},{68,... | collective-permute-start | bytes 12296 | tf_op jit(solution)/shard_map/ppermute | solution.py:25
  31.9 2.2 %copy-done.2 = bf16[2048,1024]{1,0:T(8,128)(2,1)S(1)} copy-done((bf16[2048,1024]{1,0:T(8,128)(2,1)S(1)}, bf16[2048,1024]{1,0:T(8,128)(2,1)}, u32[]{:S(2)}) %copy-start.2) | copy-done | bytes 4194328
  39.2 2.5 %pick_tiles.1 = bf16[16,32,256]{2,1,0:T(8,128)(2,1)} custom-call(s32[16]{0:T(128)} %dynamic-slice_bitcast_fusion.dest_ref, bf16[32,32,256]{2,1,0:T(8,128)(2,1)} %bitcast.4.source), custom_call_target="tpu_custom_call" | custom-call | tf_op jit(solution)/shard_map/pick_tiles/pallas_call | solution.py:140
  42.5 2.7 %collective-permute-start.5 = (bf16[512,256]{1,0:T(8,128)(2,1)}, bf16[512,256]{1,0:T(8,128)(2,1)S(1)}, u32[]{:S(2)}, u32[]{:S(2)}) collective-permute-start(bf16[512,256]{1,0:T(8,128)(2,1)} %bitcast.95), channel_id=1, source_target_pairs={{0,65},{64,0},{1,64},{65,1},{2,67},{66,2},{3,66},{67,3},{4,69},{68... | collective-permute-start | bytes 786440 | tf_op jit(solution)/shard_map/ppermute | solution.py:25
  50.6 2.0 %collective-permute-done.6.refs_3_ = bf16[512,256]{1,0:T(8,128)(2,1)S(1)} collective-permute-done((bf16[512,256]{1,0:T(8,128)(2,1)}, bf16[512,256]{1,0:T(8,128)(2,1)S(1)}, u32[]{:S(2)}, u32[]{:S(2)}) %collective-permute-start.6) | collective-permute-done | bytes 262176 | tf_op jit(solution)/shard_map/ppermute | solution.py:25
  52.6 4.1 %collective-permute-done.4.refs_1_ = bf16[512,256]{1,0:T(8,128)(2,1)S(1)} collective-permute-done((bf16[512,256]{1,0:T(8,128)(2,1)}, bf16[512,256]{1,0:T(8,128)(2,1)S(1)}, u32[]{:S(2)}, u32[]{:S(2)}) %collective-permute-start.4) | collective-permute-done | bytes 262176 | tf_op jit(solution)/shard_map/ppermute | solution.py:25
  58.7 2.9 %assemble.1 = (bf16[512,2048]{1,0:T(8,128)(2,1)S(1)}, bf16[512,512]{1,0:T(8,128)(2,1)S(1)}, bf16[512,512]{1,0:T(8,128)(2,1)S(1)}, bf16[512,256]{1,0:T(8,128)(2,1...) custom-call(s32[8]{0:T(128)S(1)} %stack.35.place_ref, ...), custom_call_target="tpu_custom_call" | custom-call | tf_op jit(solution)/shard_map/assemble/pallas_call | solution.py:178
  67.0 3.4 %fusion.5 = (f32[512]{0:T(512)S(1)}, bf16[512,1024]{1,0:T(8,128)(2,1)}) fusion(bf16[512,1024]{1,0:T(8,128)(2,1)S(1)} %copy-done.25, bf16[512,2048]{1,0:T(8,128)(2,1)S(1)} %get-tuple-element.46, bf16[2048,1024]{1,0:T(8,128)(2,1)S(1)} %bitcast.92), kind=kOutput, calls=%fused_computation.12 | convolution fusion | flops 2150104576 | bytes 8390656 | tf_op jit(solution)/shard_map/dot_general | solution.py:364
  71.0 3.3 %all-to-all-start.1 = ((f32[8,4,128]{2,1,0:T(4,128)}), f32[8,4,128]{2,1,0:T(4,128)S(1)}, u32[]{:S(2)}, u32[]{:S(2)}) async-start(f32[8,4,128]{2,1,0:T(4,128)} %broadcast_in_dim.5), calls=%async_computation.1 | async-start | bytes 32768 | tf_op jit(solution)/shard_map/all_to_all | solution.py:368
  80.9 2.7 %convolution_add_fusion.1 = f32[512,512]{1,0:T(8,128)} fusion(bf16[512,512]{1,0:T(8,128)(2,1)} %copy-done.16, f32[512]{0:T(512)S(1)} %copy-done.35, f32[512]{0:T(512)S(1)} %copy-done.43, bf16[512,1024]{1,0:T(8,128)(2,1)} %copy-done.27), kind=kOutput, calls=%fused_computation.17 | convolution fusion | flops 268959744 | bytes 2101248 | tf_op jit(solution)/shard_map/dot_general | solution.py:350
  85.0 2.2 %fusion.1 = bf16[512,1024]{1,0:T(8,128)(2,1)S(1)} fusion(bf16[512,1024]{1,0:T(8,128)(2,1)} %get-tuple-element.98, bf16[512,1024]{1,0:T(8,128)(2,1)} %get-tuple-element.41, f32[512]{0:T(512)S(1)} %bitcast.106, f32[512]{0:T(512)S(1)} %multiply_multiply_fusion, f32[512]{0:T(512)S(1)} %rsqrt_bitcast_fusion), kind=kLoop, calls=%fused_computation.8 | loop fusion | flops 4194304 | bytes 3151872 | tf_op jit(solution)/shard_map/convert_element_type | solution.py:380
  101.7 6.1 %collective-permute-done.11 = bf16[672,512]{1,0:T(8,128)(2,1)S(1)} collective-permute-done((bf16[672,512]{1,0:T(8,128)(2,1)S(1)}, bf16[672,512]{1,0:T(8,128)(2,1)S(1)}, u32[]{:S(2)}, u32[]{:S(2)}) %collective-permute-start.11) | collective-permute-done | bytes 688160 | tf_op jit(solution)/shard_map/ppermute | solution.py:20
  121.8 2.7 %collective-permute-start.18 = (bf16[464,512]{1,0:T(8,128)(2,1)S(1)}, bf16[464,512]{1,0:T(8,128)(2,1)S(1)}, u32[]{:S(2)}, u32[]{:S(2)}) collective-permute-start(bf16[464,512]{1,0:T(8,128)(2,1)S(1)} %pad_maximum_fusion.2), channel_id=1, source_target_pairs={{0,6},{2,0},{4,2},{6,4},{1,7},{3,1},{5,3},{7,5},{8,14},{10,8},{12,... | collective-permute-start | bytes 1425416 | tf_op jit(solution)/shard_map/ppermute | solution.py:20
  125.1 4.7 %collective-permute-done.23 = bf16[464,512]{1,0:T(8,128)(2,1)S(1)} collective-permute-done((bf16[464,512]{1,0:T(8,128)(2,1)S(1)}, bf16[464,512]{1,0:T(8,128)(2,1)S(1)}, u32[]{:S(2)}, u32[]{:S(2)}) %collective-permute-start.23) | collective-permute-done | bytes 475168 | tf_op jit(solution)/shard_map/ppermute | solution.py:20
  131.8 3.4 %collective-permute-done.17 = bf16[464,512]{1,0:T(8,128)(2,1)S(1)} collective-permute-done((bf16[464,512]{1,0:T(8,128)(2,1)S(1)}, bf16[464,512]{1,0:T(8,128)(2,1)S(1)}, u32[]{:S(2)}, u32[]{:S(2)}) %collective-permute-start.17) | collective-permute-done | bytes 475168 | tf_op jit(solution)/shard_map/ppermute | solution.py:20
  135.7 2.3 %collective-permute-start.24 = (bf16[232,512]{1,0:T(8,128)(2,1)S(1)}, bf16[232,512]{1,0:T(8,128)(2,1)S(1)}, u32[]{:S(2)}, u32[]{:S(2)}) collective-permute-start(bf16[232,512]{1,0:T(8,128)(2,1)S(1)} %pad_maximum_fusion.7), channel_id=1, source_target_pairs={{0,24},{8,0},{16,8},{24,16},{1,25},{9,1},{17,9},{25,17},{2,26},{10... | collective-permute-start | bytes 712712 | tf_op jit(solution)/shard_map/ppermute | solution.py:20
  138.6 4.2 %collective-permute-done.24 = bf16[232,512]{1,0:T(8,128)(2,1)S(1)} collective-permute-done((bf16[232,512]{1,0:T(8,128)(2,1)S(1)}, bf16[232,512]{1,0:T(8,128)(2,1)S(1)}, u32[]{:S(2)}, u32[]{:S(2)}) %collective-permute-start.24) | collective-permute-done | bytes 237600 | tf_op jit(solution)/shard_map/ppermute | solution.py:20
  146.8 3.3 %collective-permute-start.34 = (bf16[80,512]{1,0:T(8,128)(2,1)S(1)}, bf16[80,512]{1,0:T(8,128)(2,1)S(1)}, u32[]{:S(2)}, u32[]{:S(2)}) collective-permute-start(bf16[80,512]{1,0:T(8,128)(2,1)S(1)} %fusion.70), channel_id=1, source_target_pairs={{0,6},{2,0},{4,2},{6,4},{1,7},{3,1},{5,3},{7,5},{8,14},{10,8},{12,... | collective-permute-start | bytes 245768 | tf_op jit(solution)/shard_map/ppermute | solution.py:20
  153.8 2.6 %collective-permute-done.29 = bf16[88,512]{1,0:T(8,128)(2,1)S(1)} collective-permute-done((bf16[88,512]{1,0:T(8,128)(2,1)S(1)}, bf16[88,512]{1,0:T(8,128)(2,1)S(1)}, u32[]{:S(2)}, u32[]{:S(2)}) %collective-permute-start.29) | collective-permute-done | bytes 90144 | tf_op jit(solution)/shard_map/ppermute | solution.py:20
  156.4 2.1 %collective-permute-done.33 = bf16[88,512]{1,0:T(8,128)(2,1)S(1)} collective-permute-done((bf16[88,512]{1,0:T(8,128)(2,1)S(1)}, bf16[88,512]{1,0:T(8,128)(2,1)S(1)}, u32[]{:S(2)}, u32[]{:S(2)}) %collective-permute-start.33) | collective-permute-done | bytes 90144 | tf_op jit(solution)/shard_map/ppermute | solution.py:20
  (274 shorter events, 78.3 us)
Async XLA Ops:
  2.9 36.3 %all-to-all-start = ((bf16[16,64,256]{2,1,0:T(8,128)(2,1)}), bf16[16,64,256]{2,1,0:T(8,128)(2,1)}, u32[]{:S(2)}, u32[]{:S(2)}) async-start(bf16[16,64,256]{2,1,0:T(8,128)(2,1)} %slices_out.1), calls=%async_computation | async-start | bytes 1048576 | tf_op jit(solution)/shard_map/all_to_all | solution.py:277
  26.0 11.2 %collective-permute-start.1 = (f32[8,128]{1,0:T(8,128)S(1)}, f32[8,128]{1,0:T(8,128)S(1)}, u32[]{:S(2)}, u32[]{:S(2)}) collective-permute-start(f32[8,128]{1,0:T(8,128)S(1)} %pad_add_fusion), channel_id=1, source_target_pairs={{0,64},{64,1},{1,65},{65,0},{2,66},{66,3},{3,67},{67,2},{4,68},{68... | collective-permute-start | bytes 12296 | tf_op jit(solution)/shard_map/ppermute | solution.py:25
  27.7 9.6 %collective-permute-start.2 = (f32[8,128]{1,0:T(8,128)S(1)}, f32[8,128]{1,0:T(8,128)S(1)}, u32[]{:S(2)}, u32[]{:S(2)}) collective-permute-start(f32[8,128]{1,0:T(8,128)S(1)} %pad_add_fusion), channel_id=1, source_target_pairs={{0,1},{64,65},{1,0},{65,64},{2,3},{66,67},{3,2},{67,66},{4,5},{68,... | collective-permute-start | bytes 12296 | tf_op jit(solution)/shard_map/ppermute | solution.py:25
  41.7 10.9 %collective-permute-start.6 = (bf16[512,256]{1,0:T(8,128)(2,1)}, bf16[512,256]{1,0:T(8,128)(2,1)S(1)}, u32[]{:S(2)}, u32[]{:S(2)}) collective-permute-start(bf16[512,256]{1,0:T(8,128)(2,1)} %bitcast.93), channel_id=1, source_target_pairs={{0,1},{64,65},{1,0},{65,64},{2,3},{66,67},{3,2},{67,66},{4,5},{68,... | collective-permute-start | bytes 786440 | tf_op jit(solution)/shard_map/ppermute | solution.py:25
  42.0 14.7 %collective-permute-start.4 = (bf16[512,256]{1,0:T(8,128)(2,1)}, bf16[512,256]{1,0:T(8,128)(2,1)S(1)}, u32[]{:S(2)}, u32[]{:S(2)}) collective-permute-start(bf16[512,256]{1,0:T(8,128)(2,1)} %bitcast.94), channel_id=1, source_target_pairs={{0,64},{64,1},{1,65},{65,0},{2,66},{66,3},{3,67},{67,2},{4,68},{68... | collective-permute-start | bytes 786440 | tf_op jit(solution)/shard_map/ppermute | solution.py:25
  42.5 14.2 %collective-permute-start.5 = (bf16[512,256]{1,0:T(8,128)(2,1)}, bf16[512,256]{1,0:T(8,128)(2,1)S(1)}, u32[]{:S(2)}, u32[]{:S(2)}) collective-permute-start(bf16[512,256]{1,0:T(8,128)(2,1)} %bitcast.95), channel_id=1, source_target_pairs={{0,65},{64,0},{1,64},{65,1},{2,67},{66,2},{3,66},{67,3},{4,69},{68... | collective-permute-start | bytes 786440 | tf_op jit(solution)/shard_map/ppermute | solution.py:25
  45.3 12.3 %collective-permute-start.7 = (bf16[512,256]{1,0:T(8,128)(2,1)}, bf16[512,256]{1,0:T(8,128)(2,1)}, u32[]{:S(2)}, u32[]{:S(2)}) collective-permute-start(bf16[512,256]{1,0:T(8,128)(2,1)} %bitcast.96), channel_id=1, source_target_pairs={{0,32},{32,0},{1,33},{33,1},{2,34},{34,2},{3,35},{35,3},{4,36},{36... | collective-permute-start | bytes 786440 | tf_op jit(solution)/shard_map/ppermute | solution.py:20
  71.0 14.0 %all-to-all-start.1 = ((f32[8,4,128]{2,1,0:T(4,128)}), f32[8,4,128]{2,1,0:T(4,128)S(1)}, u32[]{:S(2)}, u32[]{:S(2)}) async-start(f32[8,4,128]{2,1,0:T(4,128)} %broadcast_in_dim.5), calls=%async_computation.1 | async-start | bytes 32768 | tf_op jit(solution)/shard_map/all_to_all | solution.py:368
  74.3 17.6 %collective-permute-start.14 = (bf16[512,512]{1,0:T(8,128)(2,1)}, bf16[512,512]{1,0:T(8,128)(2,1)}, u32[]{:S(2)}, u32[]{:S(2)}) collective-permute-start(bf16[512,512]{1,0:T(8,128)(2,1)} %fusion.8), channel_id=1, source_target_pairs={{0,8},{8,16},{16,24},{24,0},{1,9},{9,17},{17,25},{25,1},{2,10},{10... | collective-permute-start | bytes 1572872 | tf_op jit(solution)/shard_map/ppermute | solution.py:20
  76.3 17.2 %collective-permute-start.13 = (bf16[512,512]{1,0:T(8,128)(2,1)}, bf16[512,512]{1,0:T(8,128)(2,1)}, u32[]{:S(2)}, u32[]{:S(2)}) collective-permute-start(bf16[512,512]{1,0:T(8,128)(2,1)} %fusion.9), channel_id=1, source_target_pairs={{0,24},{8,0},{16,8},{24,16},{1,25},{9,1},{17,9},{25,17},{2,26},{10... | collective-permute-start | bytes 1572872 | tf_op jit(solution)/shard_map/ppermute | solution.py:20
  77.6 18.8 %collective-permute-start.19 = (bf16[512,512]{1,0:T(8,128)(2,1)}, bf16[512,512]{1,0:T(8,128)(2,1)}, u32[]{:S(2)}, u32[]{:S(2)}) collective-permute-start(bf16[512,512]{1,0:T(8,128)(2,1)} %fusion.6), channel_id=1, source_target_pairs={{0,2},{2,4},{4,6},{6,0},{1,3},{3,5},{5,7},{7,1},{8,10},{10,12},{12... | collective-permute-start | bytes 1572872 | tf_op jit(solution)/shard_map/ppermute | solution.py:20
  79.5 18.9 %collective-permute-start.20 = (bf16[512,512]{1,0:T(8,128)(2,1)}, bf16[512,512]{1,0:T(8,128)(2,1)}, u32[]{:S(2)}, u32[]{:S(2)}) collective-permute-start(bf16[512,512]{1,0:T(8,128)(2,1)} %fusion.7), channel_id=1, source_target_pairs={{0,6},{2,0},{4,2},{6,4},{1,7},{3,1},{5,3},{7,5},{8,14},{10,8},{12,... | collective-permute-start | bytes 1572872 | tf_op jit(solution)/shard_map/ppermute | solution.py:20
  88.3 19.5 %collective-permute-start.11 = (bf16[672,512]{1,0:T(8,128)(2,1)S(1)}, bf16[672,512]{1,0:T(8,128)(2,1)S(1)}, u32[]{:S(2)}, u32[]{:S(2)}) collective-permute-start(bf16[672,512]{1,0:T(8,128)(2,1)S(1)} %convolution_convert_fusion.4), channel_id=1, source_target_pairs={{0,6},{2,0},{4,2},{6,4},{1,7},{3,1},{5,3},{7,5},{8,14},{10,8},{12,... | collective-permute-start | bytes 2064392 | tf_op jit(solution)/shard_map/ppermute | solution.py:20
  91.9 17.6 %collective-permute-start.12 = (bf16[672,512]{1,0:T(8,128)(2,1)S(1)}, bf16[672,512]{1,0:T(8,128)(2,1)S(1)}, u32[]{:S(2)}, u32[]{:S(2)}) collective-permute-start(bf16[672,512]{1,0:T(8,128)(2,1)S(1)} %convolution_convert_fusion.3), channel_id=1, source_target_pairs={{0,2},{2,4},{4,6},{6,0},{1,3},{3,5},{5,7},{7,1},{8,10},{10,12},{12... | collective-permute-start | bytes 2064392 | tf_op jit(solution)/shard_map/ppermute | solution.py:20
  93.5 17.7 %collective-permute-start.22 = (bf16[672,512]{1,0:T(8,128)(2,1)S(1)}, bf16[672,512]{1,0:T(8,128)(2,1)S(1)}, u32[]{:S(2)}, u32[]{:S(2)}) collective-permute-start(bf16[672,512]{1,0:T(8,128)(2,1)S(1)} %convolution_convert_fusion.2), channel_id=1, source_target_pairs={{0,24},{8,0},{16,8},{24,16},{1,25},{9,1},{17,9},{25,17},{2,26},{10... | collective-permute-start | bytes 2064392 | tf_op jit(solution)/shard_map/ppermute | solution.py:20
  96.5 19.7 %collective-permute-start.26 = (bf16[672,512]{1,0:T(8,128)(2,1)S(1)}, bf16[672,512]{1,0:T(8,128)(2,1)S(1)}, u32[]{:S(2)}, u32[]{:S(2)}) collective-permute-start(bf16[672,512]{1,0:T(8,128)(2,1)S(1)} %convolution_convert_fusion.1), channel_id=1, source_target_pairs={{0,8},{8,16},{16,24},{24,0},{1,9},{9,17},{17,25},{25,1},{2,10},{10... | collective-permute-start | bytes 2064392 | tf_op jit(solution)/shard_map/ppermute | solution.py:20
  98.4 20.7 %collective-permute-start.15 = (bf16[256,512]{1,0:T(8,128)(2,1)S(1)}, bf16[256,512]{1,0:T(8,128)(2,1)S(1)}, u32[]{:S(2)}, u32[]{:S(2)}) collective-permute-start(bf16[256,512]{1,0:T(8,128)(2,1)S(1)} %fusion.14), channel_id=1, source_target_pairs={{0,8},{8,16},{16,24},{24,0},{1,9},{9,17},{17,25},{25,1},{2,10},{10... | collective-permute-start | bytes 786440 | tf_op jit(solution)/shard_map/ppermute | solution.py:20
  107.8 11.3 %collective-permute-start.16 = (bf16[256,512]{1,0:T(8,128)(2,1)S(1)}, bf16[256,512]{1,0:T(8,128)(2,1)S(1)}, u32[]{:S(2)}, u32[]{:S(2)}) collective-permute-start(bf16[256,512]{1,0:T(8,128)(2,1)S(1)} %fusion.15), channel_id=1, source_target_pairs={{0,24},{8,0},{16,8},{24,16},{1,25},{9,1},{17,9},{25,17},{2,26},{10... | collective-permute-start | bytes 786440 | tf_op jit(solution)/shard_map/ppermute | solution.py:20
  109.5 7.8 %collective-permute-start.25 = (bf16[256,512]{1,0:T(8,128)(2,1)S(1)}, bf16[256,512]{1,0:T(8,128)(2,1)S(1)}, u32[]{:S(2)}, u32[]{:S(2)}) collective-permute-start(bf16[256,512]{1,0:T(8,128)(2,1)S(1)} %fusion.17), channel_id=1, source_target_pairs={{0,2},{2,4},{4,6},{6,0},{1,3},{3,5},{5,7},{7,1},{8,10},{10,12},{12... | collective-permute-start | bytes 786440 | tf_op jit(solution)/shard_map/ppermute | solution.py:20
  119.5 10.3 %collective-permute-start.23 = (bf16[464,512]{1,0:T(8,128)(2,1)S(1)}, bf16[464,512]{1,0:T(8,128)(2,1)S(1)}, u32[]{:S(2)}, u32[]{:S(2)}) collective-permute-start(bf16[464,512]{1,0:T(8,128)(2,1)S(1)} %pad_maximum_fusion.3), channel_id=1, source_target_pairs={{0,24},{8,0},{16,8},{24,16},{1,25},{9,1},{17,9},{25,17},{2,26},{10... | collective-permute-start | bytes 1425416 | tf_op jit(solution)/shard_map/ppermute | solution.py:20
  120.5 10.6 %collective-permute-start.27 = (bf16[464,512]{1,0:T(8,128)(2,1)S(1)}, bf16[464,512]{1,0:T(8,128)(2,1)S(1)}, u32[]{:S(2)}, u32[]{:S(2)}) collective-permute-start(bf16[464,512]{1,0:T(8,128)(2,1)S(1)} %pad_maximum_fusion.4), channel_id=1, source_target_pairs={{0,8},{8,16},{16,24},{24,0},{1,9},{9,17},{17,25},{25,1},{2,10},{10... | collective-permute-start | bytes 1425416 | tf_op jit(solution)/shard_map/ppermute | solution.py:20
  121.8 10.0 %collective-permute-start.18 = (bf16[464,512]{1,0:T(8,128)(2,1)S(1)}, bf16[464,512]{1,0:T(8,128)(2,1)S(1)}, u32[]{:S(2)}, u32[]{:S(2)}) collective-permute-start(bf16[464,512]{1,0:T(8,128)(2,1)S(1)} %pad_maximum_fusion.2), channel_id=1, source_target_pairs={{0,6},{2,0},{4,2},{6,4},{1,7},{3,1},{5,3},{7,5},{8,14},{10,8},{12,... | collective-permute-start | bytes 1425416 | tf_op jit(solution)/shard_map/ppermute | solution.py:20
  124.5 10.7 %collective-permute-start.17 = (bf16[464,512]{1,0:T(8,128)(2,1)S(1)}, bf16[464,512]{1,0:T(8,128)(2,1)S(1)}, u32[]{:S(2)}, u32[]{:S(2)}) collective-permute-start(bf16[464,512]{1,0:T(8,128)(2,1)S(1)} %pad_maximum_fusion.1), channel_id=1, source_target_pairs={{0,2},{2,4},{4,6},{6,0},{1,3},{3,5},{5,7},{7,1},{8,10},{10,12},{12... | collective-permute-start | bytes 1425416 | tf_op jit(solution)/shard_map/ppermute | solution.py:20
  142.8 7.6 %collective-permute-start.28 = (bf16[232,512]{1,0:T(8,128)(2,1)S(1)}, bf16[232,512]{1,0:T(8,128)(2,1)S(1)}, u32[]{:S(2)}, u32[]{:S(2)}) collective-permute-start(bf16[232,512]{1,0:T(8,128)(2,1)S(1)} %pad_maximum_fusion.8), channel_id=1, source_target_pairs={{0,8},{8,16},{16,24},{24,0},{1,9},{9,17},{17,25},{25,1},{2,10},{10... | collective-permute-start | bytes 712712 | tf_op jit(solution)/shard_map/ppermute | solution.py:20
  (62 other events, 353.2 us)

commit v3 on v2

v3 whole, which is shorter than its diff:
```python
import jax
import jax.numpy as jnp
from jax import lax
from jax.experimental import pallas as pl
from jax.experimental.pallas import tpu as pltpu
from jax.sharding import Mesh, PartitionSpec as P

D = 8192
epsilon = 1e-06
N = 4
TT = 32
CAP = 2
BF = jnp.bfloat16
F32 = jnp.float32
DP = ("z", "x")
Y = ("ylo", "yhi")


def shift(value, axis, size, step):
    return lax.ppermute(value, axis, [(i, (i + step) % size) for i in range(size)])


def shift_y(value, step):
    place = lambda y: (y % 2) * 2 + y // 2
    return lax.ppermute(value, Y, [(place(y), place((y + step) % N)) for y in range(N)])


EXTRA = 16
ANY = pl.ANY
HBM = pltpu.HBM
VMEM = pltpu.VMEM


def thirds(value):
    high = lax.reduce_precision(value, 8, 7)
    rest = value - high
    middle = lax.reduce_precision(rest, 8, 7)
    return high, middle, rest - middle


def extra_rows(rows):
    rows = jnp.concatenate(rows, axis=0)
    return jnp.pad(rows, ((0, EXTRA - rows.shape[0]), (0, 0))).astype(BF)


def order_blocks():
    z, x = lax.axis_index("z"), lax.axis_index("x")
    places = [(place // N, place % N) for place in range(N * N)]
    first = [((z + b) & 3) * N + ((x + a) & 3) for a, b in places]
    second = [((z + a) & 3) * N + ((x + b) & 3) for a, b in places]
    return first, second


def slices_out(key_value_grad, newline_grad):
    blocks = N * N
    rows = key_value_grad.shape[0] // blocks
    width = key_value_grad.shape[1] // blocks
    fold = newline_grad.shape[0] // 2

    def kernel(source, lines, out, sems):
        me = (lax.axis_index("ylo") * 2 + lax.axis_index("core")) * 2 + lax.axis_index("yhi")
        copies = []

        def move(origin, target):
            copy = pltpu.make_async_copy(origin, target, sems.at[len(copies)])
            copy.start()
            copies.append(copy)

        for dest in range(blocks):
            for part in range(2):
                place = 2 * me + part
                dx, dz = place >> 2, place & 3
                column = ((dest // N + dz) & 3) * N + ((dest % N + dx) & 3)
                move(
                    source.at[pl.ds(dest * rows, rows), pl.ds(pl.multiple_of(column * width, width), width)],
                    out.at[dest, pl.ds(0, rows), pl.ds(part * width, width)],
                )
                move(
                    lines.at[pl.ds(part * fold, fold), pl.ds(dest * width, width)],
                    out.at[dest, pl.ds(rows, fold), pl.ds(part * width, width)],
                )
        for copy in copies:
            copy.wait()

    return pl.pallas_call(
        kernel,
        out_shape=jax.ShapeDtypeStruct((blocks, rows + fold, 2 * width), key_value_grad.dtype),
        grid_spec=pltpu.PrefetchScalarGridSpec(
            num_scalar_prefetch=0,
            grid=(1,),
            in_specs=[pl.BlockSpec(memory_space=pl.ANY)] * 2,
            out_specs=pl.BlockSpec(memory_space=pltpu.VMEM),
            scratch_shapes=[pltpu.SemaphoreType.DMA((4 * blocks,))],
        ),
        name="slices_out",
    )(key_value_grad, newline_grad)


CUTS = ((6, 10), (10, 14), (4, 6), (14, 16), (0, 4))


def turn_features(siglip_features, convnext_features):
    rows = siglip_features.shape[0]
    blocks = N * N
    sizes = [siglip_features.shape[1] // blocks, convnext_features.shape[1] // blocks]
    size = sum(sizes)

    def kernel(siglip_ref, convnext_ref, *refs):
        count = 2 * len(CUTS)
        outs, staged, scratch, sems = refs[:count], refs[count:2 * count], refs[2 * count:-1], refs[-1]
        for source, target in zip((siglip_ref, convnext_ref), scratch):
            for i in range(source.shape[1] // 128):
                at = slice(i * 128, (i + 1) * 128)
                target[at] = source[:, at].T.astype(F32)
        first, _ = order_blocks()

        def store(order, place, value):
            for piece, (start, stop) in enumerate(CUTS):
                if start <= place < stop:
                    at = (place - start) * size
                    staged[order * len(CUTS) + piece][at:at + size] = value

        for place in range(blocks):
            value = jnp.concatenate(
                [
                    source[pl.ds(pl.multiple_of(first[place] * n, 8), n)]
                    for source, n in zip(scratch, sizes)
                ],
                axis=0,
            ).astype(BF)
            store(0, place, value)
            store(1, (place % N) * N + place // N, value)
        copies = [pltpu.make_async_copy(staged[i], outs[i], sems.at[i]) for i in range(count)]
        for copy in copies:
            copy.start()
        for copy in copies:
            copy.wait()

    shapes = [
        jax.ShapeDtypeStruct(((stop - start) * size, rows), siglip_features.dtype) for start, stop in CUTS
    ] * 2
    outs = pl.pallas_call(
        kernel,
        out_shape=[pltpu.HBM(shape.shape, shape.dtype) for shape in shapes],
        grid_spec=pltpu.PrefetchScalarGridSpec(
            num_scalar_prefetch=0,
            grid=(1,),
            in_specs=[
                pl.BlockSpec(siglip_features.shape, lambda i: (0, 0)),
                pl.BlockSpec(convnext_features.shape, lambda i: (0, 0)),
            ],
            out_specs=[pl.BlockSpec(memory_space=pltpu.HBM)] * len(shapes),
            scratch_shapes=[pltpu.VMEM(shape.shape, shape.dtype) for shape in shapes]
            + [
                pltpu.VMEM((siglip_features.shape[1], rows), F32),
                pltpu.VMEM((convnext_features.shape[1], rows), F32),
                pltpu.SemaphoreType.DMA((len(shapes),)),
            ],
        ),
        compiler_params=pltpu.CompilerParams(vmem_limit_bytes=32 * 1024 * 1024),
        name="turn_features",
    )(siglip_features, convnext_features)
    return outs[:len(CUTS)], outs[len(CUTS):]


def pick_tiles(received, dests, extra):
    tiles = dests.shape[0]
    width = received.shape[2]
    rows = tiles * TT

    def kernel(dest_ref, source, extra_ref, out, sems):
        names = [dest_ref[j] for j in range(tiles)]
        copies = []
        for j in range(tiles):
            before = jnp.int32(0)
            for i in range(j):
                before = before + (names[i] == names[j]).astype(jnp.int32)
            copy = pltpu.make_async_copy(
                source.at[names[j], pl.ds(pl.multiple_of(before * TT, TT), TT)],
                out.at[pl.ds(j * TT, TT)],
                sems.at[j],
            )
            copy.start()
            copies.append(copy)
        out[rows:] = extra_ref[...]
        for copy in copies:
            copy.wait()

    return pl.pallas_call(
        kernel,
        out_shape=jax.ShapeDtypeStruct((rows + EXTRA, width), received.dtype),
        grid_spec=pltpu.PrefetchScalarGridSpec(
            num_scalar_prefetch=1,
            grid=(1,),
            in_specs=[
                pl.BlockSpec(memory_space=pltpu.HBM),
                pl.BlockSpec((EXTRA, width), lambda i, t: (0, 0)),
            ],
            out_specs=pl.BlockSpec((rows + EXTRA, width), lambda i, t: (0, 0)),
            scratch_shapes=[pltpu.SemaphoreType.DMA((tiles,))],
        ),
        name="pick_tiles",
    )(dests, received, extra)


def step(kernel, name, ins, outs, scratch, copies, limit=24):
    return pl.pallas_call(
        kernel,
        out_shape=[space(shape.shape, shape.dtype) for shape, space in outs],
        grid_spec=pltpu.PrefetchScalarGridSpec(
            num_scalar_prefetch=0,
            grid=(1,),
            in_specs=[pl.BlockSpec(memory_space=space) for _, space in ins],
            out_specs=[pl.BlockSpec(memory_space=space) for _, space in outs],
            scratch_shapes=list(scratch) + [pltpu.SemaphoreType.DMA((copies,))],
        ),
        compiler_params=pltpu.CompilerParams(vmem_limit_bytes=limit * 1024 * 1024),
        name=name,
    )(
        *[array if space is ANY else pltpu.with_memory_space_constraint(array, space) for array, space in ins],
    )


class Copies:
    def __init__(self, sems):
        self.sems, self.count = sems, 0

    def start(self, source, target):
        copy = pltpu.make_async_copy(source, target, self.sems.at[self.count])
        self.count += 1
        copy.start()
        return copy


def down(row):
    return jnp.broadcast_to(row, (128, row.shape[1])).T


CHUNK = 256


def tile_step(pieces, projected, key_value_weight, newline_embed):
    wide = pieces[0].shape[1]
    rows = pieces[0].shape[0] - EXTRA
    width = wide // 2
    count = len(pieces)
    blocks = 2 * count
    share = projected.shape[1]
    deep = rows // wide
    half = share // 2
    dtype = pieces[0].dtype

    def kernel(*refs):
        piece_refs = refs[:count]
        proj_hbm, weight_hbm, embed_ref = refs[count:count + 3]
        first_hbm, second_hbm, grad_hbm, normed_hbm = refs[count + 3:count + 7]
        sends, (products_ref, inverse_ref, line_ref) = refs[count + 7:count + 11], refs[count + 11:count + 14]
        sources, proj_ref, weight_ref, first, second, grad_ref, normed_ref, staged, whole, sems = refs[
            count + 14:
        ]
        copies = Copies(sems)
        arriving = [copies.start(piece_refs[p], sources.at[p]) for p in range(count)]
        waits = [copies.start(proj_hbm, proj_ref), copies.start(weight_hbm, weight_ref)]
        z, x, core = lax.axis_index("z"), lax.axis_index("x"), lax.axis_index("core")
        y = lax.axis_index("yhi") * 2 + lax.axis_index("ylo")
        extra = jnp.zeros((EXTRA, wide), F32)
        for p, (side, steps) in enumerate([(side, steps) for side in (0, 1) for steps in (0, 1, 3, 2)]):
            arriving[p].wait()
            extra = extra + sources[p, rows:].astype(F32)
            other = (y - steps) & 3
            member = ((other & 1) * 2 + ((core + side) & 1)) * 2 + (other >> 1)
            for part in range(2):
                place = 2 * member + part
                turn = (place & 3) * N + (place >> 2)
                block = ((z + (place & 3)) & 3) * N + ((x + (place >> 2)) & 3)
                value = sources[p, :rows, part * width:(part + 1) * width]
                whole[:, pl.ds(pl.multiple_of(block * width, width), width)] = value
                flipped = value.T
                first[place] = flipped
                second[turn] = flipped
        leaving = [copies.start(first, first_hbm), copies.start(second, second_hbm)]
        for i in range(deep):
            squares = extra[i:i + 1] + extra[deep + i:deep + i + 1] + extra[2 * deep + i:2 * deep + i + 1]
            inverse_ref[i * wide:(i + 1) * wide] = lax.rsqrt(down(squares) / D + epsilon)
        line = jnp.sum(
            jnp.sum(extra[3 * deep:3 * deep + 3], axis=0, keepdims=True), axis=1, keepdims=True
        )
        line = embed_ref[...].astype(F32) * lax.rsqrt(line / D + epsilon)
        line_ref[...] = line.astype(BF).astype(F32)
        waits[0].wait()
        for i in range(share // 128):
            at = slice(i * 128, (i + 1) * 128)
            normed_ref[:, at] = (proj_ref[:, at].astype(F32) * inverse_ref[...]).astype(BF)
        leaving.append(copies.start(normed_ref, normed_hbm))
        for i in range(4):
            start, stop = CUTS[i % 2]
            left = (first, second)[i // 2][start:stop].reshape(N * width, rows)
            right = normed_ref[:, (i // 2) * half:(i // 2 + 1) * half]
            staged[i] = jnp.dot(left, right, preferred_element_type=F32).astype(BF)
            leaving.append(copies.start(staged.at[i], sends[i]))
        waits[1].wait()
        products = jnp.zeros((rows, 1), F32)
        for i in range(share // CHUNK):
            at = slice(i * CHUNK, (i + 1) * CHUNK)
            grad = jnp.dot(whole[...], weight_ref[:, at], preferred_element_type=F32).astype(BF)
            grad_ref[:, at] = grad
            leaving.append(copies.start(grad_ref.at[:, at], grad_hbm.at[:, at]))
            products = products + jnp.sum(
                grad.astype(F32) * proj_ref[:, at].astype(F32), axis=1, keepdims=True
            )
        products = jnp.broadcast_to(products, (rows, 128)).T
        products = jnp.concatenate(
            [products[:1, i * 128:(i + 1) * 128] for i in range(rows // 128)]
            + [jnp.zeros((8 - rows // 128, 128), F32)],
            axis=0,
        )
        products_ref[...] = jnp.broadcast_to(products[None], products_ref.shape)
        for copy in leaving:
            copy.wait()

    turned = jax.ShapeDtypeStruct((blocks, width, rows), dtype)
    grad = jax.ShapeDtypeStruct((rows, share), BF)
    outs = step(
        kernel,
        "tile_step",
        [(piece, ANY) for piece in pieces]
        + [(projected, HBM), (key_value_weight, HBM), (newline_embed, VMEM)],
        [
            (turned, HBM),
            (turned, HBM),
            (grad, HBM),
            (grad, HBM),
        ]
        + [(jax.ShapeDtypeStruct((N * width, half), BF), HBM)] * 4
        + [
            (jax.ShapeDtypeStruct((count, 8, 128), F32), VMEM),
            (jax.ShapeDtypeStruct((rows, 128), F32), VMEM),
            (jax.ShapeDtypeStruct((1, share), F32), VMEM),
        ],
        [
            VMEM((count,) + pieces[0].shape, dtype),
            VMEM(projected.shape, BF),
            VMEM(key_value_weight.shape, BF),
            VMEM(turned.shape, dtype),
            VMEM(turned.shape, dtype),
            VMEM(grad.shape, BF),
            VMEM(grad.shape, BF),
            VMEM((4, N * width, half), BF),
            VMEM((rows, wide * count), dtype),
        ],
        count + 9 + share // CHUNK,
    )
    return outs[:2], outs[2:4], outs[4:8], outs[8:]


def rest(name, sources, rhs):
    rows, share = rhs.shape
    half = share // 2

    def kernel(*refs):
        source_refs, rhs_hbm, outs = refs[:6], refs[6], refs[7:13]
        held, rhs_ref, staged, sems = refs[13:19], refs[19], refs[20:22], refs[22]
        copies = Copies(sems)
        arriving = [copies.start(source_refs[i], held[i]) for i in range(6)]
        copies.start(rhs_hbm, rhs_ref).wait()
        leaving = []
        for i in (2, 5, 0, 1, 3, 4):
            arriving[i].wait()
            right = rhs_ref[:, (i // 3) * half:(i // 3 + 1) * half]
            value = jnp.dot(held[i][...], right, preferred_element_type=F32)
            if i % 3 == 2:
                staged[i // 3][...] = value
                leaving.append(copies.start(staged[i // 3], outs[i]))
            else:
                outs[i][...] = value
        for copy in leaving:
            copy.wait()

    shapes = [jax.ShapeDtypeStruct((source.shape[0], half), F32) for source in sources]
    outs = step(
        kernel,
        name,
        [(source, HBM) for source in sources] + [(rhs, HBM)],
        [(shape, HBM if i % 3 == 2 else VMEM) for i, shape in enumerate(shapes)],
        [VMEM(source.shape, BF) for source in sources]
        + [VMEM(rhs.shape, BF)]
        + [VMEM(shapes[i].shape, F32) for i in (2, 5)],
        9,
        limit=14,
    )
    return outs[:3], outs[3:]


def kv_rest(turned, normed):
    blocks, width, rows = turned[0].shape
    half = normed.shape[1] // 2

    def kernel(first_hbm, second_hbm, normed_hbm, *refs):
        outs, (first_ref, second_ref, normed_ref), staged, sems = refs[:6], refs[6:9], refs[9:11], refs[11]
        copies = Copies(sems)
        arriving = [
            copies.start(source.at[pl.ds(start, stop - start)], target.at[pl.ds(start, stop - start)])
            for source, target in ((first_hbm, first_ref), (second_hbm, second_ref))
            for start, stop in CUTS[2:]
        ]
        copies.start(normed_hbm, normed_ref).wait()
        leaving = []
        for i in (2, 5, 0, 1, 3, 4):
            arriving[i].wait()
            start, stop = CUTS[2 + i % 3]
            left = (first_ref, second_ref)[i // 3][start:stop].reshape((stop - start) * width, rows)
            right = normed_ref[:, (i // 3) * half:(i // 3 + 1) * half]
            value = jnp.dot(left, right, preferred_element_type=F32)
            if i % 3 == 2:
                staged[i // 3][...] = value
                leaving.append(copies.start(staged[i // 3], outs[i]))
            else:
                outs[i][...] = value
        for copy in leaving:
            copy.wait()

    shapes = [jax.ShapeDtypeStruct(((stop - start) * width, half), F32) for start, stop in CUTS[2:]] * 2
    outs = step(
        kernel,
        "kv_rest",
        [(turned[0], HBM), (turned[1], HBM), (normed, HBM)],
        [(shape, HBM if i % 3 == 2 else VMEM) for i, shape in enumerate(shapes)],
        [VMEM(turned[0].shape, BF)] * 2 + [VMEM(normed.shape, BF)] + [VMEM(shapes[2].shape, F32)] * 2,
        9,
        limit=12,
    )
    return outs[:3], outs[3:]


def x_first(products, grad, projected, inverse, features1, features2):
    rows, share = grad.shape
    half = share // 2
    size = features1[0].shape[0]

    def kernel(products_ref, grad_hbm, proj_hbm, inverse_ref, *refs):
        features, out_hbm, sends = refs[:4], refs[4], refs[5:9]
        grad_ref, proj_ref, out, sources, staged, sems = refs[9:]
        copies = Copies(sems)
        ready = [copies.start(grad_hbm, grad_ref), copies.start(proj_hbm, proj_ref)]
        arriving = [copies.start(features[i], sources.at[i]) for i in range(4)]
        total = jnp.sum(products_ref[...], axis=0)
        total = jnp.concatenate([down(total[i:i + 1]) for i in range(rows // 128)], axis=0)
        inv = inverse_ref[...]
        scale = inv * inv * inv * total / D
        for copy in ready:
            copy.wait()
        for i in range(share // 128):
            at = slice(i * 128, (i + 1) * 128)
            out[:, at] = (
                inv * grad_ref[:, at].astype(F32) - scale * proj_ref[:, at].astype(F32)
            ).astype(BF)
        leaving = [copies.start(out, out_hbm)]
        for i in range(4):
            arriving[i].wait()
            right = out[:, (i // 2) * half:(i // 2 + 1) * half]
            staged[i] = jnp.dot(sources[i], right, preferred_element_type=F32).astype(BF)
            leaving.append(copies.start(staged.at[i], sends[i]))
        for copy in leaving:
            copy.wait()

    outs = step(
        kernel,
        "x_first",
        [(products, VMEM), (grad, HBM), (projected, HBM), (inverse, VMEM)]
        + [(cut, HBM) for cut in (features1[0], features1[1], features2[0], features2[1])],
        [(jax.ShapeDtypeStruct((rows, share), BF), HBM)]
        + [(jax.ShapeDtypeStruct((size, half), BF), HBM)] * 4,
        [
            VMEM(grad.shape, BF),
            VMEM(projected.shape, BF),
            VMEM(grad.shape, BF),
            VMEM((4,) + features1[0].shape, BF),
            VMEM((4, size, half), BF),
        ],
        11,
        limit=16,
    )
    return outs[0], outs[1:3], outs[3:5]


class Sums:
    def __init__(self, partials, rows, part):
        self.partials = partials
        self.rows, self.part = rows, part
        self.half, self.down = 2 * rows, rows - part

    def first_b(self, ahead, behind):
        self.ahead, self.behind = ahead, behind
        return (
            (self.partials[0] + ahead[self.half:].astype(F32)).astype(BF),
            (self.partials[1] + behind[:self.half].astype(F32)).astype(BF),
        )

    def second_a(self, ahead, behind):
        half, rows, part = self.half, self.rows, self.part
        own = self.partials[2]
        self.low = own[:half] + self.behind[half:].astype(F32) + ahead.astype(F32)
        self.high = own[half:] + self.ahead[:half].astype(F32) + behind.astype(F32)
        return (
            jnp.concatenate([self.low[rows + part:].astype(BF), self.high[:part].astype(BF)], axis=0),
            self.high[part:rows + part].astype(BF),
        )

    def second_b(self, ahead, behind):
        rows, part, down = self.rows, self.part, self.down
        self.ahead2, self.behind2 = ahead, behind
        return (
            (self.low[rows:rows + part] + ahead[down:].astype(F32)).astype(BF),
            (self.high[rows + part:] + behind[:down].astype(F32)).astype(BF),
        )

    def result(self, ahead, behind):
        rows, part, down = self.rows, self.part, self.down
        return jnp.concatenate(
            [
                self.low[:part] + self.behind2[down:].astype(F32) + ahead.astype(F32),
                self.low[part:rows] + self.ahead2[:down].astype(F32) + behind.astype(F32),
            ],
            axis=0,
        )


def both_ways(pair, axis):
    return shift(pair[0], axis, N, 1), shift(pair[1], axis, N, 3)


def packed_both_ways(one, two, axis):
    moved = both_ways([jnp.concatenate([a, b], axis=0) for a, b in zip(one, two)], axis)
    return [m[:a.shape[0]] for m, a in zip(moved, one)], [m[a.shape[0]:] for m, a in zip(moved, one)]


def local(
    siglip_features,
    convnext_features,
    siglip_projection,
    convnext_projection,
    newline_embed,
    key_value_weight,
    tile_rank,
    row_end,
    key_value_grad,
    newline_grad,
):
    blocks = N * N
    z, x = lax.axis_index("z"), lax.axis_index("x")
    my_rank = z * N + x
    tiles = tile_rank.shape[0]
    per_device = tiles // blocks
    rows = siglip_features.shape[0]
    share = siglip_projection.shape[1]
    half = share // 2
    kv_rows = key_value_weight.shape[0] // blocks
    sig_rows = siglip_features.shape[1] // blocks
    conv_rows = convnext_features.shape[1] // blocks

    dest_rank = tile_rank.reshape(tiles)
    mine = lax.dynamic_slice_in_dim(dest_rank, my_rank * per_device, per_device)
    outgoing = slices_out(key_value_grad, newline_grad)
    received = lax.all_to_all(outgoing, DP, split_axis=0, concat_axis=0, tiled=True)

    projected = (
        jnp.dot(siglip_features, siglip_projection, preferred_element_type=F32)
        + jnp.dot(convnext_features, convnext_projection, preferred_element_type=F32)
    ).astype(BF)
    proj_values = projected.astype(F32)
    line_vector = newline_embed.astype(F32)
    wide = received.shape[2]
    deep = rows // wide
    squares = jnp.sum(proj_values * proj_values, axis=1).reshape(deep, wide)
    line_squares = jnp.sum((line_vector * line_vector).reshape(share // wide, wide), axis=0)[None]
    statistics = extra_rows(thirds(squares) + thirds(line_squares))

    features1, features2 = turn_features(siglip_features, convnext_features)
    x_rows = sig_rows + conv_rows
    received, statistics, features1, features2 = lax.optimization_barrier(
        (received, statistics, features1, features2)
    )
    own = pick_tiles(received, mine, statistics)
    own, received, dest_rank, row_end = lax.optimization_barrier((own, received, dest_rank, row_end))
    ring = [own] + [shift_y(own, s) for s in (1, 3, 2)]
    pieces = ring + [shift(piece, "core", 2, 1) for piece in ring]

    onehot = (dest_rank[:, None] == jnp.arange(blocks, dtype=jnp.int32)[None, :]).astype(jnp.int32)
    grouped = onehot.reshape(blocks, per_device, blocks)
    before = jnp.cumsum(grouped, axis=1) - grouped
    slot_place = jnp.sum(before * grouped, axis=2).reshape(tiles)
    slot = (jnp.arange(tiles, dtype=jnp.int32) // per_device) * CAP + slot_place
    slot_index = dest_rank * (blocks * CAP) + slot
    mask = jnp.sum(
        (
            (slot_index[:, None] == jnp.arange(blocks * blocks * CAP, dtype=jnp.int32)[None, :])
            & (row_end[:, None] == 1)
        ).astype(F32),
        axis=0,
    ).astype(BF)
    mask = mask.reshape(blocks, 2, blocks)
    line_rows = received[:, CAP * TT:]
    line_total = sum(
        jnp.dot(
            mask[:, part].reshape(1, blocks * blocks),
            line_rows[:, :, part * kv_rows:(part + 1) * kv_rows].reshape(blocks * blocks, kv_rows),
            preferred_element_type=F32,
        )
        for part in range(2)
    )
    line_total = jnp.broadcast_to(line_total, (kv_rows, kv_rows)).T

    turned, (normed_grad, normed), kv_sends, (products, inverse, line_normed) = tile_step(
        pieces, projected, key_value_weight, newline_embed.reshape(1, share)
    )
    products = lax.all_to_all(products, ("ylo", "core", "yhi"), split_axis=0, concat_axis=0, tiled=True)

    in0, in1 = both_ways(kv_sends[:2], "x"), both_ways(kv_sends[2:], "z")
    kv_parts0, kv_parts1 = kv_rest(turned, normed)
    kv0 = Sums(kv_parts0, kv_rows, kv_rows // 2)
    kv1 = Sums(kv_parts1, kv_rows, kv_rows // 2)
    out0, out1 = kv0.first_b(*in0), kv1.first_b(*in1)

    projected_grad, x_send0, x_send1 = x_first(
        products, normed_grad, projected, inverse, features1, features2
    )
    x_in0, x_in1 = both_ways(x_send0, "x"), both_ways(x_send1, "z")
    out0, out1, projected_grad = lax.optimization_barrier((out0, out1, projected_grad))
    in0, in1 = both_ways(out0, "x"), both_ways(out1, "z")
    kv_out0, kv_out1 = kv0.second_a(*in0), kv1.second_a(*in1)
    in0, in1 = x_in0, x_in1
    x_parts0, x_parts1 = rest("x_rest", list(features1[2:]) + list(features2[2:]), projected_grad)
    part = (x_rows // 2 + 7) // 8 * 8
    x0 = Sums(x_parts0, x_rows, part)
    x1 = Sums(x_parts1, x_rows, part)
    in0, in1 = both_ways(x0.first_b(*in0), "x"), both_ways(x1.first_b(*in1), "z")
    in0, kv_in0 = packed_both_ways(x0.second_a(*in0), kv_out0, "z")
    in1, kv_in1 = packed_both_ways(x1.second_a(*in1), kv_out1, "x")
    in0, kv_in0 = packed_both_ways(x0.second_b(*in0), kv0.second_b(*kv_in0), "z")
    in1, kv_in1 = packed_both_ways(x1.second_b(*in1), kv1.second_b(*kv_in1), "x")
    kv_result = jnp.concatenate([kv0.result(*kv_in0), kv1.result(*kv_in1)], axis=1)
    kv_result = kv_result + line_total[:, :1] * line_normed
    x_result = jnp.concatenate([x0.result(*in0), x1.result(*in1)], axis=1)
    return x_result[:sig_rows], x_result[sig_rows:], kv_result


def solution(mesh):
    fine = Mesh(mesh.devices.reshape(2, 2, N, N, 2), ("ylo", "core", "z", "x", "yhi"))
    wide = ("ylo", "core", "yhi")
    in_specs = (
        P(DP, None),
        P(DP, None),
        P(None, wide),
        P(None, wide),
        P(wide),
        P(None, wide),
        P(),
        P(),
        P(DP, None),
        P(DP, None),
    )
    out_specs = (P(DP, wide), P(DP, wide), P(DP, wide))
    return jax.shard_map(local, mesh=fine, in_specs=in_specs, out_specs=out_specs, check_vma=False)
```

time: 161 us -> 142 us (0.88)
  Pallas kernels: 9.65 us -> 30.4 us
  matrix products: 25.2 us -> 6.82 us
  local copies, waits for them, and re-layouts: 16.3 us -> 3.92 us
  waiting for transfers between devices: 40 us -> 33.4 us
  other arithmetic: 15.2 us -> 9.43 us
  starting transfers between devices: 51.1 us -> 55 us
    pallas_call x5 -> x7, Pallas kernels: 9.65 us -> 30.4 us  [the longest x4 21.2 us: step(): pl.pallas_call(kernel, out_shape=[space(shape.shape, shape.dtype) for sha...]
    dot_general x22 -> x2, matrix products: 18.7 us -> 0.25 us  [local(): jnp.dot(mask[:, part].reshape(1, blocks * blocks), line_rows[:, :, part *...]
    ppermute x29 -> x28, waiting for transfers between devices: 33.8 us -> 22.6 us  [shift(): lax.ppermute(value, axis, [(i, (i + step) % size) for i in range(size)])]
    ppermute x29 -> x28, starting transfers between devices: 30.3 us -> 38.2 us  [shift(): lax.ppermute(value, axis, [(i, (i + step) % size) for i in range(size)])]
    unnamed x99 -> x30, local copies, waits for them, and re-layouts: 6.04 us -> 1.02 us
    convert_element_type x25 -> x14, other arithmetic: 8.16 us -> 3.71 us  [the longest x4 2.28 us: first_b(): (self.partials[0] + ahead[self.half:].astype(F32)).astype(BF)]
    ppermute x6 -> x3, starting transfers between devices: 9.47 us -> 5.29 us  [shift_y(): lax.ppermute(value, Y, [(place(y), place((y + step) % N)) for y in range(...]
    transpose x2 -> x0, local copies, waits for them, and re-layouts: 3.29 us -> none  [the longest x1 1.72 us: local(): convnext_features.T.reshape(blocks, conv_rows, rows)]
  transfers between devices with their start and end apart: 37 -> 33, of which waited for: 20 -> 14; matrix products, arithmetic and copies ran while one was open for 25% -> 12% of each run, Pallas kernels for 1% -> 12%
where the time goes in v3:
time: 142 us; the launch traced here: 140 us
  starting transfers between devices  55 us (39%)
  waiting for transfers between devices  33.4 us (24%)
  Pallas kernels  30.4 us (21%)
  other arithmetic  9.43 us (7%)
  matrix products  6.82 us (5%)
  local copies, waits for them, and re-layouts  3.92 us (3%)
    ppermute x28, starting transfers between devices, shift(): lax.ppermute(value, axis, [(i, (i + step) % size) for i in range(size)])  38.2 us
    ppermute x28, waiting for transfers between devices, shift(): lax.ppermute(value, axis, [(i, (i + step) % size) for i in range(size)])  22.6 us
    pallas_call x4, Pallas kernels, step(): pl.pallas_call(kernel, out_shape=[space(shape.shape, shape.dtype) for sha...  21.2 us
    ppermute x3, waiting for transfers between devices, shift_y(): lax.ppermute(value, Y, [(place(y), place((y + step) % N)) for y in range(...  9.2 us
    all_to_all x1, starting transfers between devices, local(): lax.all_to_all(outgoing, DP, split_axis=0, concat_axis=0, tiled=True)  8.02 us
    ppermute x3, starting transfers between devices, shift_y(): lax.ppermute(value, Y, [(place(y), place((y + step) % N)) for y in range(...  5.29 us
    dot_general x1, matrix products, local(): jnp.dot(siglip_features, siglip_projection, preferred_element_type=F32)  3.66 us
    all_to_all x1, starting transfers between devices, local(): lax.all_to_all(products, ('ylo', 'core', 'yhi'), split_axis=0, concat_axi...  3.53 us
  transfers between devices with their start and end apart: 33, of which 14 were waited for; matrix products, arithmetic and copies ran while one was open for 12% of the time, Pallas kernels for 12%

profile of v3, /device:TPU:0, one launch (start us, length us, event | category | flops | bytes accessed | tf_op | source)
XLA Modules:
  0.0 140.3 jit_solution(13391993974522452552)
XLA Ops:
  0.6 2.7 %slices_out.1 = bf16[16,80,256]{2,1,0:T(8,128)(2,1)} custom-call(bf16[1024,2048]{1,0:T(8,128)(2,1)} %source.1, bf16[32,2048]{1,0:T(8,128)(2,1)} %lines.1), custom_call_target="tpu_custom_call" | custom-call | tf_op jit(solution)/shard_map/slices_out/pallas_call | solution.py:85
  3.3 8.0 %all-to-all-start = ((bf16[16,80,256]{2,1,0:T(8,128)(2,1)}), bf16[16,80,256]{2,1,0:T(8,128)(2,1)}, u32[]{:S(2)}, u32[]{:S(2)}) async-start(bf16[16,80,256]{2,1,0:T(8,128)(2,1)} %slices_out.1), calls=%async_computation | async-start | bytes 1310720 | tf_op jit(solution)/shard_map/all_to_all | solution.py:564
  11.4 3.7 %fusion.33 = f32[512,1024]{1,0:T(8,128)S(1)} fusion(bf16[512,1152]{1,0:T(8,128)(2,1)} %siglip_ref.1, bf16[1152,1024]{1,0:T(8,128)(2,1)} %param.12), kind=kOutput, calls=%fused_computation.106 | convolution fusion | flops 1207959552 | bytes 5636096 | tf_op jit(solution)/shard_map/dot_general | solution.py:567
  15.1 2.9 %multiply_reduce_fusion = (f32[512]{0:T(512)S(1)}, bf16[512,1024]{1,0:T(8,128)(2,1)}) fusion(f32[512,1024]{1,0:T(8,128)S(1)} %fusion.33, bf16[512,1536]{1,0:T(8,128)(2,1)S(1)} %copy-done.2, bf16[1536,1024]{1,0:T(8,128)(2,1)S(1)} %copy-done), kind=kOutput, calls=%fused_computation | convolution fusion | flops 1613233664 | bytes 7866368 | tf_op jit(solution)/shard_map/dot_general | solution.py:568
  18.0 3.4 %turn_features.1 = (bf16[672,512]{1,0:T(8,128)(2,1)}, bf16[672,512]{1,0:T(8,128)(2,1)}, bf16[336,512]{1,0:T(8,128)(2,1)}, bf16[336,512]{1,0:T(8,128)(2,1)}, bf16...) custom-call(bf16[512,1152]{1,0:T(8,128)(2,1)S(1)} %copy-done.3, ...), custom_call_target="tpu_custom_call" | custom-call | tf_op jit(solution)/shard_map/turn_features/pallas_call | solution.py:142
  24.4 3.1 %pick_tiles.1.refs_0_ = bf16[528,256]{1,0:T(8,128)(2,1)} custom-call(s32[16]{0:T(128)} %dynamic-slice_bitcast_fusion.dest_ref, bf16[16,80,256]{2,1,0:T(8,128)(2,1)} %all-to-all-done.source, bf16[16,256]{1,0:T(8,128)(2,1)} %pad.5.extra_ref), custom_call_target="tpu_custom_call" | custom-call | tf_op jit(solution)/shard_map/pick_tiles/pallas_call | solution.py:189
  33.6 3.7 %collective-permute-done.refs_1_ = bf16[528,256]{1,0:T(8,128)(2,1)S(1)} collective-permute-done((bf16[528,256]{1,0:T(8,128)(2,1)}, bf16[528,256]{1,0:T(8,128)(2,1)S(1)}, u32[]{:S(2)}, u32[]{:S(2)}) %collective-permute-start) | collective-permute-done | bytes 270368 | tf_op jit(solution)/shard_map/ppermute | solution.py:25
  37.3 3.8 %collective-permute-done.1.refs_2_ = bf16[528,256]{1,0:T(8,128)(2,1)S(1)} collective-permute-done((bf16[528,256]{1,0:T(8,128)(2,1)}, bf16[528,256]{1,0:T(8,128)(2,1)S(1)}, u32[]{:S(2)}, u32[]{:S(2)}) %collective-permute-start.1) | collective-permute-done | bytes 270368 | tf_op jit(solution)/shard_map/ppermute | solution.py:25
  45.3 7.3 %tile_step.1 = (bf16[16,128,512]{2,1,0:T(8,128)(2,1)}, bf16[16,128,512]{2,1,0:T(8,128)(2,1)}, bf16[512,1024]{1,0:T(8,128)(2,1)}, bf16[512,1024]{1,0:T(8,128)(2,1...) custom-call(bf16[528,256]{1,0:T(8,128)(2,1)S(1)} %copy-done.4, ...), custom_call_target="tpu_custom_call" | custom-call | tf_op jit(solution)/shard_map/tile_step/pallas_call | solution.py:207
  56.4 3.5 %all-to-all-start.1 = ((f32[8,8,128]{2,1,0:T(8,128)}), f32[8,8,128]{2,1,0:T(8,128)S(1)}, u32[]{:S(2)}, u32[]{:S(2)}) async-start(f32[8,8,128]{2,1,0:T(8,128)} %get-tuple-element.92), calls=%async_computation.1 | async-start | bytes 65536 | tf_op jit(solution)/shard_map/all_to_all | solution.py:616
  62.7 4.1 %kv_rest.1 = (f32[256,512]{1,0:T(8,128)S(1)}, f32[256,512]{1,0:T(8,128)S(1)}, f32[512,512]{1,0:T(8,128)}, f32[256,512]{1,0:T(8,128)S(1)}, f32[256,512]{1,0:T(8,128)S(1)}, /*index=5*/f32[512,512]{1,0:T(8,128)}) custom-call(bf16[16,128,512]{2,1,0:T(8,128)(2,1)} %get-tuple-element.81.first_hbm, bf16[16,128,512]{2,1,0:T(8,128)(2,1)} %get-tuple-element.82.second_hbm, ...), custom_call_target="tpu_custom_call" | custom-call | tf_op jit(solution)/shard_map/kv_rest/pallas_call | solution.py:207
  66.8 5.3 %x_first.1 = (bf16[512,1024]{1,0:T(8,128)(2,1)}, bf16[672,512]{1,0:T(8,128)(2,1)}, bf16[672,512]{1,0:T(8,128)(2,1)}, bf16[672,512]{1,0:T(8,128)(2,1)}, bf16[672,512]{1,0:T(8,128)(2,1)}) custom-call(f32[8,8,128]{2,1,0:T(8,128)S(1)} %all-to-all-done.1.products_ref, bf16[512,1024]{1,0:T(8,128)(2,1)} %get-tuple-element.93.grad_hbm, ...), custom_call_target="tpu_custom_call" | custom-call | tf_op jit(solution)/shard_map/x_first/pallas_call | solution.py:207
  84.1 4.6 %x_rest.1 = (f32[336,512]{1,0:T(8,128)S(1)}, f32[336,512]{1,0:T(8,128)S(1)}, f32[672,512]{1,0:T(8,128)}, f32[336,512]{1,0:T(8,128)S(1)}, f32[336,512]{1,0:T(8,128)S(1)}, /*index=5*/f32[672,512]{1,0:T(8,128)}) custom-call(bf16[336,512]{1,0:T(8,128)(2,1)} %get-tuple-element.72.refs_0_, bf16[336,512]{1,0:T(8,128)(2,1)} %get-tuple-element.73.refs_1_, ...), custom_call_target="tpu_custom_call" | custom-call | tf_op jit(solution)/shard_map/x_rest/pallas_call | solution.py:207
  88.7 4.3 %collective-permute-done.12 = bf16[672,512]{1,0:T(8,128)(2,1)S(1)} collective-permute-done((bf16[672,512]{1,0:T(8,128)(2,1)}, bf16[672,512]{1,0:T(8,128)(2,1)S(1)}, u32[]{:S(2)}, u32[]{:S(2)}) %collective-permute-start.12) | collective-permute-done | bytes 688160 | tf_op jit(solution)/shard_map/ppermute | solution.py:20
  93.1 3.3 %collective-permute-start.25 = (bf16[256,512]{1,0:T(8,128)(2,1)S(1)}, bf16[256,512]{1,0:T(8,128)(2,1)S(1)}, u32[]{:S(2)}, u32[]{:S(2)}) collective-permute-start(bf16[256,512]{1,0:T(8,128)(2,1)S(1)} %add_convert_fusion.5), channel_id=1, source_target_pairs={{0,24},{8,0},{16,8},{24,16},{1,25},{9,1},{17,9},{25,17},{2,26},{10... | collective-permute-start | bytes 786440 | tf_op jit(solution)/shard_map/ppermute | solution.py:20
  97.1 3.2 %collective-permute-start.14 = (bf16[336,512]{1,0:T(8,128)(2,1)S(1)}, bf16[336,512]{1,0:T(8,128)(2,1)S(1)}, u32[]{:S(2)}, u32[]{:S(2)}) collective-permute-start(bf16[336,512]{1,0:T(8,128)(2,1)S(1)} %add_convert_fusion.3), channel_id=1, source_target_pairs={{0,6},{2,0},{4,2},{6,4},{1,7},{3,1},{5,3},{7,5},{8,14},{10,8},{12,... | collective-permute-start | bytes 1032200 | tf_op jit(solution)/shard_map/ppermute | solution.py:20
  100.2 3.2 %collective-permute-done.17 = bf16[256,512]{1,0:T(8,128)(2,1)S(1)} collective-permute-done((bf16[256,512]{1,0:T(8,128)(2,1)S(1)}, bf16[256,512]{1,0:T(8,128)(2,1)S(1)}, u32[]{:S(2)}, u32[]{:S(2)}) %collective-permute-start.17) | collective-permute-done | bytes 262176 | tf_op jit(solution)/shard_map/ppermute | solution.py:20
  109.5 3.0 %collective-permute-done.23 = bf16[336,512]{1,0:T(8,128)(2,1)S(1)} collective-permute-done((bf16[336,512]{1,0:T(8,128)(2,1)S(1)}, bf16[336,512]{1,0:T(8,128)(2,1)S(1)}, u32[]{:S(2)}, u32[]{:S(2)}) %collective-permute-start.23) | collective-permute-done | bytes 344096 | tf_op jit(solution)/shard_map/ppermute | solution.py:20
  112.9 2.9 %collective-permute-start.16 = (bf16[296,512]{1,0:T(8,128)(2,1)S(1)}, bf16[296,512]{1,0:T(8,128)(2,1)S(1)}, u32[]{:S(2)}, u32[]{:S(2)}) collective-permute-start(bf16[296,512]{1,0:T(8,128)(2,1)S(1)} %pad_maximum_fusion.2), channel_id=1, source_target_pairs={{0,24},{8,0},{16,8},{24,16},{1,25},{9,1},{17,9},{25,17},{2,26},{10... | collective-permute-start | bytes 909320 | tf_op jit(solution)/shard_map/ppermute | solution.py:20
  116.0 3.3 %collective-permute-start.26 = (bf16[296,512]{1,0:T(8,128)(2,1)S(1)}, bf16[296,512]{1,0:T(8,128)(2,1)S(1)}, u32[]{:S(2)}, u32[]{:S(2)}) collective-permute-start(bf16[296,512]{1,0:T(8,128)(2,1)S(1)} %pad_maximum_fusion.4), channel_id=1, source_target_pairs={{0,6},{2,0},{4,2},{6,4},{1,7},{3,1},{5,3},{7,5},{8,14},{10,8},{12,... | collective-permute-start | bytes 909320 | tf_op jit(solution)/shard_map/ppermute | solution.py:20
  120.9 3.1 %collective-permute-start.20 = (bf16[144,512]{1,0:T(8,128)(2,1)S(1)}, bf16[144,512]{1,0:T(8,128)(2,1)S(1)}, u32[]{:S(2)}, u32[]{:S(2)}) collective-permute-start(bf16[144,512]{1,0:T(8,128)(2,1)S(1)} %pad_maximum_fusion.8), channel_id=1, source_target_pairs={{0,24},{8,0},{16,8},{24,16},{1,25},{9,1},{17,9},{25,17},{2,26},{10... | collective-permute-start | bytes 442376 | tf_op jit(solution)/shard_map/ppermute | solution.py:20
  124.3 3.8 %collective-permute-start.30 = (bf16[144,512]{1,0:T(8,128)(2,1)S(1)}, bf16[144,512]{1,0:T(8,128)(2,1)S(1)}, u32[]{:S(2)}, u32[]{:S(2)}) collective-permute-start(bf16[144,512]{1,0:T(8,128)(2,1)S(1)} %pad_maximum_fusion.9), channel_id=1, source_target_pairs={{0,6},{2,0},{4,2},{6,4},{1,7},{3,1},{5,3},{7,5},{8,14},{10,8},{12,... | collective-permute-start | bytes 442376 | tf_op jit(solution)/shard_map/ppermute | solution.py:20
  131.3 3.4 %collective-permute-done.19 = bf16[152,512]{1,0:T(8,128)(2,1)S(1)} collective-permute-done((bf16[152,512]{1,0:T(8,128)(2,1)S(1)}, bf16[152,512]{1,0:T(8,128)(2,1)S(1)}, u32[]{:S(2)}, u32[]{:S(2)}) %collective-permute-start.19) | collective-permute-done | bytes 155680 | tf_op jit(solution)/shard_map/ppermute | solution.py:20
  134.8 3.0 %collective-permute-done.29 = bf16[152,512]{1,0:T(8,128)(2,1)S(1)} collective-permute-done((bf16[152,512]{1,0:T(8,128)(2,1)S(1)}, bf16[152,512]{1,0:T(8,128)(2,1)S(1)}, u32[]{:S(2)}, u32[]{:S(2)}) %collective-permute-start.29) | collective-permute-done | bytes 155680 | tf_op jit(solution)/shard_map/ppermute | solution.py:20
  (154 shorter events, 46.6 us)
Async XLA Ops:
  3.3 21.0 %all-to-all-start = ((bf16[16,80,256]{2,1,0:T(8,128)(2,1)}), bf16[16,80,256]{2,1,0:T(8,128)(2,1)}, u32[]{:S(2)}, u32[]{:S(2)}) async-start(bf16[16,80,256]{2,1,0:T(8,128)(2,1)} %slices_out.1), calls=%async_computation | async-start | bytes 1310720 | tf_op jit(solution)/shard_map/all_to_all | solution.py:564
  27.5 9.8 %collective-permute-start = (bf16[528,256]{1,0:T(8,128)(2,1)}, bf16[528,256]{1,0:T(8,128)(2,1)S(1)}, u32[]{:S(2)}, u32[]{:S(2)}) collective-permute-start(bf16[528,256]{1,0:T(8,128)(2,1)} %pick_tiles.1.refs_0_), channel_id=1, source_target_pairs={{0,64},{64,1},{1,65},{65,0},{2,66},{66,3},{3,67},{67,2},{4,68},{68... | collective-permute-start | bytes 811016 | tf_op jit(solution)/shard_map/ppermute | solution.py:25
  29.1 12.0 %collective-permute-start.1 = (bf16[528,256]{1,0:T(8,128)(2,1)}, bf16[528,256]{1,0:T(8,128)(2,1)S(1)}, u32[]{:S(2)}, u32[]{:S(2)}) collective-permute-start(bf16[528,256]{1,0:T(8,128)(2,1)} %pick_tiles.1.refs_0_), channel_id=1, source_target_pairs={{0,65},{64,0},{1,64},{65,1},{2,67},{66,2},{3,66},{67,3},{4,69},{68... | collective-permute-start | bytes 811016 | tf_op jit(solution)/shard_map/ppermute | solution.py:25
  30.8 12.0 %collective-permute-start.2 = (bf16[528,256]{1,0:T(8,128)(2,1)}, bf16[528,256]{1,0:T(8,128)(2,1)S(1)}, u32[]{:S(2)}, u32[]{:S(2)}) collective-permute-start(bf16[528,256]{1,0:T(8,128)(2,1)} %pick_tiles.1.refs_0_), channel_id=1, source_target_pairs={{0,1},{64,65},{1,0},{65,64},{2,3},{66,67},{3,2},{67,66},{4,5},{68,... | collective-permute-start | bytes 811016 | tf_op jit(solution)/shard_map/ppermute | solution.py:25
  32.8 10.4 %collective-permute-start.3 = (bf16[528,256]{1,0:T(8,128)(2,1)}, bf16[528,256]{1,0:T(8,128)(2,1)S(1)}, u32[]{:S(2)}, u32[]{:S(2)}) collective-permute-start(bf16[528,256]{1,0:T(8,128)(2,1)} %pick_tiles.1.refs_0_), channel_id=1, source_target_pairs={{0,32},{32,0},{1,33},{33,1},{2,34},{34,2},{3,35},{35,3},{4,36},{36... | collective-permute-start | bytes 811016 | tf_op jit(solution)/shard_map/ppermute | solution.py:20
  52.5 20.4 %collective-permute-start.10 = (bf16[512,512]{1,0:T(8,128)(2,1)}, bf16[512,512]{1,0:T(8,128)(2,1)S(1)}, u32[]{:S(2)}, u32[]{:S(2)}) collective-permute-start(bf16[512,512]{1,0:T(8,128)(2,1)} %get-tuple-element.91), channel_id=1, source_target_pairs={{0,24},{8,0},{16,8},{24,16},{1,25},{9,1},{17,9},{25,17},{2,26},{10... | collective-permute-start | bytes 1572872 | tf_op jit(solution)/shard_map/ppermute | solution.py:20
  55.9 19.7 %collective-permute-start.9 = (bf16[512,512]{1,0:T(8,128)(2,1)}, bf16[512,512]{1,0:T(8,128)(2,1)}, u32[]{:S(2)}, u32[]{:S(2)}) collective-permute-start(bf16[512,512]{1,0:T(8,128)(2,1)} %get-tuple-element.89), channel_id=1, source_target_pairs={{0,8},{8,16},{16,24},{24,0},{1,9},{9,17},{17,25},{25,1},{2,10},{10... | collective-permute-start | bytes 1572872 | tf_op jit(solution)/shard_map/ppermute | solution.py:20
  56.4 10.4 %all-to-all-start.1 = ((f32[8,8,128]{2,1,0:T(8,128)}), f32[8,8,128]{2,1,0:T(8,128)S(1)}, u32[]{:S(2)}, u32[]{:S(2)}) async-start(f32[8,8,128]{2,1,0:T(8,128)} %get-tuple-element.92), calls=%async_computation.1 | async-start | bytes 65536 | tf_op jit(solution)/shard_map/all_to_all | solution.py:616
  59.9 17.6 %collective-permute-start.8 = (bf16[512,512]{1,0:T(8,128)(2,1)}, bf16[512,512]{1,0:T(8,128)(2,1)}, u32[]{:S(2)}, u32[]{:S(2)}) collective-permute-start(bf16[512,512]{1,0:T(8,128)(2,1)} %get-tuple-element.87), channel_id=1, source_target_pairs={{0,6},{2,0},{4,2},{6,4},{1,7},{3,1},{5,3},{7,5},{8,14},{10,8},{12,... | collective-permute-start | bytes 1572872 | tf_op jit(solution)/shard_map/ppermute | solution.py:20
  62.7 18.3 %collective-permute-start.7 = (bf16[512,512]{1,0:T(8,128)(2,1)}, bf16[512,512]{1,0:T(8,128)(2,1)}, u32[]{:S(2)}, u32[]{:S(2)}) collective-permute-start(bf16[512,512]{1,0:T(8,128)(2,1)} %get-tuple-element.85), channel_id=1, source_target_pairs={{0,2},{2,4},{4,6},{6,0},{1,3},{3,5},{5,7},{7,1},{8,10},{10,12},{12... | collective-permute-start | bytes 1572872 | tf_op jit(solution)/shard_map/ppermute | solution.py:20
  72.1 20.8 %collective-permute-start.12 = (bf16[672,512]{1,0:T(8,128)(2,1)}, bf16[672,512]{1,0:T(8,128)(2,1)S(1)}, u32[]{:S(2)}, u32[]{:S(2)}) collective-permute-start(bf16[672,512]{1,0:T(8,128)(2,1)} %get-tuple-element.104), channel_id=1, source_target_pairs={{0,2},{2,4},{4,6},{6,0},{1,3},{3,5},{5,7},{7,1},{8,10},{10,12},{12... | collective-permute-start | bytes 2064392 | tf_op jit(solution)/shard_map/ppermute | solution.py:20
  73.0 20.1 %collective-permute-start.11 = (bf16[672,512]{1,0:T(8,128)(2,1)}, bf16[672,512]{1,0:T(8,128)(2,1)S(1)}, u32[]{:S(2)}, u32[]{:S(2)}) collective-permute-start(bf16[672,512]{1,0:T(8,128)(2,1)} %get-tuple-element.102), channel_id=1, source_target_pairs={{0,6},{2,0},{4,2},{6,4},{1,7},{3,1},{5,3},{7,5},{8,14},{10,8},{12,... | collective-permute-start | bytes 2064392 | tf_op jit(solution)/shard_map/ppermute | solution.py:20
  75.6 20.9 %collective-permute-start.22 = (bf16[672,512]{1,0:T(8,128)(2,1)}, bf16[672,512]{1,0:T(8,128)(2,1)S(1)}, u32[]{:S(2)}, u32[]{:S(2)}) collective-permute-start(bf16[672,512]{1,0:T(8,128)(2,1)} %get-tuple-element.112), channel_id=1, source_target_pairs={{0,8},{8,16},{16,24},{24,0},{1,9},{9,17},{17,25},{25,1},{2,10},{10... | collective-permute-start | bytes 2064392 | tf_op jit(solution)/shard_map/ppermute | solution.py:20
  77.5 19.2 %collective-permute-start.21 = (bf16[672,512]{1,0:T(8,128)(2,1)S(1)}, bf16[672,512]{1,0:T(8,128)(2,1)S(1)}, u32[]{:S(2)}, u32[]{:S(2)}) collective-permute-start(bf16[672,512]{1,0:T(8,128)(2,1)S(1)} %copy-done.13), channel_id=1, source_target_pairs={{0,24},{8,0},{16,8},{24,16},{1,25},{9,1},{17,9},{25,17},{2,26},{10... | collective-permute-start | bytes 2064392 | tf_op jit(solution)/shard_map/ppermute | solution.py:20
  82.1 15.0 %collective-permute-start.15 = (bf16[256,512]{1,0:T(8,128)(2,1)S(1)}, bf16[256,512]{1,0:T(8,128)(2,1)S(1)}, u32[]{:S(2)}, u32[]{:S(2)}) collective-permute-start(bf16[256,512]{1,0:T(8,128)(2,1)S(1)} %add_convert_fusion.7), channel_id=1, source_target_pairs={{0,6},{2,0},{4,2},{6,4},{1,7},{3,1},{5,3},{7,5},{8,14},{10,8},{12,... | collective-permute-start | bytes 786440 | tf_op jit(solution)/shard_map/ppermute | solution.py:20
  92.9 10.5 %collective-permute-start.17 = (bf16[256,512]{1,0:T(8,128)(2,1)S(1)}, bf16[256,512]{1,0:T(8,128)(2,1)S(1)}, u32[]{:S(2)}, u32[]{:S(2)}) collective-permute-start(bf16[256,512]{1,0:T(8,128)(2,1)S(1)} %add_convert_fusion.8), channel_id=1, source_target_pairs={{0,2},{2,4},{4,6},{6,0},{1,3},{3,5},{5,7},{7,1},{8,10},{10,12},{12... | collective-permute-start | bytes 786440 | tf_op jit(solution)/shard_map/ppermute | solution.py:20
  93.1 11.1 %collective-permute-start.25 = (bf16[256,512]{1,0:T(8,128)(2,1)S(1)}, bf16[256,512]{1,0:T(8,128)(2,1)S(1)}, u32[]{:S(2)}, u32[]{:S(2)}) collective-permute-start(bf16[256,512]{1,0:T(8,128)(2,1)S(1)} %add_convert_fusion.5), channel_id=1, source_target_pairs={{0,24},{8,0},{16,8},{24,16},{1,25},{9,1},{17,9},{25,17},{2,26},{10... | collective-permute-start | bytes 786440 | tf_op jit(solution)/shard_map/ppermute | solution.py:20
  96.5 10.1 %collective-permute-start.27 = (bf16[256,512]{1,0:T(8,128)(2,1)S(1)}, bf16[256,512]{1,0:T(8,128)(2,1)S(1)}, u32[]{:S(2)}, u32[]{:S(2)}) collective-permute-start(bf16[256,512]{1,0:T(8,128)(2,1)S(1)} %add_convert_fusion.6), channel_id=1, source_target_pairs={{0,8},{8,16},{16,24},{24,0},{1,9},{9,17},{17,25},{25,1},{2,10},{10... | collective-permute-start | bytes 786440 | tf_op jit(solution)/shard_map/ppermute | solution.py:20
  96.7 12.4 %collective-permute-start.13 = (bf16[336,512]{1,0:T(8,128)(2,1)S(1)}, bf16[336,512]{1,0:T(8,128)(2,1)S(1)}, u32[]{:S(2)}, u32[]{:S(2)}) collective-permute-start(bf16[336,512]{1,0:T(8,128)(2,1)S(1)} %add_convert_fusion.4), channel_id=1, source_target_pairs={{0,2},{2,4},{4,6},{6,0},{1,3},{3,5},{5,7},{7,1},{8,10},{10,12},{12... | collective-permute-start | bytes 1032200 | tf_op jit(solution)/shard_map/ppermute | solution.py:20
  97.1 12.1 %collective-permute-start.14 = (bf16[336,512]{1,0:T(8,128)(2,1)S(1)}, bf16[336,512]{1,0:T(8,128)(2,1)S(1)}, u32[]{:S(2)}, u32[]{:S(2)}) collective-permute-start(bf16[336,512]{1,0:T(8,128)(2,1)S(1)} %add_convert_fusion.3), channel_id=1, source_target_pairs={{0,6},{2,0},{4,2},{6,4},{1,7},{3,1},{5,3},{7,5},{8,14},{10,8},{12,... | collective-permute-start | bytes 1032200 | tf_op jit(solution)/shard_map/ppermute | solution.py:20
  103.4 9.1 %collective-permute-start.23 = (bf16[336,512]{1,0:T(8,128)(2,1)S(1)}, bf16[336,512]{1,0:T(8,128)(2,1)S(1)}, u32[]{:S(2)}, u32[]{:S(2)}) collective-permute-start(bf16[336,512]{1,0:T(8,128)(2,1)S(1)} %add_convert_fusion.2), channel_id=1, source_target_pairs={{0,8},{8,16},{16,24},{24,0},{1,9},{9,17},{17,25},{25,1},{2,10},{10... | collective-permute-start | bytes 1032200 | tf_op jit(solution)/shard_map/ppermute | solution.py:20
  104.2 8.3 %collective-permute-start.24 = (bf16[336,512]{1,0:T(8,128)(2,1)S(1)}, bf16[336,512]{1,0:T(8,128)(2,1)S(1)}, u32[]{:S(2)}, u32[]{:S(2)}) collective-permute-start(bf16[336,512]{1,0:T(8,128)(2,1)S(1)} %add_convert_fusion.1), channel_id=1, source_target_pairs={{0,24},{8,0},{16,8},{24,16},{1,25},{9,1},{17,9},{25,17},{2,26},{10... | collective-permute-start | bytes 1032200 | tf_op jit(solution)/shard_map/ppermute | solution.py:20
  115.8 12.3 %collective-permute-start.18 = (bf16[296,512]{1,0:T(8,128)(2,1)S(1)}, bf16[296,512]{1,0:T(8,128)(2,1)S(1)}, u32[]{:S(2)}, u32[]{:S(2)}) collective-permute-start(bf16[296,512]{1,0:T(8,128)(2,1)S(1)} %pad_maximum_fusion.3), channel_id=1, source_target_pairs={{0,8},{8,16},{16,24},{24,0},{1,9},{9,17},{17,25},{25,1},{2,10},{10... | collective-permute-start | bytes 909320 | tf_op jit(solution)/shard_map/ppermute | solution.py:20
  115.9 12.2 %collective-permute-start.28 = (bf16[296,512]{1,0:T(8,128)(2,1)S(1)}, bf16[296,512]{1,0:T(8,128)(2,1)S(1)}, u32[]{:S(2)}, u32[]{:S(2)}) collective-permute-start(bf16[296,512]{1,0:T(8,128)(2,1)S(1)} %pad_maximum_fusion.5), channel_id=1, source_target_pairs={{0,2},{2,4},{4,6},{6,0},{1,3},{3,5},{5,7},{7,1},{8,10},{10,12},{12... | collective-permute-start | bytes 909320 | tf_op jit(solution)/shard_map/ppermute | solution.py:20
  (24 other events, 173.5 us)

commit v4 on v3

--- a/solution.py
+++ b/solution.py
@@ -237,6 +237,7 @@
 
 
 CHUNK = 256
+FAR = (2, 1, 3)
 
 
 def tile_step(pieces, projected, key_value_weight, newline_embed):
@@ -253,10 +254,10 @@
     def kernel(*refs):
         piece_refs = refs[:count]
         proj_hbm, weight_hbm, embed_ref = refs[count:count + 3]
-        first_hbm, second_hbm, grad_hbm, normed_hbm = refs[count + 3:count + 7]
-        sends, (products_ref, inverse_ref, line_ref) = refs[count + 7:count + 11], refs[count + 11:count + 14]
+        kept, (grad_hbm, normed_hbm) = refs[count + 3:count + 9], refs[count + 9:count + 11]
+        sends, (products_ref, inverse_ref, line_ref) = refs[count + 11:count + 15], refs[count + 15:count + 18]
         sources, proj_ref, weight_ref, first, second, grad_ref, normed_ref, staged, whole, sems = refs[
-            count + 14:
+            count + 18:
         ]
         copies = Copies(sems)
         arriving = [copies.start(piece_refs[p], sources.at[p]) for p in range(count)]
@@ -278,7 +279,10 @@
                 flipped = value.T
                 first[place] = flipped
                 second[turn] = flipped
-        leaving = [copies.start(first, first_hbm), copies.start(second, second_hbm)]
+        leaving = [
+            copies.start((first, second)[i // 3].at[pl.ds(start, stop - start)], kept[i])
+            for i, (start, stop) in enumerate(CUTS[2:] * 2)
+        ]
         for i in range(deep):
             squares = extra[i:i + 1] + extra[deep + i:deep + i + 1] + extra[2 * deep + i:2 * deep + i + 1]
             inverse_ref[i * wide:(i + 1) * wide] = lax.rsqrt(down(squares) / D + epsilon)
@@ -323,11 +327,10 @@
     outs = step(
         kernel,
         "tile_step",
-        [(piece, ANY) for piece in pieces]
+        [(pieces[0], HBM)] + [(piece, ANY) for piece in pieces[1:]]
         + [(projected, HBM), (key_value_weight, HBM), (newline_embed, VMEM)],
-        [
-            (turned, HBM),
-            (turned, HBM),
+        [(jax.ShapeDtypeStruct((stop - start, width, rows), dtype), HBM) for start, stop in CUTS[2:]] * 2
+        + [
             (grad, HBM),
             (grad, HBM),
         ]
@@ -348,88 +351,47 @@
             VMEM((4, N * width, half), BF),
             VMEM((rows, wide * count), dtype),
         ],
-        count + 9 + share // CHUNK,
-    )
-    return outs[:2], outs[2:4], outs[4:8], outs[8:]
-
-
-def rest(name, sources, rhs):
-    rows, share = rhs.shape
+        count + 13 + share // CHUNK,
+    )
+    return outs[:6], outs[6:8], outs[8:12], outs[12:]
+
+
+def x_rest(features, projected_grad, turned, normed):
+    rows, share = normed.shape
     half = share // 2
+    lefts = list(features) + list(turned)
+    arrays = lefts + [projected_grad, normed]
+    count = len(lefts)
+    tall = [left.size // rows for left in lefts]
+    shapes = [jax.ShapeDtypeStruct((height, half), F32) for height in tall]
 
     def kernel(*refs):
-        source_refs, rhs_hbm, outs = refs[:6], refs[6], refs[7:13]
-        held, rhs_ref, staged, sems = refs[13:19], refs[19], refs[20:22], refs[22]
+        ins, outs = refs[:count + 2], refs[count + 2:2 * count + 2]
+        held, sems = refs[2 * count + 2:-1], refs[-1]
         copies = Copies(sems)
-        arriving = [copies.start(source_refs[i], held[i]) for i in range(6)]
-        copies.start(rhs_hbm, rhs_ref).wait()
-        leaving = []
-        for i in (2, 5, 0, 1, 3, 4):
+        right_sides = [copies.start(ins[count + i], held[count + i]) for i in range(2)]
+        arriving = [copies.start(ins[i], held[i]) for i in range(count)]
+        for i in range(count):
+            which = i // (count // 2)
+            if i % (count // 2) == 0:
+                right_sides[which].wait()
             arriving[i].wait()
-            right = rhs_ref[:, (i // 3) * half:(i // 3 + 1) * half]
-            value = jnp.dot(held[i][...], right, preferred_element_type=F32)
-            if i % 3 == 2:
-                staged[i // 3][...] = value
-                leaving.append(copies.start(staged[i // 3], outs[i]))
-            else:
-                outs[i][...] = value
-        for copy in leaving:
-            copy.wait()
-
-    shapes = [jax.ShapeDtypeStruct((source.shape[0], half), F32) for source in sources]
+            order = (i // 3) % 2
+            right = held[count + which][:, order * half:(order + 1) * half]
+            outs[i][...] = jnp.dot(
+                held[i][...].reshape(tall[i], rows), right, preferred_element_type=F32
+            )
+
     outs = step(
         kernel,
-        name,
-        [(source, HBM) for source in sources] + [(rhs, HBM)],
-        [(shape, HBM if i % 3 == 2 else VMEM) for i, shape in enumerate(shapes)],
-        [VMEM(source.shape, BF) for source in sources]
-        + [VMEM(rhs.shape, BF)]
-        + [VMEM(shapes[i].shape, F32) for i in (2, 5)],
-        9,
-        limit=14,
-    )
-    return outs[:3], outs[3:]
-
-
-def kv_rest(turned, normed):
-    blocks, width, rows = turned[0].shape
-    half = normed.shape[1] // 2
-
-    def kernel(first_hbm, second_hbm, normed_hbm, *refs):
-        outs, (first_ref, second_ref, normed_ref), staged, sems = refs[:6], refs[6:9], refs[9:11], refs[11]
-        copies = Copies(sems)
-        arriving = [
-            copies.start(source.at[pl.ds(start, stop - start)], target.at[pl.ds(start, stop - start)])
-            for source, target in ((first_hbm, first_ref), (second_hbm, second_ref))
-            for start, stop in CUTS[2:]
-        ]
-        copies.start(normed_hbm, normed_ref).wait()
-        leaving = []
-        for i in (2, 5, 0, 1, 3, 4):
-            arriving[i].wait()
-            start, stop = CUTS[2 + i % 3]
-            left = (first_ref, second_ref)[i // 3][start:stop].reshape((stop - start) * width, rows)
-            right = normed_ref[:, (i // 3) * half:(i // 3 + 1) * half]
-            value = jnp.dot(left, right, preferred_element_type=F32)
-            if i % 3 == 2:
-                staged[i // 3][...] = value
-                leaving.append(copies.start(staged[i // 3], outs[i]))
-            else:
-                outs[i][...] = value
-        for copy in leaving:
-            copy.wait()
-
-    shapes = [jax.ShapeDtypeStruct(((stop - start) * width, half), F32) for start, stop in CUTS[2:]] * 2
-    outs = step(
-        kernel,
-        "kv_rest",
-        [(turned[0], HBM), (turned[1], HBM), (normed, HBM)],
-        [(shape, HBM if i % 3 == 2 else VMEM) for i, shape in enumerate(shapes)],
-        [VMEM(turned[0].shape, BF)] * 2 + [VMEM(normed.shape, BF)] + [VMEM(shapes[2].shape, F32)] * 2,
-        9,
-        limit=12,
-    )
-    return outs[:3], outs[3:]
+        "x_rest",
+        [(array, HBM) for array in arrays],
+        [(shape, VMEM) for shape in shapes],
+        [VMEM(array.shape, BF) for array in arrays],
+        count + 2,
+        limit=16,
+    )
+    return outs[:3], outs[3:6], outs[6:9], outs[9:]
 
 
 def x_first(products, grad, projected, inverse, features1, features2):
@@ -437,18 +399,14 @@
     half = share // 2
     size = features1[0].shape[0]
 
-    def kernel(products_ref, grad_hbm, proj_hbm, inverse_ref, *refs):
+    def kernel(products_ref, grad_ref, proj_ref, inverse_ref, *refs):
         features, out_hbm, sends = refs[:4], refs[4], refs[5:9]
-        grad_ref, proj_ref, out, sources, staged, sems = refs[9:]
+        out, staged, sems = refs[9:]
         copies = Copies(sems)
-        ready = [copies.start(grad_hbm, grad_ref), copies.start(proj_hbm, proj_ref)]
-        arriving = [copies.start(features[i], sources.at[i]) for i in range(4)]
         total = jnp.sum(products_ref[...], axis=0)
         total = jnp.concatenate([down(total[i:i + 1]) for i in range(rows // 128)], axis=0)
         inv = inverse_ref[...]
         scale = inv * inv * inv * total / D
-        for copy in ready:
-            copy.wait()
         for i in range(share // 128):
             at = slice(i * 128, (i + 1) * 128)
             out[:, at] = (
@@ -456,9 +414,8 @@
             ).astype(BF)
         leaving = [copies.start(out, out_hbm)]
         for i in range(4):
-            arriving[i].wait()
             right = out[:, (i // 2) * half:(i // 2 + 1) * half]
-            staged[i] = jnp.dot(sources[i], right, preferred_element_type=F32).astype(BF)
+            staged[i] = jnp.dot(features[i][...], right, preferred_element_type=F32).astype(BF)
             leaving.append(copies.start(staged.at[i], sends[i]))
         for copy in leaving:
             copy.wait()
@@ -466,72 +423,41 @@
     outs = step(
         kernel,
         "x_first",
-        [(products, VMEM), (grad, HBM), (projected, HBM), (inverse, VMEM)]
-        + [(cut, HBM) for cut in (features1[0], features1[1], features2[0], features2[1])],
+        [(products, VMEM), (grad, VMEM), (projected, VMEM), (inverse, VMEM)]
+        + [(cut, VMEM) for cut in (features1[0], features1[1], features2[0], features2[1])],
         [(jax.ShapeDtypeStruct((rows, share), BF), HBM)]
         + [(jax.ShapeDtypeStruct((size, half), BF), HBM)] * 4,
         [
             VMEM(grad.shape, BF),
-            VMEM(projected.shape, BF),
-            VMEM(grad.shape, BF),
-            VMEM((4,) + features1[0].shape, BF),
             VMEM((4, size, half), BF),
         ],
-        11,
-        limit=16,
+        5,
+        limit=12,
     )
     return outs[0], outs[1:3], outs[3:5]
 
 
-class Sums:
-    def __init__(self, partials, rows, part):
-        self.partials = partials
-        self.rows, self.part = rows, part
-        self.half, self.down = 2 * rows, rows - part
-
-    def first_b(self, ahead, behind):
-        self.ahead, self.behind = ahead, behind
-        return (
-            (self.partials[0] + ahead[self.half:].astype(F32)).astype(BF),
-            (self.partials[1] + behind[:self.half].astype(F32)).astype(BF),
-        )
-
-    def second_a(self, ahead, behind):
-        half, rows, part = self.half, self.rows, self.part
-        own = self.partials[2]
-        self.low = own[:half] + self.behind[half:].astype(F32) + ahead.astype(F32)
-        self.high = own[half:] + self.ahead[:half].astype(F32) + behind.astype(F32)
-        return (
-            jnp.concatenate([self.low[rows + part:].astype(BF), self.high[:part].astype(BF)], axis=0),
-            self.high[part:rows + part].astype(BF),
-        )
-
-    def second_b(self, ahead, behind):
-        rows, part, down = self.rows, self.part, self.down
-        self.ahead2, self.behind2 = ahead, behind
-        return (
-            (self.low[rows:rows + part] + ahead[down:].astype(F32)).astype(BF),
-            (self.high[rows + part:] + behind[:down].astype(F32)).astype(BF),
-        )
-
-    def result(self, ahead, behind):
-        rows, part, down = self.rows, self.part, self.down
-        return jnp.concatenate(
-            [
-                self.low[:part] + self.behind2[down:].astype(F32) + ahead.astype(F32),
-                self.low[part:rows] + self.ahead2[:down].astype(F32) + behind.astype(F32),
-            ],
-            axis=0,
-        )
-
-
-def both_ways(pair, axis):
-    return shift(pair[0], axis, N, 1), shift(pair[1], axis, N, 3)
-
-
-def packed_both_ways(one, two, axis):
-    moved = both_ways([jnp.concatenate([a, b], axis=0) for a, b in zip(one, two)], axis)
-    return [m[:a.shape[0]] for m, a in zip(moved, one)], [m[a.shape[0]:] for m, a in zip(moved, one)]
+def ring_sends(partials, ahead, behind):
+    near, far, _ = partials
+    half = near.shape[0]
+    return (
+        (near + ahead[half:].astype(F32)).astype(BF),
+        (far + behind[:half].astype(F32)).astype(BF),
+    )
+
+
+def ring_blocks(partials, ahead, behind, ahead2, behind2):
+    own = partials[2]
+    half = own.shape[0] // 2
+    low = own[:half] + behind[half:].astype(F32) + ahead2.astype(F32)
+    high = own[half:] + ahead[:half].astype(F32) + behind2.astype(F32)
+    size = half // 2
+    return low[:size], low[size:], high[:size], high[size:]
+
+
+def straight(blocks, axis):
+    arrived = [shift(blocks[d].astype(BF), axis, N, d).astype(F32) for d in FAR]
+    return blocks[0] + arrived[0] + arrived[1] + arrived[2]
 
 
 def local(
@@ -610,37 +536,39 @@
     )
     line_total = jnp.broadcast_to(line_total, (kv_rows, kv_rows)).T
 
+    newline_embed, line_total = lax.optimization_barrier((newline_embed, line_total))
     turned, (normed_grad, normed), kv_sends, (products, inverse, line_normed) = tile_step(
         pieces, projected, key_value_weight, newline_embed.reshape(1, share)
     )
     products = lax.all_to_all(products, ("ylo", "core", "yhi"), split_axis=0, concat_axis=0, tiled=True)
 
-    in0, in1 = both_ways(kv_sends[:2], "x"), both_ways(kv_sends[2:], "z")
-    kv_parts0, kv_parts1 = kv_rest(turned, normed)
-    kv0 = Sums(kv_parts0, kv_rows, kv_rows // 2)
-    kv1 = Sums(kv_parts1, kv_rows, kv_rows // 2)
-    out0, out1 = kv0.first_b(*in0), kv1.first_b(*in1)
-
+    def both_ways(pair, axis):
+        return shift(pair[0], axis, N, 1), shift(pair[1], axis, N, 3)
+
+    kv_in = [both_ways(kv_sends[:2], "x"), both_ways(kv_sends[2:], "z")]
     projected_grad, x_send0, x_send1 = x_first(
         products, normed_grad, projected, inverse, features1, features2
     )
-    x_in0, x_in1 = both_ways(x_send0, "x"), both_ways(x_send1, "z")
-    out0, out1, projected_grad = lax.optimization_barrier((out0, out1, projected_grad))
-    in0, in1 = both_ways(out0, "x"), both_ways(out1, "z")
-    kv_out0, kv_out1 = kv0.second_a(*in0), kv1.second_a(*in1)
-    in0, in1 = x_in0, x_in1
-    x_parts0, x_parts1 = rest("x_rest", list(features1[2:]) + list(features2[2:]), projected_grad)
-    part = (x_rows // 2 + 7) // 8 * 8
-    x0 = Sums(x_parts0, x_rows, part)
-    x1 = Sums(x_parts1, x_rows, part)
-    in0, in1 = both_ways(x0.first_b(*in0), "x"), both_ways(x1.first_b(*in1), "z")
-    in0, kv_in0 = packed_both_ways(x0.second_a(*in0), kv_out0, "z")
-    in1, kv_in1 = packed_both_ways(x1.second_a(*in1), kv_out1, "x")
-    in0, kv_in0 = packed_both_ways(x0.second_b(*in0), kv0.second_b(*kv_in0), "z")
-    in1, kv_in1 = packed_both_ways(x1.second_b(*in1), kv1.second_b(*kv_in1), "x")
-    kv_result = jnp.concatenate([kv0.result(*kv_in0), kv1.result(*kv_in1)], axis=1)
+    x_in = [both_ways(x_send0, "x"), both_ways(x_send1, "z")]
+    kv_in, projected_grad = lax.optimization_barrier((kv_in, projected_grad))
+    parts = x_rest(list(features1[2:]) + list(features2[2:]), projected_grad, turned, normed)
+    results = []
+    for i, (first, second) in enumerate((("x", "z"), ("z", "x"))):
+        x_parts, kv_parts = parts[i], parts[2 + i]
+        sends = [
+            jnp.concatenate(pair, axis=0)
+            for pair in zip(ring_sends(x_parts, *x_in[i]), ring_sends(kv_parts, *kv_in[i]))
+        ]
+        ahead, behind = both_ways(sends, first)
+        size = x_parts[0].shape[0]
+        x_blocks = ring_blocks(x_parts, *x_in[i], ahead[:size], behind[:size])
+        kv_blocks = ring_blocks(kv_parts, *kv_in[i], ahead[size:], behind[size:])
+        results.append(
+            straight([jnp.concatenate(pair, axis=0) for pair in zip(x_blocks, kv_blocks)], second)
+        )
+    result = jnp.concatenate(results, axis=1)
+    x_result, kv_result = result[:x_rows], result[x_rows:]
     kv_result = kv_result + line_total[:, :1] * line_normed
-    x_result = jnp.concatenate([x0.result(*in0), x1.result(*in1)], axis=1)
     return x_result[:sig_rows], x_result[sig_rows:], kv_result
 
 

time: 142 us -> 137 us (0.965); the launches traced: 140 us -> 137 us
  starting transfers between devices: 55 us -> 39.3 us
  waiting for transfers between devices: 33.4 us -> 44.8 us
  blocking collectives: 0 us -> 9 us
  Pallas kernels: 30.4 us -> 26 us
  other arithmetic: 9.43 us -> 5.6 us
    ppermute x28 -> x22, starting transfers between devices: 38.2 us -> 26 us  [shift(): lax.ppermute(value, axis, [(i, (i + step) % size) for i in range(size)])]
    ppermute x28 -> x22, waiting for transfers between devices: 22.6 us -> 33.8 us  [shift(): lax.ppermute(value, axis, [(i, (i + step) % size) for i in range(size)])]
    all_to_all x0 -> x1, blocking collectives: none -> 9 us  [local(): lax.all_to_all(products, ('ylo', 'core', 'yhi'), split_axis=0, concat_axi...]
    pallas_call x4 -> x3, Pallas kernels: 21.2 us -> 16.7 us  [step(): pl.pallas_call(kernel, out_shape=[space(shape.shape, shape.dtype) for sha...]
    all_to_all x1 -> x0, starting transfers between devices: 3.53 us -> none  [local(): lax.all_to_all(products, ('ylo', 'core', 'yhi'), split_axis=0, concat_axi...]
    convert_element_type x14 -> x8, other arithmetic: 3.71 us -> 0.79 us  [the longest x4 0.4 us: ring_sends(): (far + behind[:half].astype(F32)).astype(BF)]
  transfers between devices with their start and end apart: 33 -> 26, of which waited for: 14 -> 11; matrix products, arithmetic and copies ran while one was open for 12% -> 9% of each run, Pallas kernels for 12% -> 9%
where the time goes in v4:
time: 137 us
  waiting for transfers between devices  44.8 us (33%)
  starting transfers between devices  39.3 us (29%)
  Pallas kernels  26 us (19%)
  blocking collectives  9 us (7%)
  matrix products  6.68 us (5%)
  other arithmetic  5.6 us (4%)
  local copies, waits for them, and re-layouts  4.42 us (3%)
    ppermute x22, waiting for transfers between devices, shift(): lax.ppermute(value, axis, [(i, (i + step) % size) for i in range(size)])  33.8 us
    ppermute x22, starting transfers between devices, shift(): lax.ppermute(value, axis, [(i, (i + step) % size) for i in range(size)])  26 us
    pallas_call x3, Pallas kernels, step(): pl.pallas_call(kernel, out_shape=[space(shape.shape, shape.dtype) for sha...  16.7 us
    ppermute x3, waiting for transfers between devices, shift_y(): lax.ppermute(value, Y, [(place(y), place((y + step) % N)) for y in range(...  9.37 us
    all_to_all x1, blocking collectives, local(): lax.all_to_all(products, ('ylo', 'core', 'yhi'), split_axis=0, concat_axi...  9 us
    all_to_all x1, starting transfers between devices, local(): lax.all_to_all(outgoing, DP, split_axis=0, concat_axis=0, tiled=True)  8.02 us
    ppermute x3, starting transfers between devices, shift_y(): lax.ppermute(value, Y, [(place(y), place((y + step) % N)) for y in range(...  5.3 us
    dot_general x1, matrix products, local(): jnp.dot(siglip_features, siglip_projection, preferred_element_type=F32)  3.66 us
  transfers between devices with their start and end apart: 26, of which 11 were waited for; matrix products, arithmetic and copies ran while one was open for 9% of the time, Pallas kernels for 9%

profile of v4, /device:TPU:0, one launch (start us, length us, event | category | flops | bytes accessed | tf_op | source)
XLA Modules:
  0.0 136.9 jit_solution(13485078547326892063)
XLA Ops:
  0.6 2.7 %slices_out.1 = bf16[16,80,256]{2,1,0:T(8,128)(2,1)} custom-call(bf16[1024,2048]{1,0:T(8,128)(2,1)} %source.1, bf16[32,2048]{1,0:T(8,128)(2,1)} %lines.1), custom_call_target="tpu_custom_call" | custom-call | tf_op jit(solution)/shard_map/slices_out/pallas_call | solution.py:85
  3.4 8.0 %all-to-all-start = ((bf16[16,80,256]{2,1,0:T(8,128)(2,1)}), bf16[16,80,256]{2,1,0:T(8,128)(2,1)}, u32[]{:S(2)}, u32[]{:S(2)}) async-start(bf16[16,80,256]{2,1,0:T(8,128)(2,1)} %slices_out.1), calls=%async_computation | async-start | bytes 1310720 | tf_op jit(solution)/shard_map/all_to_all | solution.py:490
  11.4 3.7 %fusion.21 = f32[512,1024]{1,0:T(8,128)S(1)} fusion(bf16[512,1152]{1,0:T(8,128)(2,1)} %siglip_ref.1, bf16[1152,1024]{1,0:T(8,128)(2,1)} %param.12), kind=kOutput, calls=%fused_computation.82 | convolution fusion | flops 1207959552 | bytes 5636096 | tf_op jit(solution)/shard_map/dot_general | solution.py:493
  15.1 2.8 %multiply_reduce_fusion = (f32[512]{0:T(512)S(1)}, bf16[512,1024]{1,0:T(8,128)(2,1)}) fusion(f32[512,1024]{1,0:T(8,128)S(1)} %fusion.21, bf16[512,1536]{1,0:T(8,128)(2,1)S(1)} %copy-done.3, bf16[1536,1024]{1,0:T(8,128)(2,1)S(1)} %copy-done), kind=kOutput, calls=%fused_computation | convolution fusion | flops 1613233664 | bytes 7866368 | tf_op jit(solution)/shard_map/dot_general | solution.py:494
  17.9 3.4 %turn_features.1 = (bf16[672,512]{1,0:T(8,128)(2,1)}, bf16[672,512]{1,0:T(8,128)(2,1)}, bf16[336,512]{1,0:T(8,128)(2,1)}, bf16[336,512]{1,0:T(8,128)(2,1)}, bf16...) custom-call(bf16[512,1152]{1,0:T(8,128)(2,1)S(1)} %copy-done.4, ...), custom_call_target="tpu_custom_call" | custom-call | tf_op jit(solution)/shard_map/turn_features/pallas_call | solution.py:142
  24.4 3.1 %pick_tiles.1.refs_0_ = bf16[528,256]{1,0:T(8,128)(2,1)} custom-call(s32[16]{0:T(128)} %dynamic-slice_bitcast_fusion.dest_ref, bf16[16,80,256]{2,1,0:T(8,128)(2,1)} %all-to-all-done.source, bf16[16,256]{1,0:T(8,128)(2,1)} %pad.5.extra_ref), custom_call_target="tpu_custom_call" | custom-call | tf_op jit(solution)/shard_map/pick_tiles/pallas_call | solution.py:189
  27.6 3.3 %collective-permute-start.2 = (bf16[528,256]{1,0:T(8,128)(2,1)}, bf16[528,256]{1,0:T(8,128)(2,1)S(1)}, u32[]{:S(2)}, u32[]{:S(2)}) collective-permute-start(bf16[528,256]{1,0:T(8,128)(2,1)} %pick_tiles.1.refs_0_), channel_id=1, source_target_pairs={{0,1},{64,65},{1,0},{65,64},{2,3},{66,67},{3,2},{67,66},{4,5},{68,... | collective-permute-start | bytes 811016 | tf_op jit(solution)/shard_map/ppermute | solution.py:25
  35.0 3.7 %collective-permute-done.2.refs_3_ = bf16[528,256]{1,0:T(8,128)(2,1)S(1)} collective-permute-done((bf16[528,256]{1,0:T(8,128)(2,1)}, bf16[528,256]{1,0:T(8,128)(2,1)S(1)}, u32[]{:S(2)}, u32[]{:S(2)}) %collective-permute-start.2) | collective-permute-done | bytes 270368 | tf_op jit(solution)/shard_map/ppermute | solution.py:25
  38.7 5.7 %collective-permute-done.1.refs_2_ = bf16[528,256]{1,0:T(8,128)(2,1)S(1)} collective-permute-done((bf16[528,256]{1,0:T(8,128)(2,1)}, bf16[528,256]{1,0:T(8,128)(2,1)S(1)}, u32[]{:S(2)}, u32[]{:S(2)}) %collective-permute-start.1) | collective-permute-done | bytes 270368 | tf_op jit(solution)/shard_map/ppermute | solution.py:25
  46.3 7.6 %tile_step.1 = (bf16[2,128,512]{2,1,0:T(8,128)(2,1)}, bf16[2,128,512]{2,1,0:T(8,128)(2,1)}, bf16[4,128,512]{2,1,0:T(8,128)(2,1)}, bf16[2,128,512]{2,1,0:T(8,128)...) custom-call(bf16[528,256]{1,0:T(8,128)(2,1)} %pick_tiles.1.refs_0_, ...), custom_call_target="tpu_custom_call" | custom-call | tf_op jit(solution)/shard_map/tile_step/pallas_call | solution.py:207
  54.7 2.7 %collective-permute-start.8 = (bf16[512,512]{1,0:T(8,128)(2,1)}, bf16[512,512]{1,0:T(8,128)(2,1)S(1)}, u32[]{:S(2)}, u32[]{:S(2)}) collective-permute-start(bf16[512,512]{1,0:T(8,128)(2,1)} %get-tuple-element.98), channel_id=1, source_target_pairs={{0,6},{2,0},{4,2},{6,4},{1,7},{3,1},{5,3},{7,5},{8,14},{10,8},{12,... | collective-permute-start | bytes 1572872 | tf_op jit(solution)/shard_map/ppermute | solution.py:20
  57.6 3.0 %collective-permute-start.10 = (bf16[512,512]{1,0:T(8,128)(2,1)}, bf16[512,512]{1,0:T(8,128)(2,1)S(1)}, u32[]{:S(2)}, u32[]{:S(2)}) collective-permute-start(bf16[512,512]{1,0:T(8,128)(2,1)} %get-tuple-element.100), channel_id=1, source_target_pairs={{0,24},{8,0},{16,8},{24,16},{1,25},{9,1},{17,9},{25,17},{2,26},{10... | collective-permute-start | bytes 1572872 | tf_op jit(solution)/shard_map/ppermute | solution.py:20
  60.6 9.0 %all_to_all.10.products_ref = f32[8,8,128]{2,1,0:T(8,128)S(1)} all-to-all(f32[8,8,128]{2,1,0:T(8,128)S(1)} %get-tuple-element.101), channel_id=1, replica_groups=mesh['ylo'=2,'core'=2,'z'=4,'x'=4,'yhi'=2] {'ylo','core','yhi'}, dimensions={0} | all-to-all | bytes 65536 | tf_op jit(solution)/shard_map/all_to_all | solution.py:543
  70.9 2.9 %x_first.1 = (bf16[512,1024]{1,0:T(8,128)(2,1)}, bf16[672,512]{1,0:T(8,128)(2,1)}, bf16[672,512]{1,0:T(8,128)(2,1)}, bf16[672,512]{1,0:T(8,128)(2,1)}, bf16[672,512]{1,0:T(8,128)(2,1)}) custom-call(f32[8,8,128]{2,1,0:T(8,128)S(1)} %all_to_all.10.products_ref, bf16[512,1024]{1,0:T(8,128)(2,1)S(1)} %copy-done.5, bf16[512,1024]{1,0:T(8,128)(2,1)S(1)} %copy-done.2, ...), custom_call_target="tpu_custom_call" | custom-call | tf_op jit(solution)/shard_map/x_first/pallas_call | solution.py:207
  74.1 1.8 %collective-permute-start.12 = (bf16[672,512]{1,0:T(8,128)(2,1)}, bf16[672,512]{1,0:T(8,128)(2,1)S(1)}, u32[]{:S(2)}, u32[]{:S(2)}) collective-permute-start(bf16[672,512]{1,0:T(8,128)(2,1)} %get-tuple-element.114), channel_id=1, source_target_pairs={{0,2},{2,4},{4,6},{6,0},{1,3},{3,5},{5,7},{7,1},{8,10},{10,12},{12... | collective-permute-start | bytes 2064392 | tf_op jit(solution)/shard_map/ppermute | solution.py:20
  77.9 6.3 %x_rest.1 = (f32[336,512]{1,0:T(8,128)S(1)}, f32[336,512]{1,0:T(8,128)S(1)}, f32[672,512]{1,0:T(8,128)S(1)}, f32[336,512]{1,0:T(8,128)S(1)}, f32[336,512]{1,0:T(...) custom-call(bf16[336,512]{1,0:T(8,128)(2,1)} %get-tuple-element.78.r, ...), custom_call_target="tpu_custom_call" | custom-call | tf_op jit(solution)/shard_map/x_rest/pallas_call | solution.py:207
  84.5 8.5 %collective-permute-done.18 = bf16[672,512]{1,0:T(8,128)(2,1)S(1)} collective-permute-done((bf16[672,512]{1,0:T(8,128)(2,1)}, bf16[672,512]{1,0:T(8,128)(2,1)S(1)}, u32[]{:S(2)}, u32[]{:S(2)}) %collective-permute-start.18) | collective-permute-done | bytes 688160 | tf_op jit(solution)/shard_map/ppermute | solution.py:20
  95.7 2.2 %collective-permute-start.14 = (bf16[592,512]{1,0:T(8,128)(2,1)S(1)}, bf16[592,512]{1,0:T(8,128)(2,1)S(1)}, u32[]{:S(2)}, u32[]{:S(2)}) collective-permute-start(bf16[592,512]{1,0:T(8,128)(2,1)S(1)} %pad_maximum_fusion.1), channel_id=1, source_target_pairs={{0,6},{2,0},{4,2},{6,4},{1,7},{3,1},{5,3},{7,5},{8,14},{10,8},{12,... | collective-permute-start | bytes 1818632 | tf_op jit(solution)/shard_map/ppermute | solution.py:20
  98.1 9.4 %collective-permute-done.21 = bf16[592,512]{1,0:T(8,128)(2,1)S(1)} collective-permute-done((bf16[592,512]{1,0:T(8,128)(2,1)S(1)}, bf16[592,512]{1,0:T(8,128)(2,1)S(1)}, u32[]{:S(2)}, u32[]{:S(2)}) %collective-permute-start.21) | collective-permute-done | bytes 606240 | tf_op jit(solution)/shard_map/ppermute | solution.py:20
  107.5 2.7 %collective-permute-done.20 = bf16[592,512]{1,0:T(8,128)(2,1)S(1)} collective-permute-done((bf16[592,512]{1,0:T(8,128)(2,1)S(1)}, bf16[592,512]{1,0:T(8,128)(2,1)S(1)}, u32[]{:S(2)}, u32[]{:S(2)}) %collective-permute-start.20) | collective-permute-done | bytes 606240 | tf_op jit(solution)/shard_map/ppermute | solution.py:20
  111.4 2.8 %collective-permute-start.24 = (bf16[296,512]{1,0:T(8,128)(2,1)S(1)}, bf16[296,512]{1,0:T(8,128)(2,1)S(1)}, u32[]{:S(2)}, u32[]{:S(2)}) collective-permute-start(bf16[296,512]{1,0:T(8,128)(2,1)S(1)} %pad_maximum_fusion.11), channel_id=1, source_target_pairs={{0,6},{2,0},{4,2},{6,4},{1,7},{3,1},{5,3},{7,5},{8,14},{10,8},{12,... | collective-permute-start | bytes 909320 | tf_op jit(solution)/shard_map/ppermute | solution.py:20
  116.0 4.3 %collective-permute-start.17 = (bf16[296,512]{1,0:T(8,128)(2,1)S(1)}, bf16[296,512]{1,0:T(8,128)(2,1)S(1)}, u32[]{:S(2)}, u32[]{:S(2)}) collective-permute-start(bf16[296,512]{1,0:T(8,128)(2,1)S(1)} %pad_maximum_fusion.8), channel_id=1, source_target_pairs={{0,24},{8,0},{16,8},{24,16},{1,25},{9,1},{17,9},{25,17},{2,26},{10... | collective-permute-start | bytes 909320 | tf_op jit(solution)/shard_map/ppermute | solution.py:20
  120.4 5.6 %collective-permute-done.23 = bf16[296,512]{1,0:T(8,128)(2,1)S(1)} collective-permute-done((bf16[296,512]{1,0:T(8,128)(2,1)S(1)}, bf16[296,512]{1,0:T(8,128)(2,1)S(1)}, u32[]{:S(2)}, u32[]{:S(2)}) %collective-permute-start.23) | collective-permute-done | bytes 303136 | tf_op jit(solution)/shard_map/ppermute | solution.py:20
  128.3 6.0 %collective-permute-done.15 = bf16[296,512]{1,0:T(8,128)(2,1)S(1)} collective-permute-done((bf16[296,512]{1,0:T(8,128)(2,1)S(1)}, bf16[296,512]{1,0:T(8,128)(2,1)S(1)}, u32[]{:S(2)}, u32[]{:S(2)}) %collective-permute-start.15) | collective-permute-done | bytes 303136 | tf_op jit(solution)/shard_map/ppermute | solution.py:20
  (129 shorter events, 24.7 us)
Async XLA Ops:
  3.4 21.0 %all-to-all-start = ((bf16[16,80,256]{2,1,0:T(8,128)(2,1)}), bf16[16,80,256]{2,1,0:T(8,128)(2,1)}, u32[]{:S(2)}, u32[]{:S(2)}) async-start(bf16[16,80,256]{2,1,0:T(8,128)(2,1)} %slices_out.1), calls=%async_computation | async-start | bytes 1310720 | tf_op jit(solution)/shard_map/all_to_all | solution.py:490
  27.5 17.8 %collective-permute-start.3 = (bf16[528,256]{1,0:T(8,128)(2,1)}, bf16[528,256]{1,0:T(8,128)(2,1)S(1)}, u32[]{:S(2)}, u32[]{:S(2)}) collective-permute-start(bf16[528,256]{1,0:T(8,128)(2,1)} %pick_tiles.1.refs_0_), channel_id=1, source_target_pairs={{0,32},{32,0},{1,33},{33,1},{2,34},{34,2},{3,35},{35,3},{4,36},{36... | collective-permute-start | bytes 811016 | tf_op jit(solution)/shard_map/ppermute | solution.py:20
  27.6 11.1 %collective-permute-start.2 = (bf16[528,256]{1,0:T(8,128)(2,1)}, bf16[528,256]{1,0:T(8,128)(2,1)S(1)}, u32[]{:S(2)}, u32[]{:S(2)}) collective-permute-start(bf16[528,256]{1,0:T(8,128)(2,1)} %pick_tiles.1.refs_0_), channel_id=1, source_target_pairs={{0,1},{64,65},{1,0},{65,64},{2,3},{66,67},{3,2},{67,66},{4,5},{68,... | collective-permute-start | bytes 811016 | tf_op jit(solution)/shard_map/ppermute | solution.py:25
  30.9 13.5 %collective-permute-start.1 = (bf16[528,256]{1,0:T(8,128)(2,1)}, bf16[528,256]{1,0:T(8,128)(2,1)S(1)}, u32[]{:S(2)}, u32[]{:S(2)}) collective-permute-start(bf16[528,256]{1,0:T(8,128)(2,1)} %pick_tiles.1.refs_0_), channel_id=1, source_target_pairs={{0,65},{64,0},{1,64},{65,1},{2,67},{66,2},{3,66},{67,3},{4,69},{68... | collective-permute-start | bytes 811016 | tf_op jit(solution)/shard_map/ppermute | solution.py:25
  31.9 12.5 %collective-permute-start = (bf16[528,256]{1,0:T(8,128)(2,1)}, bf16[528,256]{1,0:T(8,128)(2,1)S(1)}, u32[]{:S(2)}, u32[]{:S(2)}) collective-permute-start(bf16[528,256]{1,0:T(8,128)(2,1)} %pick_tiles.1.refs_0_), channel_id=1, source_target_pairs={{0,64},{64,1},{1,65},{65,0},{2,66},{66,3},{3,67},{67,2},{4,68},{68... | collective-permute-start | bytes 811016 | tf_op jit(solution)/shard_map/ppermute | solution.py:25
  38.7 6.6 %collective-permute-start.6 = (bf16[528,256]{1,0:T(8,128)(2,1)S(1)}, bf16[528,256]{1,0:T(8,128)(2,1)S(1)}, u32[]{:S(2)}, u32[]{:S(2)}) collective-permute-start(bf16[528,256]{1,0:T(8,128)(2,1)S(1)} %collective-permute-done.2.refs_3_), channel_id=1, source_target_pairs={{0,32},{32,0},{1,33},{33,1},{2,34},{34,2},{3,35},{35,3},{4,36},{36... | collective-permute-start | bytes 811016 | tf_op jit(solution)/shard_map/ppermute | solution.py:20
  53.9 20.2 %collective-permute-start.7 = (bf16[512,512]{1,0:T(8,128)(2,1)}, bf16[512,512]{1,0:T(8,128)(2,1)S(1)}, u32[]{:S(2)}, u32[]{:S(2)}) collective-permute-start(bf16[512,512]{1,0:T(8,128)(2,1)} %get-tuple-element.97), channel_id=1, source_target_pairs={{0,2},{2,4},{4,6},{6,0},{1,3},{3,5},{5,7},{7,1},{8,10},{10,12},{12... | collective-permute-start | bytes 1572872 | tf_op jit(solution)/shard_map/ppermute | solution.py:20
  54.7 21.2 %collective-permute-start.8 = (bf16[512,512]{1,0:T(8,128)(2,1)}, bf16[512,512]{1,0:T(8,128)(2,1)S(1)}, u32[]{:S(2)}, u32[]{:S(2)}) collective-permute-start(bf16[512,512]{1,0:T(8,128)(2,1)} %get-tuple-element.98), channel_id=1, source_target_pairs={{0,6},{2,0},{4,2},{6,4},{1,7},{3,1},{5,3},{7,5},{8,14},{10,8},{12,... | collective-permute-start | bytes 1572872 | tf_op jit(solution)/shard_map/ppermute | solution.py:20
  57.4 18.8 %collective-permute-start.9 = (bf16[512,512]{1,0:T(8,128)(2,1)}, bf16[512,512]{1,0:T(8,128)(2,1)S(1)}, u32[]{:S(2)}, u32[]{:S(2)}) collective-permute-start(bf16[512,512]{1,0:T(8,128)(2,1)} %get-tuple-element.99), channel_id=1, source_target_pairs={{0,8},{8,16},{16,24},{24,0},{1,9},{9,17},{17,25},{25,1},{2,10},{10... | collective-permute-start | bytes 1572872 | tf_op jit(solution)/shard_map/ppermute | solution.py:20
  57.6 20.3 %collective-permute-start.10 = (bf16[512,512]{1,0:T(8,128)(2,1)}, bf16[512,512]{1,0:T(8,128)(2,1)S(1)}, u32[]{:S(2)}, u32[]{:S(2)}) collective-permute-start(bf16[512,512]{1,0:T(8,128)(2,1)} %get-tuple-element.100), channel_id=1, source_target_pairs={{0,24},{8,0},{16,8},{24,16},{1,25},{9,1},{17,9},{25,17},{2,26},{10... | collective-permute-start | bytes 1572872 | tf_op jit(solution)/shard_map/ppermute | solution.py:20
  73.8 21.7 %collective-permute-start.11 = (bf16[672,512]{1,0:T(8,128)(2,1)}, bf16[672,512]{1,0:T(8,128)(2,1)S(1)}, u32[]{:S(2)}, u32[]{:S(2)}) collective-permute-start(bf16[672,512]{1,0:T(8,128)(2,1)} %get-tuple-element.112), channel_id=1, source_target_pairs={{0,6},{2,0},{4,2},{6,4},{1,7},{3,1},{5,3},{7,5},{8,14},{10,8},{12,... | collective-permute-start | bytes 2064392 | tf_op jit(solution)/shard_map/ppermute | solution.py:20
  74.1 23.8 %collective-permute-start.12 = (bf16[672,512]{1,0:T(8,128)(2,1)}, bf16[672,512]{1,0:T(8,128)(2,1)S(1)}, u32[]{:S(2)}, u32[]{:S(2)}) collective-permute-start(bf16[672,512]{1,0:T(8,128)(2,1)} %get-tuple-element.114), channel_id=1, source_target_pairs={{0,2},{2,4},{4,6},{6,0},{1,3},{3,5},{5,7},{7,1},{8,10},{10,12},{12... | collective-permute-start | bytes 2064392 | tf_op jit(solution)/shard_map/ppermute | solution.py:20
  75.9 17.1 %collective-permute-start.18 = (bf16[672,512]{1,0:T(8,128)(2,1)}, bf16[672,512]{1,0:T(8,128)(2,1)S(1)}, u32[]{:S(2)}, u32[]{:S(2)}) collective-permute-start(bf16[672,512]{1,0:T(8,128)(2,1)} %get-tuple-element.122), channel_id=1, source_target_pairs={{0,24},{8,0},{16,8},{24,16},{1,25},{9,1},{17,9},{25,17},{2,26},{10... | collective-permute-start | bytes 2064392 | tf_op jit(solution)/shard_map/ppermute | solution.py:20
  76.1 18.6 %collective-permute-start.19 = (bf16[672,512]{1,0:T(8,128)(2,1)}, bf16[672,512]{1,0:T(8,128)(2,1)S(1)}, u32[]{:S(2)}, u32[]{:S(2)}) collective-permute-start(bf16[672,512]{1,0:T(8,128)(2,1)} %get-tuple-element.124), channel_id=1, source_target_pairs={{0,8},{8,16},{16,24},{24,0},{1,9},{9,17},{17,25},{25,1},{2,10},{10... | collective-permute-start | bytes 2064392 | tf_op jit(solution)/shard_map/ppermute | solution.py:20
  93.2 14.3 %collective-permute-start.21 = (bf16[592,512]{1,0:T(8,128)(2,1)S(1)}, bf16[592,512]{1,0:T(8,128)(2,1)S(1)}, u32[]{:S(2)}, u32[]{:S(2)}) collective-permute-start(bf16[592,512]{1,0:T(8,128)(2,1)S(1)} %pad_maximum_fusion.3), channel_id=1, source_target_pairs={{0,24},{8,0},{16,8},{24,16},{1,25},{9,1},{17,9},{25,17},{2,26},{10... | collective-permute-start | bytes 1818632 | tf_op jit(solution)/shard_map/ppermute | solution.py:20
  94.9 15.3 %collective-permute-start.20 = (bf16[592,512]{1,0:T(8,128)(2,1)S(1)}, bf16[592,512]{1,0:T(8,128)(2,1)S(1)}, u32[]{:S(2)}, u32[]{:S(2)}) collective-permute-start(bf16[592,512]{1,0:T(8,128)(2,1)S(1)} %pad_maximum_fusion.2), channel_id=1, source_target_pairs={{0,8},{8,16},{16,24},{24,0},{1,9},{9,17},{17,25},{25,1},{2,10},{10... | collective-permute-start | bytes 1818632 | tf_op jit(solution)/shard_map/ppermute | solution.py:20
  95.7 19.5 %collective-permute-start.14 = (bf16[592,512]{1,0:T(8,128)(2,1)S(1)}, bf16[592,512]{1,0:T(8,128)(2,1)S(1)}, u32[]{:S(2)}, u32[]{:S(2)}) collective-permute-start(bf16[592,512]{1,0:T(8,128)(2,1)S(1)} %pad_maximum_fusion.1), channel_id=1, source_target_pairs={{0,6},{2,0},{4,2},{6,4},{1,7},{3,1},{5,3},{7,5},{8,14},{10,8},{12,... | collective-permute-start | bytes 1818632 | tf_op jit(solution)/shard_map/ppermute | solution.py:20
  98.0 17.1 %collective-permute-start.13 = (bf16[592,512]{1,0:T(8,128)(2,1)S(1)}, bf16[592,512]{1,0:T(8,128)(2,1)S(1)}, u32[]{:S(2)}, u32[]{:S(2)}) collective-permute-start(bf16[592,512]{1,0:T(8,128)(2,1)S(1)} %pad_maximum_fusion), channel_id=1, source_target_pairs={{0,2},{2,4},{4,6},{6,0},{1,3},{3,5},{5,7},{7,1},{8,10},{10,12},{12... | collective-permute-start | bytes 1818632 | tf_op jit(solution)/shard_map/ppermute | solution.py:20
  110.8 15.2 %collective-permute-start.23 = (bf16[296,512]{1,0:T(8,128)(2,1)S(1)}, bf16[296,512]{1,0:T(8,128)(2,1)S(1)}, u32[]{:S(2)}, u32[]{:S(2)}) collective-permute-start(bf16[296,512]{1,0:T(8,128)(2,1)S(1)} %pad_maximum_fusion.10), channel_id=1, source_target_pairs={{0,2},{2,4},{4,6},{6,0},{1,3},{3,5},{5,7},{7,1},{8,10},{10,12},{12... | collective-permute-start | bytes 909320 | tf_op jit(solution)/shard_map/ppermute | solution.py:20
  111.4 16.1 %collective-permute-start.24 = (bf16[296,512]{1,0:T(8,128)(2,1)S(1)}, bf16[296,512]{1,0:T(8,128)(2,1)S(1)}, u32[]{:S(2)}, u32[]{:S(2)}) collective-permute-start(bf16[296,512]{1,0:T(8,128)(2,1)S(1)} %pad_maximum_fusion.11), channel_id=1, source_target_pairs={{0,6},{2,0},{4,2},{6,4},{1,7},{3,1},{5,3},{7,5},{8,14},{10,8},{12,... | collective-permute-start | bytes 909320 | tf_op jit(solution)/shard_map/ppermute | solution.py:20
  114.3 13.3 %collective-permute-start.22 = (bf16[296,512]{1,0:T(8,128)(2,1)S(1)}, bf16[296,512]{1,0:T(8,128)(2,1)S(1)}, u32[]{:S(2)}, u32[]{:S(2)}) collective-permute-start(bf16[296,512]{1,0:T(8,128)(2,1)S(1)} %pad_maximum_fusion.9), channel_id=1, source_target_pairs={{0,4},{2,6},{4,0},{6,2},{1,5},{3,7},{5,1},{7,3},{8,12},{10,14},{12... | collective-permute-start | bytes 909320 | tf_op jit(solution)/shard_map/ppermute | solution.py:20
  115.9 12.4 %collective-permute-start.16 = (bf16[296,512]{1,0:T(8,128)(2,1)S(1)}, bf16[296,512]{1,0:T(8,128)(2,1)S(1)}, u32[]{:S(2)}, u32[]{:S(2)}) collective-permute-start(bf16[296,512]{1,0:T(8,128)(2,1)S(1)} %pad_maximum_fusion.7), channel_id=1, source_target_pairs={{0,8},{8,16},{16,24},{24,0},{1,9},{9,17},{17,25},{25,1},{2,10},{10... | collective-permute-start | bytes 909320 | tf_op jit(solution)/shard_map/ppermute | solution.py:20
  116.0 12.3 %collective-permute-start.17 = (bf16[296,512]{1,0:T(8,128)(2,1)S(1)}, bf16[296,512]{1,0:T(8,128)(2,1)S(1)}, u32[]{:S(2)}, u32[]{:S(2)}) collective-permute-start(bf16[296,512]{1,0:T(8,128)(2,1)S(1)} %pad_maximum_fusion.8), channel_id=1, source_target_pairs={{0,24},{8,0},{16,8},{24,16},{1,25},{9,1},{17,9},{25,17},{2,26},{10... | collective-permute-start | bytes 909320 | tf_op jit(solution)/shard_map/ppermute | solution.py:20
  126.0 8.3 %collective-permute-start.15 = (bf16[296,512]{1,0:T(8,128)(2,1)S(1)}, bf16[296,512]{1,0:T(8,128)(2,1)S(1)}, u32[]{:S(2)}, u32[]{:S(2)}) collective-permute-start(bf16[296,512]{1,0:T(8,128)(2,1)S(1)} %pad_maximum_fusion.6), channel_id=1, source_target_pairs={{0,16},{8,24},{16,0},{24,8},{1,17},{9,25},{17,1},{25,9},{2,18},{10... | collective-permute-start | bytes 909320 | tf_op jit(solution)/shard_map/ppermute | solution.py:20
  (15 other events, 166.6 us)

commit v5 on v4

--- a/solution.py
+++ b/solution.py
@@ -260,21 +260,23 @@
             count + 18:
         ]
         copies = Copies(sems)
-        arriving = [copies.start(piece_refs[p], sources.at[p]) for p in range(count)]
+        held = copies.start(piece_refs[0], sources)
         waits = [copies.start(proj_hbm, proj_ref), copies.start(weight_hbm, weight_ref)]
         z, x, core = lax.axis_index("z"), lax.axis_index("x"), lax.axis_index("core")
         y = lax.axis_index("yhi") * 2 + lax.axis_index("ylo")
         extra = jnp.zeros((EXTRA, wide), F32)
         for p, (side, steps) in enumerate([(side, steps) for side in (0, 1) for steps in (0, 1, 3, 2)]):
-            arriving[p].wait()
-            extra = extra + sources[p, rows:].astype(F32)
+            if p == 0:
+                held.wait()
+            source = piece_refs[p] if p else sources
+            extra = extra + source[rows:].astype(F32)
             other = (y - steps) & 3
             member = ((other & 1) * 2 + ((core + side) & 1)) * 2 + (other >> 1)
             for part in range(2):
                 place = 2 * member + part
                 turn = (place & 3) * N + (place >> 2)
                 block = ((z + (place & 3)) & 3) * N + ((x + (place >> 2)) & 3)
-                value = sources[p, :rows, part * width:(part + 1) * width]
+                value = source[:rows, part * width:(part + 1) * width]
                 whole[:, pl.ds(pl.multiple_of(block * width, width), width)] = value
                 flipped = value.T
                 first[place] = flipped
@@ -327,7 +329,7 @@
     outs = step(
         kernel,
         "tile_step",
-        [(pieces[0], HBM)] + [(piece, ANY) for piece in pieces[1:]]
+        [(pieces[0], HBM)] + [(piece, VMEM) for piece in pieces[1:]]
         + [(projected, HBM), (key_value_weight, HBM), (newline_embed, VMEM)],
         [(jax.ShapeDtypeStruct((stop - start, width, rows), dtype), HBM) for start, stop in CUTS[2:]] * 2
         + [
@@ -341,7 +343,7 @@
             (jax.ShapeDtypeStruct((1, share), F32), VMEM),
         ],
         [
-            VMEM((count,) + pieces[0].shape, dtype),
+            VMEM(pieces[0].shape, dtype),
             VMEM(projected.shape, BF),
             VMEM(key_value_weight.shape, BF),
             VMEM(turned.shape, dtype),
@@ -455,9 +457,12 @@
     return low[:size], low[size:], high[:size], high[size:]
 
 
-def straight(blocks, axis):
-    arrived = [shift(blocks[d].astype(BF), axis, N, d).astype(F32) for d in FAR]
-    return blocks[0] + arrived[0] + arrived[1] + arrived[2]
+def straight(blocks, axis, after=None):
+    leaving = [blocks[d].astype(BF) for d in FAR]
+    if after is not None:
+        leaving[1], after = lax.optimization_barrier((leaving[1], after))
+    arrived = [shift(block, axis, N, d) for block, d in zip(leaving, FAR)]
+    return blocks[0] + sum(a.astype(F32) for a in arrived), arrived[1]
 
 
 def local(
@@ -552,8 +557,8 @@
     x_in = [both_ways(x_send0, "x"), both_ways(x_send1, "z")]
     kv_in, projected_grad = lax.optimization_barrier((kv_in, projected_grad))
     parts = x_rest(list(features1[2:]) + list(features2[2:]), projected_grad, turned, normed)
-    results = []
-    for i, (first, second) in enumerate((("x", "z"), ("z", "x"))):
+    results, after = [], None
+    for i, first, second in ((1, "z", "x"), (0, "x", "z")):
         x_parts, kv_parts = parts[i], parts[2 + i]
         sends = [
             jnp.concatenate(pair, axis=0)
@@ -563,13 +568,16 @@
         size = x_parts[0].shape[0]
         x_blocks = ring_blocks(x_parts, *x_in[i], ahead[:size], behind[:size])
         kv_blocks = ring_blocks(kv_parts, *kv_in[i], ahead[size:], behind[size:])
-        results.append(
-            straight([jnp.concatenate(pair, axis=0) for pair in zip(x_blocks, kv_blocks)], second)
+        result, after = straight(
+            [jnp.concatenate(pair, axis=0) for pair in zip(x_blocks, kv_blocks)], second, after
         )
-    result = jnp.concatenate(results, axis=1)
-    x_result, kv_result = result[:x_rows], result[x_rows:]
+        results.insert(0, result)
+    siglip_result, convnext_result, kv_result = [
+        jnp.concatenate([result[start:stop] for result in results], axis=1)
+        for start, stop in ((0, sig_rows), (sig_rows, x_rows), (x_rows, x_rows + kv_rows))
+    ]
     kv_result = kv_result + line_total[:, :1] * line_normed
-    return x_result[:sig_rows], x_result[sig_rows:], kv_result
+    return siglip_result, convnext_result, kv_result
 
 
 def solution(mesh):

time: 137 us -> 137 us (level)
  starting transfers between devices: 39.3 us -> 37.9 us
    slice x2 -> x0, other arithmetic: 1.51 us -> none  [local(): return (x_result[:sig_rows], x_result[sig_rows:], kv_result)]
    concatenate x0 -> x2, other arithmetic: none -> 1.51 us  [local(): jnp.concatenate([result[start:stop] for result in results], axis=1)]
    ppermute x22, starting transfers between devices: 26 us -> 24.5 us  [shift(): lax.ppermute(value, axis, [(i, (i + step) % size) for i in range(size)])]
where the time goes in v5:
time: 137 us; the launch traced here: 136 us
  waiting for transfers between devices  45.8 us (33%)
  starting transfers between devices  37.9 us (28%)
  Pallas kernels  25.5 us (19%)
  blocking collectives  9 us (7%)
  matrix products  6.77 us (5%)
  other arithmetic  5.42 us (4%)
  local copies, waits for them, and re-layouts  4.59 us (3%)
    ppermute x22, waiting for transfers between devices, shift(): lax.ppermute(value, axis, [(i, (i + step) % size) for i in range(size)])  34.9 us
    ppermute x22, starting transfers between devices, shift(): lax.ppermute(value, axis, [(i, (i + step) % size) for i in range(size)])  24.5 us
    pallas_call x3, Pallas kernels, step(): pl.pallas_call(kernel, out_shape=[space(shape.shape, shape.dtype) for sha...  16.3 us
    ppermute x3, waiting for transfers between devices, shift_y(): lax.ppermute(value, Y, [(place(y), place((y + step) % N)) for y in range(...  9.37 us
    all_to_all x1, blocking collectives, local(): lax.all_to_all(products, ('ylo', 'core', 'yhi'), split_axis=0, concat_axi...  9 us
    all_to_all x1, starting transfers between devices, local(): lax.all_to_all(outgoing, DP, split_axis=0, concat_axis=0, tiled=True)  8.02 us
    ppermute x3, starting transfers between devices, shift_y(): lax.ppermute(value, Y, [(place(y), place((y + step) % N)) for y in range(...  5.3 us
    dot_general x1, matrix products, local(): jnp.dot(siglip_features, siglip_projection, preferred_element_type=F32)  3.66 us
  transfers between devices with their start and end apart: 26, of which 11 were waited for; matrix products, arithmetic and copies ran while one was open for 9% of the time, Pallas kernels for 9%

profile of v5, /device:TPU:0, one launch (start us, length us, event | category | flops | bytes accessed | tf_op | source)
XLA Modules:
  0.0 136.2 jit_solution(3997031750788182222)
XLA Ops:
  0.6 2.7 %slices_out.1 = bf16[16,80,256]{2,1,0:T(8,128)(2,1)} custom-call(bf16[1024,2048]{1,0:T(8,128)(2,1)} %source.1, bf16[32,2048]{1,0:T(8,128)(2,1)} %lines.1), custom_call_target="tpu_custom_call" | custom-call | tf_op jit(solution)/shard_map/slices_out/pallas_call | solution.py:85
  3.4 8.0 %all-to-all-start = ((bf16[16,80,256]{2,1,0:T(8,128)(2,1)}), bf16[16,80,256]{2,1,0:T(8,128)(2,1)}, u32[]{:S(2)}, u32[]{:S(2)}) async-start(bf16[16,80,256]{2,1,0:T(8,128)(2,1)} %slices_out.1), calls=%async_computation | async-start | bytes 1310720 | tf_op jit(solution)/shard_map/all_to_all | solution.py:495
  11.4 3.7 %fusion.16 = f32[512,1024]{1,0:T(8,128)S(1)} fusion(bf16[512,1152]{1,0:T(8,128)(2,1)} %siglip_ref.1, bf16[1152,1024]{1,0:T(8,128)(2,1)} %param.12), kind=kOutput, calls=%fused_computation.77 | convolution fusion | flops 1207959552 | bytes 5636096 | tf_op jit(solution)/shard_map/dot_general | solution.py:498
  15.1 2.9 %multiply_reduce_fusion = (f32[512]{0:T(512)S(1)}, bf16[512,1024]{1,0:T(8,128)(2,1)}) fusion(f32[512,1024]{1,0:T(8,128)S(1)} %fusion.16, bf16[512,1536]{1,0:T(8,128)(2,1)S(1)} %copy-done.3, bf16[1536,1024]{1,0:T(8,128)(2,1)S(1)} %copy-done), kind=kOutput, calls=%fused_computation | convolution fusion | flops 1613233664 | bytes 7866368 | tf_op jit(solution)/shard_map/dot_general | solution.py:499
  18.0 3.4 %turn_features.1 = (bf16[672,512]{1,0:T(8,128)(2,1)}, bf16[672,512]{1,0:T(8,128)(2,1)}, bf16[336,512]{1,0:T(8,128)(2,1)}, bf16[336,512]{1,0:T(8,128)(2,1)}, bf16...) custom-call(bf16[512,1152]{1,0:T(8,128)(2,1)S(1)} %copy-done.4, ...), custom_call_target="tpu_custom_call" | custom-call | tf_op jit(solution)/shard_map/turn_features/pallas_call | solution.py:142
  24.4 3.1 %pick_tiles.1.refs_0_ = bf16[528,256]{1,0:T(8,128)(2,1)} custom-call(s32[16]{0:T(128)} %dynamic-slice_bitcast_fusion.dest_ref, bf16[16,80,256]{2,1,0:T(8,128)(2,1)} %all-to-all-done.source, bf16[16,256]{1,0:T(8,128)(2,1)} %pad.5.extra_ref), custom_call_target="tpu_custom_call" | custom-call | tf_op jit(solution)/shard_map/pick_tiles/pallas_call | solution.py:189
  27.6 3.3 %collective-permute-start.2 = (bf16[528,256]{1,0:T(8,128)(2,1)}, bf16[528,256]{1,0:T(8,128)(2,1)S(1)}, u32[]{:S(2)}, u32[]{:S(2)}) collective-permute-start(bf16[528,256]{1,0:T(8,128)(2,1)} %pick_tiles.1.refs_0_), channel_id=1, source_target_pairs={{0,1},{64,65},{1,0},{65,64},{2,3},{66,67},{3,2},{67,66},{4,5},{68,... | collective-permute-start | bytes 811016 | tf_op jit(solution)/shard_map/ppermute | solution.py:25
  35.0 3.7 %collective-permute-done.2.refs_3_ = bf16[528,256]{1,0:T(8,128)(2,1)S(1)} collective-permute-done((bf16[528,256]{1,0:T(8,128)(2,1)}, bf16[528,256]{1,0:T(8,128)(2,1)S(1)}, u32[]{:S(2)}, u32[]{:S(2)}) %collective-permute-start.2) | collective-permute-done | bytes 270368 | tf_op jit(solution)/shard_map/ppermute | solution.py:25
  38.7 5.7 %collective-permute-done.1.refs_2_ = bf16[528,256]{1,0:T(8,128)(2,1)S(1)} collective-permute-done((bf16[528,256]{1,0:T(8,128)(2,1)}, bf16[528,256]{1,0:T(8,128)(2,1)S(1)}, u32[]{:S(2)}, u32[]{:S(2)}) %collective-permute-start.1) | collective-permute-done | bytes 270368 | tf_op jit(solution)/shard_map/ppermute | solution.py:25
  46.3 7.1 %tile_step.1 = (bf16[2,128,512]{2,1,0:T(8,128)(2,1)}, bf16[2,128,512]{2,1,0:T(8,128)(2,1)}, bf16[4,128,512]{2,1,0:T(8,128)(2,1)}, bf16[2,128,512]{2,1,0:T(8,128)...) custom-call(bf16[528,256]{1,0:T(8,128)(2,1)} %pick_tiles.1.refs_0_, ...), custom_call_target="tpu_custom_call" | custom-call | tf_op jit(solution)/shard_map/tile_step/pallas_call | solution.py:207
  54.0 2.7 %collective-permute-start.8 = (bf16[512,512]{1,0:T(8,128)(2,1)}, bf16[512,512]{1,0:T(8,128)(2,1)S(1)}, u32[]{:S(2)}, u32[]{:S(2)}) collective-permute-start(bf16[512,512]{1,0:T(8,128)(2,1)} %get-tuple-element.99), channel_id=1, source_target_pairs={{0,6},{2,0},{4,2},{6,4},{1,7},{3,1},{5,3},{7,5},{8,14},{10,8},{12,... | collective-permute-start | bytes 1572872 | tf_op jit(solution)/shard_map/ppermute | solution.py:20
  57.0 2.9 %collective-permute-start.10 = (bf16[512,512]{1,0:T(8,128)(2,1)}, bf16[512,512]{1,0:T(8,128)(2,1)S(1)}, u32[]{:S(2)}, u32[]{:S(2)}) collective-permute-start(bf16[512,512]{1,0:T(8,128)(2,1)} %get-tuple-element.101), channel_id=1, source_target_pairs={{0,24},{8,0},{16,8},{24,16},{1,25},{9,1},{17,9},{25,17},{2,26},{10... | collective-permute-start | bytes 1572872 | tf_op jit(solution)/shard_map/ppermute | solution.py:20
  60.0 9.0 %all_to_all.10.products_ref = f32[8,8,128]{2,1,0:T(8,128)S(1)} all-to-all(f32[8,8,128]{2,1,0:T(8,128)S(1)} %get-tuple-element.102), channel_id=1, replica_groups=mesh['ylo'=2,'core'=2,'z'=4,'x'=4,'yhi'=2] {'ylo','core','yhi'}, dimensions={0} | all-to-all | bytes 65536 | tf_op jit(solution)/shard_map/all_to_all | solution.py:548
  70.2 2.9 %x_first.1 = (bf16[512,1024]{1,0:T(8,128)(2,1)}, bf16[672,512]{1,0:T(8,128)(2,1)}, bf16[672,512]{1,0:T(8,128)(2,1)}, bf16[672,512]{1,0:T(8,128)(2,1)}, bf16[672,512]{1,0:T(8,128)(2,1)}) custom-call(f32[8,8,128]{2,1,0:T(8,128)S(1)} %all_to_all.10.products_ref, bf16[512,1024]{1,0:T(8,128)(2,1)S(1)} %copy-done.5, bf16[512,1024]{1,0:T(8,128)(2,1)S(1)} %copy-done.2, ...), custom_call_target="tpu_custom_call" | custom-call | tf_op jit(solution)/shard_map/x_first/pallas_call | solution.py:207
  77.3 6.3 %x_rest.1 = (f32[336,512]{1,0:T(8,128)S(1)}, f32[336,512]{1,0:T(8,128)S(1)}, f32[672,512]{1,0:T(8,128)S(1)}, f32[336,512]{1,0:T(8,128)S(1)}, f32[336,512]{1,0:T(...) custom-call(bf16[336,512]{1,0:T(8,128)(2,1)} %get-tuple-element.79.r, ...), custom_call_target="tpu_custom_call" | custom-call | tf_op jit(solution)/shard_map/x_rest/pallas_call | solution.py:207
  83.9 8.5 %collective-permute-done.16 = bf16[672,512]{1,0:T(8,128)(2,1)S(1)} collective-permute-done((bf16[672,512]{1,0:T(8,128)(2,1)}, bf16[672,512]{1,0:T(8,128)(2,1)S(1)}, u32[]{:S(2)}, u32[]{:S(2)}) %collective-permute-start.16) | collective-permute-done | bytes 688160 | tf_op jit(solution)/shard_map/ppermute | solution.py:20
  95.0 2.3 %collective-permute-start.14 = (bf16[592,512]{1,0:T(8,128)(2,1)S(1)}, bf16[592,512]{1,0:T(8,128)(2,1)S(1)}, u32[]{:S(2)}, u32[]{:S(2)}) collective-permute-start(bf16[592,512]{1,0:T(8,128)(2,1)S(1)} %pad_maximum_fusion.1), channel_id=1, source_target_pairs={{0,6},{2,0},{4,2},{6,4},{1,7},{3,1},{5,3},{7,5},{8,14},{10,8},{12,... | collective-permute-start | bytes 1818632 | tf_op jit(solution)/shard_map/ppermute | solution.py:20
  97.5 9.3 %collective-permute-done.22 = bf16[592,512]{1,0:T(8,128)(2,1)S(1)} collective-permute-done((bf16[592,512]{1,0:T(8,128)(2,1)S(1)}, bf16[592,512]{1,0:T(8,128)(2,1)S(1)}, u32[]{:S(2)}, u32[]{:S(2)}) %collective-permute-start.22) | collective-permute-done | bytes 606240 | tf_op jit(solution)/shard_map/ppermute | solution.py:20
  106.8 2.7 %collective-permute-done.18 = bf16[592,512]{1,0:T(8,128)(2,1)S(1)} collective-permute-done((bf16[592,512]{1,0:T(8,128)(2,1)S(1)}, bf16[592,512]{1,0:T(8,128)(2,1)S(1)}, u32[]{:S(2)}, u32[]{:S(2)}) %collective-permute-start.18) | collective-permute-done | bytes 606240 | tf_op jit(solution)/shard_map/ppermute | solution.py:20
  110.7 2.8 %collective-permute-start.24 = (bf16[296,512]{1,0:T(8,128)(2,1)S(1)}, bf16[296,512]{1,0:T(8,128)(2,1)S(1)}, u32[]{:S(2)}, u32[]{:S(2)}) collective-permute-start(bf16[296,512]{1,0:T(8,128)(2,1)S(1)} %pad_maximum_fusion.10), channel_id=1, source_target_pairs={{0,6},{2,0},{4,2},{6,4},{1,7},{3,1},{5,3},{7,5},{8,14},{10,8},{12,... | collective-permute-start | bytes 909320 | tf_op jit(solution)/shard_map/ppermute | solution.py:20
  115.2 4.3 %collective-permute-start.21 = (bf16[296,512]{1,0:T(8,128)(2,1)S(1)}, bf16[296,512]{1,0:T(8,128)(2,1)S(1)}, u32[]{:S(2)}, u32[]{:S(2)}) collective-permute-start(bf16[296,512]{1,0:T(8,128)(2,1)S(1)} %pad_maximum_fusion.8), channel_id=1, source_target_pairs={{0,24},{8,0},{16,8},{24,16},{1,25},{9,1},{17,9},{25,17},{2,26},{10... | collective-permute-start | bytes 909320 | tf_op jit(solution)/shard_map/ppermute | solution.py:20
  119.7 5.7 %collective-permute-done.19 = bf16[296,512]{1,0:T(8,128)(2,1)S(1)} collective-permute-done((bf16[296,512]{1,0:T(8,128)(2,1)S(1)}, bf16[296,512]{1,0:T(8,128)(2,1)S(1)}, u32[]{:S(2)}, u32[]{:S(2)}) %collective-permute-start.19) | collective-permute-done | bytes 303136 | tf_op jit(solution)/shard_map/ppermute | solution.py:20
  125.7 2.4 %collective-permute-done.21 = bf16[296,512]{1,0:T(8,128)(2,1)S(1)} collective-permute-done((bf16[296,512]{1,0:T(8,128)(2,1)S(1)}, bf16[296,512]{1,0:T(8,128)(2,1)S(1)}, u32[]{:S(2)}, u32[]{:S(2)}) %collective-permute-start.21) | collective-permute-done | bytes 303136 | tf_op jit(solution)/shard_map/ppermute | solution.py:20
  128.1 5.3 %collective-permute-done.20 = bf16[296,512]{1,0:T(8,128)(2,1)S(1)} collective-permute-done((bf16[296,512]{1,0:T(8,128)(2,1)S(1)}, bf16[296,512]{1,0:T(8,128)(2,1)S(1)}, u32[]{:S(2)}, u32[]{:S(2)}) %collective-permute-start.20) | collective-permute-done | bytes 303136 | tf_op jit(solution)/shard_map/ppermute | solution.py:20
  (139 shorter events, 24.5 us)
Async XLA Ops:
  3.4 21.0 %all-to-all-start = ((bf16[16,80,256]{2,1,0:T(8,128)(2,1)}), bf16[16,80,256]{2,1,0:T(8,128)(2,1)}, u32[]{:S(2)}, u32[]{:S(2)}) async-start(bf16[16,80,256]{2,1,0:T(8,128)(2,1)} %slices_out.1), calls=%async_computation | async-start | bytes 1310720 | tf_op jit(solution)/shard_map/all_to_all | solution.py:495
  27.5 17.8 %collective-permute-start.3 = (bf16[528,256]{1,0:T(8,128)(2,1)}, bf16[528,256]{1,0:T(8,128)(2,1)S(1)}, u32[]{:S(2)}, u32[]{:S(2)}) collective-permute-start(bf16[528,256]{1,0:T(8,128)(2,1)} %pick_tiles.1.refs_0_), channel_id=1, source_target_pairs={{0,32},{32,0},{1,33},{33,1},{2,34},{34,2},{3,35},{35,3},{4,36},{36... | collective-permute-start | bytes 811016 | tf_op jit(solution)/shard_map/ppermute | solution.py:20
  27.6 11.1 %collective-permute-start.2 = (bf16[528,256]{1,0:T(8,128)(2,1)}, bf16[528,256]{1,0:T(8,128)(2,1)S(1)}, u32[]{:S(2)}, u32[]{:S(2)}) collective-permute-start(bf16[528,256]{1,0:T(8,128)(2,1)} %pick_tiles.1.refs_0_), channel_id=1, source_target_pairs={{0,1},{64,65},{1,0},{65,64},{2,3},{66,67},{3,2},{67,66},{4,5},{68,... | collective-permute-start | bytes 811016 | tf_op jit(solution)/shard_map/ppermute | solution.py:25
  30.8 13.5 %collective-permute-start.1 = (bf16[528,256]{1,0:T(8,128)(2,1)}, bf16[528,256]{1,0:T(8,128)(2,1)S(1)}, u32[]{:S(2)}, u32[]{:S(2)}) collective-permute-start(bf16[528,256]{1,0:T(8,128)(2,1)} %pick_tiles.1.refs_0_), channel_id=1, source_target_pairs={{0,65},{64,0},{1,64},{65,1},{2,67},{66,2},{3,66},{67,3},{4,69},{68... | collective-permute-start | bytes 811016 | tf_op jit(solution)/shard_map/ppermute | solution.py:25
  31.9 12.5 %collective-permute-start = (bf16[528,256]{1,0:T(8,128)(2,1)}, bf16[528,256]{1,0:T(8,128)(2,1)S(1)}, u32[]{:S(2)}, u32[]{:S(2)}) collective-permute-start(bf16[528,256]{1,0:T(8,128)(2,1)} %pick_tiles.1.refs_0_), channel_id=1, source_target_pairs={{0,64},{64,1},{1,65},{65,0},{2,66},{66,3},{3,67},{67,2},{4,68},{68... | collective-permute-start | bytes 811016 | tf_op jit(solution)/shard_map/ppermute | solution.py:25
  38.7 6.6 %collective-permute-start.6 = (bf16[528,256]{1,0:T(8,128)(2,1)S(1)}, bf16[528,256]{1,0:T(8,128)(2,1)S(1)}, u32[]{:S(2)}, u32[]{:S(2)}) collective-permute-start(bf16[528,256]{1,0:T(8,128)(2,1)S(1)} %collective-permute-done.2.refs_3_), channel_id=1, source_target_pairs={{0,32},{32,0},{1,33},{33,1},{2,34},{34,2},{3,35},{35,3},{4,36},{36... | collective-permute-start | bytes 811016 | tf_op jit(solution)/shard_map/ppermute | solution.py:20
  53.4 20.1 %collective-permute-start.7 = (bf16[512,512]{1,0:T(8,128)(2,1)}, bf16[512,512]{1,0:T(8,128)(2,1)S(1)}, u32[]{:S(2)}, u32[]{:S(2)}) collective-permute-start(bf16[512,512]{1,0:T(8,128)(2,1)} %get-tuple-element.98), channel_id=1, source_target_pairs={{0,2},{2,4},{4,6},{6,0},{1,3},{3,5},{5,7},{7,1},{8,10},{10,12},{12... | collective-permute-start | bytes 1572872 | tf_op jit(solution)/shard_map/ppermute | solution.py:20
  54.0 21.2 %collective-permute-start.8 = (bf16[512,512]{1,0:T(8,128)(2,1)}, bf16[512,512]{1,0:T(8,128)(2,1)S(1)}, u32[]{:S(2)}, u32[]{:S(2)}) collective-permute-start(bf16[512,512]{1,0:T(8,128)(2,1)} %get-tuple-element.99), channel_id=1, source_target_pairs={{0,6},{2,0},{4,2},{6,4},{1,7},{3,1},{5,3},{7,5},{8,14},{10,8},{12,... | collective-permute-start | bytes 1572872 | tf_op jit(solution)/shard_map/ppermute | solution.py:20
  56.7 18.9 %collective-permute-start.9 = (bf16[512,512]{1,0:T(8,128)(2,1)}, bf16[512,512]{1,0:T(8,128)(2,1)S(1)}, u32[]{:S(2)}, u32[]{:S(2)}) collective-permute-start(bf16[512,512]{1,0:T(8,128)(2,1)} %get-tuple-element.100), channel_id=1, source_target_pairs={{0,8},{8,16},{16,24},{24,0},{1,9},{9,17},{17,25},{25,1},{2,10},{10... | collective-permute-start | bytes 1572872 | tf_op jit(solution)/shard_map/ppermute | solution.py:20
  57.0 20.3 %collective-permute-start.10 = (bf16[512,512]{1,0:T(8,128)(2,1)}, bf16[512,512]{1,0:T(8,128)(2,1)S(1)}, u32[]{:S(2)}, u32[]{:S(2)}) collective-permute-start(bf16[512,512]{1,0:T(8,128)(2,1)} %get-tuple-element.101), channel_id=1, source_target_pairs={{0,24},{8,0},{16,8},{24,16},{1,25},{9,1},{17,9},{25,17},{2,26},{10... | collective-permute-start | bytes 1572872 | tf_op jit(solution)/shard_map/ppermute | solution.py:20
  73.1 21.7 %collective-permute-start.11 = (bf16[672,512]{1,0:T(8,128)(2,1)}, bf16[672,512]{1,0:T(8,128)(2,1)S(1)}, u32[]{:S(2)}, u32[]{:S(2)}) collective-permute-start(bf16[672,512]{1,0:T(8,128)(2,1)} %get-tuple-element.113), channel_id=1, source_target_pairs={{0,6},{2,0},{4,2},{6,4},{1,7},{3,1},{5,3},{7,5},{8,14},{10,8},{12,... | collective-permute-start | bytes 2064392 | tf_op jit(solution)/shard_map/ppermute | solution.py:20
  73.5 23.7 %collective-permute-start.12 = (bf16[672,512]{1,0:T(8,128)(2,1)}, bf16[672,512]{1,0:T(8,128)(2,1)S(1)}, u32[]{:S(2)}, u32[]{:S(2)}) collective-permute-start(bf16[672,512]{1,0:T(8,128)(2,1)} %get-tuple-element.115), channel_id=1, source_target_pairs={{0,2},{2,4},{4,6},{6,0},{1,3},{3,5},{5,7},{7,1},{8,10},{10,12},{12... | collective-permute-start | bytes 2064392 | tf_op jit(solution)/shard_map/ppermute | solution.py:20
  75.2 17.1 %collective-permute-start.16 = (bf16[672,512]{1,0:T(8,128)(2,1)}, bf16[672,512]{1,0:T(8,128)(2,1)S(1)}, u32[]{:S(2)}, u32[]{:S(2)}) collective-permute-start(bf16[672,512]{1,0:T(8,128)(2,1)} %get-tuple-element.123), channel_id=1, source_target_pairs={{0,24},{8,0},{16,8},{24,16},{1,25},{9,1},{17,9},{25,17},{2,26},{10... | collective-permute-start | bytes 2064392 | tf_op jit(solution)/shard_map/ppermute | solution.py:20
  75.6 18.5 %collective-permute-start.17 = (bf16[672,512]{1,0:T(8,128)(2,1)}, bf16[672,512]{1,0:T(8,128)(2,1)S(1)}, u32[]{:S(2)}, u32[]{:S(2)}) collective-permute-start(bf16[672,512]{1,0:T(8,128)(2,1)} %get-tuple-element.125), channel_id=1, source_target_pairs={{0,8},{8,16},{16,24},{24,0},{1,9},{9,17},{17,25},{25,1},{2,10},{10... | collective-permute-start | bytes 2064392 | tf_op jit(solution)/shard_map/ppermute | solution.py:20
  92.5 14.3 %collective-permute-start.22 = (bf16[592,512]{1,0:T(8,128)(2,1)S(1)}, bf16[592,512]{1,0:T(8,128)(2,1)S(1)}, u32[]{:S(2)}, u32[]{:S(2)}) collective-permute-start(bf16[592,512]{1,0:T(8,128)(2,1)S(1)} %pad_maximum_fusion.3), channel_id=1, source_target_pairs={{0,24},{8,0},{16,8},{24,16},{1,25},{9,1},{17,9},{25,17},{2,26},{10... | collective-permute-start | bytes 1818632 | tf_op jit(solution)/shard_map/ppermute | solution.py:20
  94.3 15.2 %collective-permute-start.18 = (bf16[592,512]{1,0:T(8,128)(2,1)S(1)}, bf16[592,512]{1,0:T(8,128)(2,1)S(1)}, u32[]{:S(2)}, u32[]{:S(2)}) collective-permute-start(bf16[592,512]{1,0:T(8,128)(2,1)S(1)} %pad_maximum_fusion.2), channel_id=1, source_target_pairs={{0,8},{8,16},{16,24},{24,0},{1,9},{9,17},{17,25},{25,1},{2,10},{10... | collective-permute-start | bytes 1818632 | tf_op jit(solution)/shard_map/ppermute | solution.py:20
  95.0 19.6 %collective-permute-start.14 = (bf16[592,512]{1,0:T(8,128)(2,1)S(1)}, bf16[592,512]{1,0:T(8,128)(2,1)S(1)}, u32[]{:S(2)}, u32[]{:S(2)}) collective-permute-start(bf16[592,512]{1,0:T(8,128)(2,1)S(1)} %pad_maximum_fusion.1), channel_id=1, source_target_pairs={{0,6},{2,0},{4,2},{6,4},{1,7},{3,1},{5,3},{7,5},{8,14},{10,8},{12,... | collective-permute-start | bytes 1818632 | tf_op jit(solution)/shard_map/ppermute | solution.py:20
  97.4 17.1 %collective-permute-start.13 = (bf16[592,512]{1,0:T(8,128)(2,1)S(1)}, bf16[592,512]{1,0:T(8,128)(2,1)S(1)}, u32[]{:S(2)}, u32[]{:S(2)}) collective-permute-start(bf16[592,512]{1,0:T(8,128)(2,1)S(1)} %pad_maximum_fusion), channel_id=1, source_target_pairs={{0,2},{2,4},{4,6},{6,0},{1,3},{3,5},{5,7},{7,1},{8,10},{10,12},{12... | collective-permute-start | bytes 1818632 | tf_op jit(solution)/shard_map/ppermute | solution.py:20
  110.1 15.3 %collective-permute-start.19 = (bf16[296,512]{1,0:T(8,128)(2,1)S(1)}, bf16[296,512]{1,0:T(8,128)(2,1)S(1)}, u32[]{:S(2)}, u32[]{:S(2)}) collective-permute-start(bf16[296,512]{1,0:T(8,128)(2,1)S(1)} %pad_maximum_fusion.7), channel_id=1, source_target_pairs={{0,2},{2,4},{4,6},{6,0},{1,3},{3,5},{5,7},{7,1},{8,10},{10,12},{12... | collective-permute-start | bytes 909320 | tf_op jit(solution)/shard_map/ppermute | solution.py:20
  110.7 14.8 %collective-permute-start.24 = (bf16[296,512]{1,0:T(8,128)(2,1)S(1)}, bf16[296,512]{1,0:T(8,128)(2,1)S(1)}, u32[]{:S(2)}, u32[]{:S(2)}) collective-permute-start(bf16[296,512]{1,0:T(8,128)(2,1)S(1)} %pad_maximum_fusion.10), channel_id=1, source_target_pairs={{0,6},{2,0},{4,2},{6,4},{1,7},{3,1},{5,3},{7,5},{8,14},{10,8},{12,... | collective-permute-start | bytes 909320 | tf_op jit(solution)/shard_map/ppermute | solution.py:20
  113.5 11.9 %collective-permute-start.23 = (bf16[296,512]{1,0:T(8,128)(2,1)S(1)}, bf16[296,512]{1,0:T(8,128)(2,1)S(1)}, u32[]{:S(2)}, u32[]{:S(2)}) collective-permute-start(bf16[296,512]{1,0:T(8,128)(2,1)S(1)} %pad_maximum_fusion.9), channel_id=1, source_target_pairs={{0,4},{2,6},{4,0},{6,2},{1,5},{3,7},{5,1},{7,3},{8,12},{10,14},{12... | collective-permute-start | bytes 909320 | tf_op jit(solution)/shard_map/ppermute | solution.py:20
  115.2 12.9 %collective-permute-start.21 = (bf16[296,512]{1,0:T(8,128)(2,1)S(1)}, bf16[296,512]{1,0:T(8,128)(2,1)S(1)}, u32[]{:S(2)}, u32[]{:S(2)}) collective-permute-start(bf16[296,512]{1,0:T(8,128)(2,1)S(1)} %pad_maximum_fusion.8), channel_id=1, source_target_pairs={{0,24},{8,0},{16,8},{24,16},{1,25},{9,1},{17,9},{25,17},{2,26},{10... | collective-permute-start | bytes 909320 | tf_op jit(solution)/shard_map/ppermute | solution.py:20
  119.5 8.5 %collective-permute-start.15 = (bf16[296,512]{1,0:T(8,128)(2,1)S(1)}, bf16[296,512]{1,0:T(8,128)(2,1)S(1)}, u32[]{:S(2)}, u32[]{:S(2)}) collective-permute-start(bf16[296,512]{1,0:T(8,128)(2,1)S(1)} %pad_maximum_fusion.5), channel_id=1, source_target_pairs={{0,16},{8,24},{16,0},{24,8},{1,17},{9,25},{17,1},{25,9},{2,18},{10... | collective-permute-start | bytes 909320 | tf_op jit(solution)/shard_map/ppermute | solution.py:20
  125.3 8.0 %collective-permute-start.20 = (bf16[296,512]{1,0:T(8,128)(2,1)S(1)}, bf16[296,512]{1,0:T(8,128)(2,1)S(1)}, u32[]{:S(2)}, u32[]{:S(2)}) collective-permute-start(bf16[296,512]{1,0:T(8,128)(2,1)S(1)} %pad_maximum_fusion.6), channel_id=1, source_target_pairs={{0,8},{8,16},{16,24},{24,0},{1,9},{9,17},{17,25},{25,1},{2,10},{10... | collective-permute-start | bytes 909320 | tf_op jit(solution)/shard_map/ppermute | solution.py:20
  (18 other events, 174.1 us)
